TPU v7x, 32 devices: a whole 2x2x4 slice. The times are simulated.
32 devices in a mesh: dp: 16 (over z, y, x), tensor: 2 (over core).
Axes of the slice: x: 2, y: 2, z: 4, core: 2. Of those that a mesh axis runs over, the one named last changes fastest.
Arguments:
- layer_in: bfloat16 [32768, 768], P(('dp', 'tensor')), may hold values from -6 to 6
- upstream: bfloat16 [32768, 768], P(('dp', 'tensor')), may hold values from -6 to 6
- lengths: int32 [32], P('dp'), may hold values from 256 to 1024, as said below
- rescale: float32 [768], replicated, may hold values from 0.5 to 1.5
- gating: bfloat16 [768, 1536], P('dp', 'tensor'), may hold values from -0.21875 to 0.21875
- content: bfloat16 [768, 1536], P('dp', 'tensor'), may hold values from -0.21875 to 0.21875
- selector: bfloat16 [768, 128], P('dp'), may hold values from -0.21875 to 0.21875
- timestep: bfloat16 [768, 24], P('dp', 'tensor'), may hold values from -0.21875 to 0.21875
- filters: float32 [4, 1536], P(None, 'tensor'), may hold values from -3 to 3
- kernels: float32 [4, 128], replicated, may hold values from -3 to 3
- biases: float32 [24], P('tensor'), may hold values from -6 to -2
- decays: float32 [24], P('tensor'), may hold values from -1 to 2
- shortcut: float32 [24], P('tensor'), may hold values from 0.5 to 1.5
- amplitude: float32 [1536], P('tensor'), may hold values from 0.5 to 1.5
- outgoing: bfloat16 [1536, 768], P('tensor', 'dp'), may hold values from -0.15625 to 0.15625
Outputs:
- layer_out: bfloat16 [32768, 768], P(('dp', 'tensor'))
- input_grad: bfloat16 [32768, 768], P(('dp', 'tensor'))
- rescale_grad: float32 [768], replicated
- gating_grad: float32 [768, 1536], P('dp', 'tensor')
- content_grad: float32 [768, 1536], P('dp', 'tensor')
- selector_grad: float32 [768, 128], P('dp')
- timestep_grad: float32 [768, 24], P('dp', 'tensor')
- filters_grad: float32 [4, 1536], P(None, 'tensor')
- kernels_grad: float32 [4, 128], replicated
- biases_grad: float32 [24], P('tensor')
- decays_grad: float32 [24], P('tensor')
- shortcut_grad: float32 [24], P('tensor')
- amplitude_grad: float32 [1536], P('tensor')
- outgoing_grad: float32 [1536, 768], P('tensor', 'dp')
Inputs may be any that keep to these rules, and one draw needn't show every extreme that they name: lengths[s] is the number of valid tokens of sequence s; in every draw some sequence fills all 1024 of its slots.
All inputs are finite; a program needn't handle non-finite values.
Results may differ from a plain program's by a relative error of at most 0.011.
Values may be sent and summed in bfloat16 or wider, within the bound.
No kernel may reach another device: no remote copies, remote signals or barrier semaphores. Data moves between devices by JAX's collectives and lax.ppermute only.
A program may use at most 256 MiB of HBM per device.

v0:
```python
import functools

import jax
import jax.numpy as jnp
from jax import lax
from jax.sharding import PartitionSpec as P

INNER_WIDTH = 1536
BLOCK_ROWS = 128


epsilon = 1e-05
precise = lax.Precision.HIGHEST


def causal_conv(values, kernel):
    taps = kernel.shape[0]
    length = values.shape[0]
    padded = jnp.pad(values, ((taps - 1, 0), (0, 0)))
    summed = jnp.zeros_like(values)
    for offset in range(taps):
        summed = summed + padded[offset : offset + length] * kernel[offset]
    return summed


def prepare(mask_full, values_in, select_in, step_in, filters, kernels, biases):
    values_act = jax.nn.silu(causal_conv(values_in, filters)) * mask_full[:, None]
    select_act = jax.nn.silu(causal_conv(select_in, kernels))
    step_sizes = jax.nn.softplus(step_in + biases)
    return (values_act, select_act, step_sizes)


def mix_heads(values_low, select_low, step_sizes, decays, shortcut, gate_in):
    length = values_low.shape[0]
    head_count = step_sizes.shape[1]
    head_width = values_low.shape[1] // head_count
    state_size = select_low.shape[1] // 2
    block_count = length // BLOCK_ROWS
    b_rows = select_low[:, :state_size].reshape(block_count, BLOCK_ROWS, state_size)
    c_rows = select_low[:, state_size:].reshape(block_count, BLOCK_ROWS, state_size)
    head_values = values_low.reshape(block_count, BLOCK_ROWS, head_count, head_width)
    log_decay = (-jnp.exp(decays) * step_sizes).reshape(block_count, BLOCK_ROWS, head_count)
    inclusive = jnp.cumsum(log_decay, axis=1)
    exclusive = inclusive - log_decay
    block_total = inclusive[:, -1]
    inclusive_heads = inclusive.transpose(0, 2, 1)
    exclusive_heads = exclusive.transpose(0, 2, 1)
    places = jnp.arange(BLOCK_ROWS)
    below_mask = (places[:, None] > places[None, :])[None, None, :, :]
    above_mask = (places[:, None] < places[None, :])[None, None, :, :]
    ahead_log = jnp.where(
        below_mask, inclusive_heads[:, :, :, None] - inclusive_heads[:, :, None, :], -1e30
    )
    behind_log = jnp.where(
        above_mask, exclusive_heads[:, :, None, :] - exclusive_heads[:, :, :, None], -1e30
    )
    gram_rows = jnp.einsum("cis,cjs->cij", c_rows, b_rows, precision=precise)
    scaled = head_values * step_sizes.reshape(block_count, BLOCK_ROWS, head_count)[..., None]
    scaled_heads = scaled.transpose(0, 2, 1, 3)
    coupling = gram_rows[:, None, :, :] * (jnp.exp(ahead_log) + jnp.exp(behind_log))
    inner_part = jnp.einsum("chij,chjp->cihp", coupling, scaled_heads, precision=precise)
    decay_out = jnp.exp(block_total[:, None, :] - inclusive)
    decay_in = jnp.exp(exclusive)
    gained_ahead = jnp.einsum("cjh,cjs,cjhp->chsp", decay_out, b_rows, scaled, precision=precise)
    gained_behind = jnp.einsum("cjh,cjs,cjhp->chsp", decay_in, b_rows, scaled, precision=precise)
    carry_decay = jnp.exp(block_total)

    def carry_step(state_now, pieces_in):
        block_decay, gained_state = pieces_in
        return (block_decay[:, None, None] * state_now + gained_state, state_now)

    empty_state = jnp.zeros((head_count, state_size, head_width), jnp.float32)
    _, earlier_state = lax.scan(carry_step, empty_state, (carry_decay, gained_ahead))
    _, later_state = lax.scan(carry_step, empty_state, (carry_decay, gained_behind), reverse=True)
    from_earlier = (
        jnp.einsum("cis,chsp->cihp", c_rows, earlier_state, precision=precise)
        * jnp.exp(inclusive)[..., None]
    )
    from_later = (
        jnp.einsum("cis,chsp->cihp", c_rows, later_state, precision=precise)
        * jnp.exp(block_total[:, None, :] - exclusive)[..., None]
    )
    mixed_out = inner_part + from_earlier + from_later + shortcut[:, None] * head_values
    return mixed_out.reshape(length, head_count * head_width) * jax.nn.silu(gate_in)


def arrange(gathered, tensor_rank, bc_share):
    full_gate, full_values, full_select, full_step, full_out = gathered
    forward_cat = jnp.concatenate((full_gate, full_values, full_select, full_step), axis=1)
    own_select = lax.dynamic_slice_in_dim(full_select, tensor_rank * bc_share, bc_share, 1)
    backward_cat = jnp.concatenate((full_gate, full_values, own_select, full_step), axis=1)
    return (forward_cat, backward_cat, full_out)


def place_slice(piece, tensor_rank, parts):
    last_axis = piece.ndim - 1
    full_shape = piece.shape[:-1] + (piece.shape[-1] * parts,)
    return lax.dynamic_update_slice_in_dim(
        jnp.zeros(full_shape, jnp.float32), piece, tensor_rank * piece.shape[-1], last_axis
    )


def own_slice(summed, tensor_rank, width_own):
    return lax.dynamic_slice_in_dim(summed, tensor_rank * width_own, width_own, summed.ndim - 1)


def on_device(
    layer_in,
    upstream,
    lengths,
    rescale,
    gating,
    content,
    selector,
    timestep,
    filters,
    kernels,
    biases,
    decays,
    shortcut,
    amplitude,
    outgoing,
):
    parts = lax.axis_size("tensor")
    tensor_rank = lax.axis_index("tensor")
    micro_count = lengths.shape[0]
    half_rows = layer_in.shape[0] // micro_count
    length = half_rows * parts
    inner_local = gating.shape[1]
    head_local = timestep.shape[1]
    state_cols = selector.shape[1]
    bc_share = state_cols // parts
    first_only = (tensor_rank == 0).astype(jnp.float32)
    positions = jnp.arange(length)
    own_positions = tensor_rank * half_rows + jnp.arange(half_rows)
    outputs_list = []
    grads_list = []
    total_in = None
    total_out = None
    rescale_acc = jnp.zeros(rescale.shape, jnp.float32)
    filters_acc = jnp.zeros(filters.shape, jnp.float32)
    kernels_acc = jnp.zeros(kernels.shape, jnp.float32)
    biases_acc = jnp.zeros(biases.shape, jnp.float32)
    decays_acc = jnp.zeros(decays.shape, jnp.float32)
    shortcut_acc = jnp.zeros(shortcut.shape, jnp.float32)
    amplitude_acc = jnp.zeros(amplitude.shape, jnp.float32)
    for micro_step in range(micro_count):
        forward_cat, backward_cat, full_out = arrange(
            (
                lax.all_gather(gating, "dp", axis=0, tiled=True),
                lax.all_gather(content, "dp", axis=0, tiled=True),
                lax.all_gather(selector, "dp", axis=0, tiled=True),
                lax.all_gather(timestep, "dp", axis=0, tiled=True),
                lax.all_gather(outgoing, "dp", axis=1, tiled=True),
            ),
            tensor_rank,
            bc_share,
        )
        low_end = micro_step * half_rows
        tok_rows = layer_in[low_end : low_end + half_rows].astype(jnp.float32)
        seq_length = lengths[micro_step]
        mask_own = (own_positions < seq_length).astype(jnp.float32)
        mask_full = (positions < seq_length).astype(jnp.float32)
        inverse = lax.rsqrt(jnp.mean(tok_rows * tok_rows, axis=-1, keepdims=True) + epsilon)
        unit_rows = tok_rows * inverse
        normed = (unit_rows * rescale).astype(jnp.bfloat16)
        sequence = lax.all_gather(normed, "tensor", axis=0, tiled=True)
        projected = jnp.dot(sequence, forward_cat, preferred_element_type=jnp.float32)
        gate_in = projected[:, :inner_local]
        values_in = projected[:, inner_local : 2 * inner_local]
        select_in = projected[:, 2 * inner_local : 2 * inner_local + state_cols]
        step_in = projected[:, 2 * inner_local + state_cols :]
        prepared, prepare_back = jax.vjp(
            functools.partial(prepare, mask_full),
            values_in,
            select_in,
            step_in,
            filters,
            kernels,
            biases,
        )
        values_act, select_act, step_sizes = prepared
        values_low = lax.optimization_barrier(values_act.astype(jnp.bfloat16)).astype(jnp.float32)
        select_low = lax.optimization_barrier(select_act.astype(jnp.bfloat16)).astype(jnp.float32)
        gated_pre, mix_back = jax.vjp(
            mix_heads, values_low, select_low, step_sizes, decays, shortcut, gate_in
        )
        squares = lax.psum(jnp.sum(gated_pre * gated_pre, axis=-1), "tensor")
        out_scale = lax.rsqrt(squares / INNER_WIDTH + epsilon)[:, None]
        gated = (gated_pre * out_scale * amplitude).astype(jnp.bfloat16)
        branch = lax.psum_scatter(
            jnp.dot(gated, full_out, preferred_element_type=jnp.float32).astype(jnp.bfloat16),
            "tensor",
            scatter_dimension=0,
            tiled=True,
        ).astype(jnp.float32)
        outputs_list.append((mask_own[:, None] * (tok_rows + branch)).astype(jnp.bfloat16))
        grad_rows_out = (
            upstream[low_end : low_end + half_rows].astype(jnp.float32) * mask_own[:, None]
        )
        grad_branch = lax.all_gather(
            grad_rows_out.astype(jnp.bfloat16), "tensor", axis=0, tiled=True
        )
        grad_out_mb = jnp.einsum(
            "ri,rd->id", gated, grad_branch, preferred_element_type=jnp.float32
        )
        grad_gated = jnp.einsum(
            "rd,id->ri", grad_branch, full_out, preferred_element_type=jnp.float32
        )
        weighted = grad_gated * amplitude
        cross = lax.psum(jnp.sum(weighted * gated_pre, axis=-1), "tensor")
        grad_pre = out_scale * weighted - gated_pre * out_scale**3 * (cross / INNER_WIDTH)[:, None]
        amplitude_acc = amplitude_acc + jnp.sum(grad_gated * gated_pre * out_scale, axis=0)
        grad_values_low, grad_select_part, grad_steps, grad_decays, grad_shortcut, grad_gate = (
            mix_back(grad_pre)
        )
        grad_select = lax.psum(grad_select_part.astype(jnp.bfloat16), "tensor").astype(jnp.float32)
        grad_values_in, grad_select_in, grad_step_in, grad_filters, grad_kernels, grad_biases = (
            prepare_back((grad_values_low, grad_select, grad_steps))
        )
        grad_proj = jnp.concatenate(
            (grad_gate, grad_values_in, grad_select_in, grad_step_in), axis=1
        ).astype(jnp.bfloat16)
        own_part = lax.dynamic_slice_in_dim(
            grad_proj, 2 * inner_local + tensor_rank * bc_share, bc_share, 1
        )
        grad_back = jnp.concatenate(
            (
                grad_proj[:, : 2 * inner_local],
                own_part,
                grad_proj[:, 2 * inner_local + state_cols :],
            ),
            axis=1,
        )
        grad_in_mb = jnp.einsum(
            "rd,rc->dc", sequence, grad_proj, preferred_element_type=jnp.float32
        )
        grad_normed = lax.psum_scatter(
            jnp.einsum(
                "rc,dc->rd", grad_back, backward_cat, preferred_element_type=jnp.float32
            ).astype(jnp.bfloat16),
            "tensor",
            scatter_dimension=0,
            tiled=True,
        ).astype(jnp.float32)
        weighted_in = grad_normed * rescale
        grad_input = (
            grad_rows_out
            + inverse * weighted_in
            - unit_rows * inverse * jnp.mean(weighted_in * unit_rows, axis=-1, keepdims=True)
        )
        grads_list.append(grad_input.astype(jnp.bfloat16))
        rescale_acc = rescale_acc + jnp.sum(grad_normed * unit_rows, axis=0)
        filters_acc = filters_acc + grad_filters
        kernels_acc = kernels_acc + grad_kernels
        biases_acc = biases_acc + grad_biases
        decays_acc = decays_acc + grad_decays
        shortcut_acc = shortcut_acc + grad_shortcut
        share_in, share_out = (grad_in_mb, grad_out_mb)
        total_in = share_in if total_in is None else total_in + share_in
        total_out = share_out if total_out is None else total_out + share_out
    total_in, total_out = (
        lax.psum_scatter(total_in, "dp", scatter_dimension=0, tiled=True),
        lax.psum_scatter(total_out, "dp", scatter_dimension=1, tiled=True),
    )
    small_sums = lax.psum(
        (
            rescale_acc,
            kernels_acc * first_only,
            place_slice(filters_acc, tensor_rank, parts),
            place_slice(biases_acc, tensor_rank, parts),
            place_slice(decays_acc, tensor_rank, parts),
            place_slice(shortcut_acc, tensor_rank, parts),
            place_slice(amplitude_acc, tensor_rank, parts),
        ),
        ("dp", "tensor"),
    )
    layer_out = jnp.concatenate(outputs_list, axis=0)
    input_grad = jnp.concatenate(grads_list, axis=0)
    gating_grad = total_in[:, :inner_local]
    content_grad = total_in[:, inner_local : 2 * inner_local]
    selector_grad = total_in[:, 2 * inner_local : 2 * inner_local + state_cols]
    timestep_grad = total_in[
        :, 2 * inner_local + state_cols : 2 * inner_local + state_cols + head_local
    ]
    filters_grad = own_slice(small_sums[2], tensor_rank, inner_local)
    biases_grad = own_slice(small_sums[3], tensor_rank, head_local)
    decays_grad = own_slice(small_sums[4], tensor_rank, head_local)
    shortcut_grad = own_slice(small_sums[5], tensor_rank, head_local)
    amplitude_grad = own_slice(small_sums[6], tensor_rank, inner_local)
    return (
        layer_out,
        input_grad,
        small_sums[0],
        gating_grad,
        content_grad,
        selector_grad,
        timestep_grad,
        filters_grad,
        small_sums[1],
        biases_grad,
        decays_grad,
        shortcut_grad,
        amplitude_grad,
        total_out,
    )


def solution(mesh):
    return jax.shard_map(
        on_device,
        mesh=mesh,
        in_specs=(
            P(("dp", "tensor"), None),
            P(("dp", "tensor"), None),
            P("dp"),
            P(),
            P("dp", "tensor"),
            P("dp", "tensor"),
            P("dp", None),
            P("dp", "tensor"),
            P(None, "tensor"),
            P(),
            P("tensor"),
            P("tensor"),
            P("tensor"),
            P("tensor"),
            P("tensor", "dp"),
        ),
        out_specs=(
            P(("dp", "tensor"), None),
            P(("dp", "tensor"), None),
            P(),
            P("dp", "tensor"),
            P("dp", "tensor"),
            P("dp", None),
            P("dp", "tensor"),
            P(None, "tensor"),
            P(),
            P("tensor"),
            P("tensor"),
            P("tensor"),
            P("tensor"),
            P("tensor", "dp"),
        ),
        check_vma=False,
    )
```

profile of v0, /device:TPU:0, one launch (start us, length us, event | category | flops | bytes accessed | tf_op | source)
XLA Modules:
  0.0 1310.7 jit_solution(3207367767485504378)
XLA Ops:
  22.2 42.8 %all-gather = bf16[16,48,12]{1,2,0:T(8,128)(2,1)S(1)} all-gather(bf16[1,48,12]{1,2,0:T(8,128)(2,1)S(1)} %bitcast.647), channel_id=1, replica_groups=mesh['dp'=16,'tensor'=2] {'dp'}, dimensions={0}, use_global_device_ids=true | all-gather | bytes 19584 | tf_op jit(solution)/shard_map/all_gather | solution.py:153
  65.2 36.8 %all_gather.35 = bf16[768,128]{1,0:T(8,128)(2,1)S(1)} all-gather(bf16[48,128]{1,0:T(8,128)(2,1)S(1)} %copy-done.187), channel_id=1, replica_groups=mesh['dp'=16,'tensor'=2] {'dp'}, dimensions={0}, use_global_device_ids=true | all-gather | bytes 208896 | tf_op jit(solution)/shard_map/all_gather | solution.py:152
  104.0 39.9 %all-gather.13.cloned.1.call-done = bf16[768,768]{1,0:T(8,128)(2,1)} async-done(((bf16[48,768]{1,0:T(8,128)(2,1)}), bf16[768,768]{1,0:T(8,128)(2,1)}) %all-gather.13.cloned.1.call-update) | async-done | bytes 1179664 | tf_op jit(solution)/shard_map/all_gather | solution.py:151
  164.4 23.8 %fusion.373 = f32[8,128,12]{2,0,1:T(8,128)S(1)} fusion(f32[8,128,12]{2,0,1:T(8,128)S(1)} %copy.531), kind=kOutput, calls=%fused_computation.612 | output fusion | flops 1560576 | bytes 98304 | tf_op jit(solution)/shard_map/jvp(jit(cumsum))/reduce_window_sum | solution.py:43
  211.0 13.0 multiply_convert_fusion.3
  240.2 29.2 %while.138 = (s32[]{:T(128)}, f32[12,64,64]{2,1,0:T(8,128)}, f32[8,12,64,64]{3,2,1,0:T(8,128)}, f32[8,12,1,1]{1,3,2,0:T(1,128)S(1)}, f32[8,12]{1,0:T(8,128)S(1)}...) while((s32[]{:T(128)}, f32[12,64,64]{2,1,0:T(8,128)}, f32[8,12,64,64]{3,2,1,0:T(8,128)}, ...), condition=%wide.region_12.14_spmd.clone, body=%wide.region_11.13_spmd.clone.sunk | while | flops 196611 | bytes 1378044 | solution.py:73
  283.9 29.1 %while.139 = (s32[]{:T(128)}, f32[12,64,64]{2,1,0:T(8,128)}, f32[8,12,64,64]{3,2,1,0:T(8,128)}, f32[8,12,1,1]{1,3,2,0:T(1,128)S(1)}, f32[8,12]{1,0:T(8,128)S(1)}...) while((s32[]{:T(128)}, f32[12,64,64]{2,1,0:T(8,128)}, ...), condition=%wide.region_14.16_spmd.clone, body=%wide.region_13.15_spmd.clone.sunk | while | flops 196612 | bytes 1377556 | solution.py:74
  330.1 16.8 %fusion.97 = f32[8,128,12,64]{1,3,2,0:T(8,128)S(1)} fusion(f32[8,128,12,64]{1,3,2,0:T(8,128)} %bitcast.600, f32[8,128,12,64]{1,3,2,0:T(8,128)} %bitcast.598, f32[8,128,12,64]{1,0,3,2:T(8,128)S(1)} %bitcast.567, f32[8,12,128]{2,1,0:T(8,128)} %copy.535, f32[8,12,128]{2,1,0:T(8,128)} %copy.532, f32[8,128,128]{2,1,0:T(8,128)} %fusion.289, ...), kind=kOutput, calls=%fused_computation.181 | convolution fusion | flops 1222901760 | bytes 13385776 | tf_op jit(solution)/shard_map/jvp(chij,chjp->cihp)/dot_general | solution.py:61
  366.2 28.9 %while.136 = (s32[]{:T(128)}, f32[12,64,64]{2,1,0:T(8,128)}, f32[8,12,64,64]{3,2,1,0:T(8,128)}, f32[8,12,1,1]{1,3,2,0:T(1,128)S(1)}, f32[8,12]{1,0:T(8,128)S(1)}...) while((s32[]{:T(128)}, f32[12,64,64]{2,1,0:T(8,128)}, f32[8,12,64,64]{3,2,1,0:T(8,128)}, ...), condition=%wide.region_3.5_spmd.clone, body=%wide.region_2.4_spmd.clone.sunk | while | flops 196611 | bytes 1378044 | solution.py:73
  409.9 15.4 %while.137 = (s32[]{:T(128)}, f32[12,64,64]{2,1,0:T(8,128)S(1)}, f32[8,12,64,64]{3,2,1,0:T(8,128)}, f32[8,12,1,1]{1,3,2,0:T(1,128)S(1)}, f32[8,12]{1,0:T(8,128)S...) while((s32[]{:T(128)}, f32[12,64,64]{2,1,0:T(8,128)S(1)}, ...), condition=%wide.region_5.7_spmd.clone, body=%wide.region_4.6_spmd.clone.sunk | while | flops 196612 | bytes 1180948 | solution.py:74
  440.0 16.3 %fusion.101 = f32[8,128,12,64]{1,3,2,0:T(8,128)S(1)} fusion(f32[8,128,12,64]{1,3,2,0:T(8,128)} %bitcast.604, f32[8,128,12,64]{1,3,2,0:T(8,128)} %bitcast.602, f32[8,128,12,64]{1,0,3,2:T(8,128)S(1)} %bitcast.574, f32[8,12,128]{2,1,0:T(8,128)S(1)} %copy.508, f32[8,12,128]{2,1,0:T(8,128)S(1)} %copy.505, f32[8,128,128]{2,1,0:T(8,128)} %fusion.298, ...), kind=kOutput, calls=%fused_computation.186 | convolution fusion | flops 1222901760 | bytes 13385776 | tf_op jit(solution)/shard_map/jvp(chij,chjp->cihp)/dot_general | solution.py:61
  486.0 13.8 %fusion.64 = (f32[768]{0:T(1024)}, f32[1024,768]{0,1:T(8,128)S(1)}, bf16[1024,768]{0,1:T(8,128)(2,1)}, bf16[1024,768]{0,1:T(8,128)(2,1)}, f32[768]{0:T(1024)}, /*index=5*/f32[1024,768]{0,1:T(8,128)S(1)}) fusion(bf16[1024,768]{0,1:T(8,128)(2,1)} %get-tuple-element.1362, f32[1024,1676]{0,1:T(8,128)} %copy-done.24, f32[1024]{0:T(1024)S(1)} %broadcast_multiply_fusion.19, ...), kind=kLoop, calls=%fused_computation.123 | loop fusion | flops 33028608 | bytes 37782528 | tf_op jit(solution)/shard_map/transpose(jvp())/reduce_sum | solution.py:83
  507.9 10.3 fusion.20
  526.2 10.1 fusion.14
  540.4 12.5 fusion.84
  555.0 51.9 %while.140 = (s32[]{:T(128)}, f32[12,64,64]{2,1,0:T(8,128)}, f32[8,12]{1,0:T(8,128)S(1)}, f32[8,12,64,64]{3,2,1,0:T(8,128)}, f32[8,12,64,64]{2,3,1,0:T(8,128)}, ...) while((s32[]{:T(128)}, f32[12,64,64]{2,1,0:T(8,128)}, ...), condition=%wide.region_22.24_spmd.clone, body=%wide.region_20.23_spmd.clone.sunk | while | flops 294903 | bytes 2556824 | solution.py:74
  627.5 51.8 %while.142 = (s32[]{:T(128)}, f32[12,64,64]{2,1,0:T(8,128)}, f32[8,12]{1,0:T(8,128)S(1)}, f32[8,12,64,64]{3,2,1,0:T(8,128)}, f32[8,12,64,64]{2,3,1,0:T(8,128)}, ...) while((s32[]{:T(128)}, f32[12,64,64]{2,1,0:T(8,128)}, ...), condition=%wide.region_44.46_spmd.clone, body=%wide.region_42.45_spmd.clone.sunk | while | flops 294903 | bytes 2556824 | solution.py:74
  696.0 51.5 %while.141 = (s32[]{:T(128)}, f32[12,64,64]{2,1,0:T(8,128)}, f32[8,12]{1,0:T(8,128)S(1)}, f32[8,12,64,64]{3,2,1,0:T(8,128)}, f32[8,12,64,64]{2,3,1,0:T(8,128)}, ...) while((s32[]{:T(128)}, f32[12,64,64]{2,1,0:T(8,128)}, ...), condition=%wide.region_25.27_spmd.clone, body=%wide.region_23.26_spmd.clone.sunk | while | flops 294904 | bytes 2556336 | solution.py:73
  747.5 12.4 multiply_reduce_fusion.15
  765.8 51.8 %while.143 = (s32[]{:T(128)}, f32[12,64,64]{2,1,0:T(8,128)}, f32[8,12]{1,0:T(8,128)S(1)}, f32[8,12,64,64]{3,2,1,0:T(8,128)}, f32[8,12,64,64]{2,3,1,0:T(8,128)}, ...) while((s32[]{:T(128)}, f32[12,64,64]{2,1,0:T(8,128)}, ...), condition=%wide.region_47.49_spmd.clone, body=%wide.region_45.48_spmd.clone.sunk | while | flops 294904 | bytes 2556336 | solution.py:73
  838.3 27.9 %fusion.43 = (f32[8,12,128]{2,1,0:T(8,128)}, f32[8,12,128]{2,1,0:T(8,128)}, f32[8,12,128]{2,1,0:T(8,128)}, f32[8,12,128]{2,1,0:T(8,128)}, f32[8,128,128]{2,1,0:T...) fusion(f32[8,12,128]{2,1,0:T(8,128)S(1)} %copy-done.141, ...), kind=kOutput, calls=%fused_computation.89 | convolution fusion | flops 1258717184 | bytes 15351808 | tf_op jit(solution)/shard_map/transpose(jvp(chij,chjp->cihp))/dot_general | solution.py:61
  1023.1 41.6 %all-reduce.42 = (f32[768]{0:T(1024)}, f32[4,1536]{1,0:T(4,128)S(1)}, f32[4,128]{1,0:T(4,128)}, f32[24]{0:T(128)S(1)}, f32[24]{0:T(128)S(1)}, /*index=5*/f32[24]{0:T(128)S(1)}, f32[1536]{0:T(1024)S(1)}) all-reduce(f32[768]{0:T(1024)S(1)} %add.463, ...), channel_id=1, replica_groups=mesh['dp'=16,'tensor'=2] {'dp','tensor'}, use_global_device_ids=true, to_apply=%region_64.66 | all-reduce | flops 9032 | bytes 72256 | tf_op jit(solution)/shard_map/psum | solution.py:266
  1073.4 97.9 %reduce-scatter.15.cloned.1.call-done = f32[48,1676]{1,0:T(8,128)} async-done(((f32[768,1676]{1,0:T(8,128)}), f32[48,1676]{1,0:T(8,128)}) %reduce-scatter.15.cloned.1.call-update) | async-done | bytes 321808 | tf_op jit(solution)/shard_map/reduce_scatter | solution.py:263
  1175.8 128.2 %reduce-scatter.17.cloned.1.call-done = f32[768,48]{0,1:T(8,128)} async-done(((f32[768,768]{0,1:T(8,128)}), f32[768,48]{0,1:T(8,128)}) %reduce-scatter.17.cloned.1.call-update) | async-done | bytes 147472 | tf_op jit(solution)/shard_map/reduce_scatter | solution.py:264
  (1082 shorter events, 749.5 us)
Async XLA Ops:
  7.2 96.8 %all-gather.17.cloned.1.call-start = ((), (), s32[]{:S(2)}) async-start(), calls=%async_computation.11 | async-start | bytes 2359296 | tf_op jit(solution)/shard_map/all_gather | solution.py:167
  12.7 91.3 %all-gather.11.cloned.1.call-start = ((), (), s32[]{:S(2)}) async-start(), calls=%async_computation.7 | async-start | bytes 1253376 | tf_op jit(solution)/shard_map/all_gather | solution.py:150
  13.5 88.5 %copy-start.214 = (f32[12]{0:T(128)S(1)}, f32[12]{0:T(128)}, u32[]{:S(2)}) copy-start(f32[12]{0:T(128)} %param.43) | copy-start | bytes 148
  13.5 88.5 %copy-start.188 = (f32[4,768]{1,0:T(4,128)S(1)}, f32[4,768]{1,0:T(4,128)}, u32[]{:S(2)}) copy-start(f32[4,768]{1,0:T(4,128)} %param.40) | copy-start | bytes 36868
  13.5 130.4 %all-gather.13.cloned.1.call-start = ((), (), s32[]{:S(2)}) async-start(), calls=%async_computation.8 | async-start | bytes 1253376 | tf_op jit(solution)/shard_map/all_gather | solution.py:151
  14.2 88.4 %copy-start.207 = (f32[4,128]{1,0:T(4,128)S(1)}, f32[4,128]{1,0:T(4,128)}, u32[]{:S(2)}) copy-start(f32[4,128]{1,0:T(4,128)} %param.41) | copy-start | bytes 6148
  14.2 140.3 %all-gather.9.cloned.1.call-start = ((), (), s32[]{:S(2)}) async-start(), calls=%async_computation.6 | async-start | bytes 2359296 | tf_op jit(solution)/shard_map/all_gather | solution.py:167
  14.8 455.5 %all-gather.21.cloned.1.call-start = ((), (), s32[]{:S(2)}) async-start(), calls=%async_computation.15 | async-start | bytes 2359296 | tf_op jit(solution)/shard_map/all_gather | solution.py:201
  18.3 452.0 %all-gather.15.cloned.1.call-start = ((), (), s32[]{:S(2)}) async-start(), calls=%async_computation.9 | async-start | bytes 1253376 | tf_op jit(solution)/shard_map/all_gather | solution.py:154
  18.9 456.3 %all-gather.19.cloned.1.call-start = ((), (), s32[]{:S(2)}) async-start(), calls=%async_computation.13 | async-start | bytes 2359296 | tf_op jit(solution)/shard_map/all_gather | solution.py:201
  19.6 937.7 %all-reduce.48.cloned.1.call-start = ((), (), s32[]{:S(2)}) async-start(), calls=%async_computation.19 | async-start | bytes 1048576 | tf_op jit(solution)/shard_map/psum | solution.py:217
  65.2 89.4 %copy-start.107 = (bf16[16,48,12]{2,1,0:T(8,128)(2,1)}, bf16[16,48,12]{2,1,0:T(8,128)(2,1)S(1)}, u32[]{:S(2)}) copy-start(bf16[16,48,12]{2,1,0:T(8,128)(2,1)S(1)} %copy.690) | copy-start | bytes 55300
  102.6 108.4 %copy-start.155 = (f32[768]{0:T(1024)}, f32[768]{0:T(1024)S(1)}, u32[]{:S(2)}) copy-start(f32[768]{0:T(1024)S(1)} %get-tuple-element.1221) | copy-start | bytes 9220
  102.6 108.4 %copy-start.157 = (f32[768]{0:T(1024)}, f32[768]{0:T(1024)S(1)}, u32[]{:S(2)}) copy-start(f32[768]{0:T(1024)S(1)} %get-tuple-element.1222) | copy-start | bytes 9220
  225.3 104.7 %copy-start = (f32[96,8,8,128]{3,2,1,0:T(8,128)}, f32[96,8,8,128]{3,2,1,0:T(8,128)S(1)}, u32[]{:S(2)}) copy-start(f32[96,8,8,128]{3,2,1,0:T(8,128)S(1)} %copy.724) | copy-start | bytes 9437188
  353.3 86.7 %copy-start.4 = (f32[96,8,8,128]{3,2,1,0:T(8,128)}, f32[96,8,8,128]{3,2,1,0:T(8,128)S(1)}, u32[]{:S(2)}) copy-start(f32[96,8,8,128]{3,2,1,0:T(8,128)S(1)} %copy.716) | copy-start | bytes 9437188
  437.6 70.3 %copy-start.144 = (f32[8,12,128]{2,1,0:T(8,128)}, f32[8,12,128]{2,1,0:T(8,128)S(1)}, u32[]{:S(2)}) copy-start(f32[8,12,128]{2,1,0:T(8,128)S(1)} %copy.508) | copy-start | bytes 147460
  440.0 67.9 %copy-start.140 = (f32[8,12,128]{2,1,0:T(8,128)}, f32[8,12,128]{2,1,0:T(8,128)S(1)}, u32[]{:S(2)}) copy-start(f32[8,12,128]{2,1,0:T(8,128)S(1)} %copy.505) | copy-start | bytes 147460
  937.1 82.9 %reduce-scatter.13.cloned.1.call-start = ((), (), s32[]{:S(2)}) async-start(), calls=%async_computation.16 | async-start | bytes 2359296 | tf_op jit(solution)/shard_map/reduce_scatter | solution.py:238
  972.0 48.0 %reduce-scatter.11.cloned.1.call-start = ((), (), s32[]{:S(2)}) async-start(), calls=%async_computation.14 | async-start | bytes 2359296 | tf_op jit(solution)/shard_map/reduce_scatter | solution.py:238
  986.9 80.9 %reduce-scatter.9.cloned.1.call-start = ((), (), s32[]{:S(2)}) async-start(), calls=%async_computation.12 | async-start | bytes 2359296 | tf_op jit(solution)/shard_map/reduce_scatter | solution.py:191
  991.0 76.8 %reduce-scatter.7.cloned.1.call-start = ((), (), s32[]{:S(2)}) async-start(), calls=%async_computation.10 | async-start | bytes 2359296 | tf_op jit(solution)/shard_map/reduce_scatter | solution.py:191
  996.1 175.2 %reduce-scatter.15.cloned.1.call-start = ((), (), s32[]{:S(2)}) async-start(), calls=%async_computation.17 | async-start | bytes 5849088 | tf_op jit(solution)/shard_map/reduce_scatter | solution.py:263
  1011.4 292.6 %reduce-scatter.17.cloned.1.call-start = ((), (), s32[]{:S(2)}) async-start(), calls=%async_computation.18 | async-start | bytes 2506752 | tf_op jit(solution)/shard_map/reduce_scatter | solution.py:264
  (209 other events, 1625.0 us)
Sparse Core Ops, SparseCore 0:
  12.8 12.4 all-gather.16
  28.1 57.7 all-gather.10
  88.8 55.0 all-gather.12
  145.8 8.6 all-gather.8
  155.9 10.9 all-gather.20
  169.6 57.2 all-gather.14
  228.5 8.6 all-gather.18
  937.2 19.9 all-reduce.47
  972.2 10.2 reduce-scatter.12
  987.0 10.2 reduce-scatter.10
  999.6 10.2 reduce-scatter.8
  1012.0 10.3 reduce-scatter.6
  1028.5 142.8 reduce-scatter.14
  1177.4 126.5 reduce-scatter.16
where the time goes:
time: 1320 us; the launch traced here: 1310 us
  other arithmetic  348 us (26%)
  matrix products  304 us (23%)
  waiting for transfers between devices  276 us (21%)
  local copies, waits for them, and re-layouts  239 us (18%)
  blocking collectives  126 us (10%)
  between operations  16.9 us (1%)
    reduce_scatter x1, waiting for transfers between devices, on_device(): lax.psum_scatter(total_out, 'dp', scatter_dimension=1, tiled=True)  128 us
    reduce_scatter x1, waiting for transfers between devices, on_device(): lax.psum_scatter(total_in, 'dp', scatter_dimension=0, tiled=True)  97.9 us
    dot_general x6, matrix products, mix_heads(): jnp.einsum('chij,chjp->cihp', coupling, scaled_heads, precision=precise)  93.9 us
    dynamic_update_slice x64, other arithmetic, mix_heads(): lax.scan(carry_step, empty_state, (carry_decay, gained_ahead))  71 us
    reduce_sum x32, other arithmetic, carry_step(): return (block_decay[:, None, None] * state_now + gained_state, state_now)  66.1 us
    dynamic_slice x64, local copies, waits for them, and re-layouts, mix_heads(): lax.scan(carry_step, empty_state, (carry_decay, gained_ahead))  62.6 us
    add x32, other arithmetic, carry_step(): return (block_decay[:, None, None] * state_now + gained_state, state_now)  55.8 us
    dot_general x6, matrix products, mix_heads(): jnp.einsum('cjh,cjs,cjhp->chsp', decay_out, b_rows, scaled, precision=pre...  48.9 us
  transfers between devices with their start and end apart: 14, of which 5 were waited for; matrix products, arithmetic and copies ran while one was open for 31% of the time, Pallas kernels for 0%

commit v1 on v0

v1 whole, which is shorter than its diff:
```python
import functools

import jax
import jax.numpy as jnp
from jax import lax
from jax.experimental import pallas as pl
from jax.experimental.pallas import tpu as pltpu
from jax.sharding import PartitionSpec as P

BLOCK = 128
HEAD = 64
STATE = 64
GROUP = 256
LOG2E = 1.4426950408889634
epsilon = 1e-05
f32 = jnp.float32
bf16 = jnp.bfloat16
ANY = pl.ANY


def dot(a, b):
    return lax.dot_general(a, b, (((1,), (0,)), ((), ())), preferred_element_type=f32)


def dot_nt(a, b):
    return lax.dot_general(a, b, (((1,), (1,)), ((), ())), preferred_element_type=f32)


def dot_full(a, b):
    return lax.dot_general(
        a, b, (((1,), (0,)), ((), ())), preferred_element_type=f32, precision=lax.Precision.HIGHEST
    )


def iota(shape, axis):
    return lax.broadcasted_iota(jnp.int32, shape, axis)


def chunk(c):
    return pl.ds(pl.multiple_of(c * BLOCK, BLOCK), BLOCK)


def halo(c):
    return pl.ds(pl.multiple_of(c * BLOCK, BLOCK), BLOCK + 8)


def sigmoid(v):
    return 1.0 / (1.0 + jnp.exp(-v))


def conv_taps(padded, taps_ref):
    total = padded[8 : 8 + BLOCK] * taps_ref[3:4]
    for back in range(1, 4):
        total = total + padded[8 - back : 8 - back + BLOCK] * taps_ref[3 - back : 4 - back]
    return total


def lane_low():
    return iota((BLOCK, 2 * HEAD), 1) < HEAD


def spread(block, column):
    return jnp.broadcast_to(block[:, column : column + 1], (BLOCK, BLOCK))


def pair_rows(piece, low):
    return jnp.concatenate(
        (jnp.where(low, piece, 0.0), jnp.where(low, 0.0, piece)), axis=0
    ).astype(bf16)


def prep_kernel(
    normed, selector, timestep, kernels, biases, rates,
    select_in, b_rows, c_rows, select_t, gram, gram_t,
    ends, starts, steps, ends_t, starts_t, steps_t, slope_t, padded,
):
    chunks = normed.shape[0] // BLOCK
    groups = ends_t.shape[0]
    per = GROUP // HEAD
    down = iota((BLOCK, BLOCK), 0)
    across = iota((BLOCK, BLOCK), 1)
    tri = (down >= across).astype(f32)
    off = (down != across).astype(f32)
    padded[0:8] = jnp.zeros((8, BLOCK), f32)

    def project(c, carry):
        rows = chunk(c)
        selected = dot(normed[rows], selector[...])
        select_in[rows] = selected
        padded[pl.ds(pl.multiple_of(c * BLOCK + 8, 8), BLOCK)] = selected
        return carry

    lax.fori_loop(0, chunks, project, 0)

    def body(c, carry):
        rows = chunk(c)
        tokens = normed[rows]
        pre = conv_taps(padded[halo(c)], kernels)
        act = pre * sigmoid(pre)
        act_t = act.T.astype(bf16)
        act = act.astype(bf16)
        b_rows[rows] = act[:, :STATE]
        c_rows[rows] = act[:, STATE:]
        select_t[c] = act_t
        gram[c] = dot(act[:, STATE:], act_t[:STATE]) * off
        gram_t[c] = dot(act[:, :STATE], act_t[STATE:]) * off
        logits = dot(tokens, timestep[...]) + biases[...]
        small = jnp.exp(-jnp.abs(logits))
        whole = 1.0 + small
        log_part = jnp.where(
            whole == 1.0, small, jnp.log(whole) * (small / jnp.where(whole == 1.0, 1.0, whole - 1.0))
        )
        step = jnp.maximum(logits, 0.0) + log_part
        decay = -rates[...] * step
        inclusive = dot_full(tri, decay)
        end = inclusive * LOG2E
        start = (inclusive - decay) * LOG2E
        ends[rows] = end
        starts[rows] = start
        steps[rows] = step
        turned = ((ends_t, end), (starts_t, start), (steps_t, step), (slope_t, sigmoid(logits)))
        for target, value in turned:
            value_t = value.T
            for g in range(groups):
                target[g, 0:per, rows] = value_t[g * per : (g + 1) * per]
        return carry

    lax.fori_loop(0, chunks, body, 0)


def roll_heads(source, target, base):
    shift = lax.rem(BLOCK - base, BLOCK)
    target[...] = pltpu.roll(source[...], shift, 1)


def mix_kernel(
    half, length, normed, content, filters, shortcut, c_rows, select_t, gram,
    ends, starts, steps, ends_t, starts_t,
    mixed, x_low, values, early, late,
    padded, ends_g, starts_g, steps_g, scaled, gain_e, gain_l, totals,
):
    heads_half = pl.num_programs(0) * (GROUP // HEAD)
    base = half * heads_half + pl.program_id(0) * (GROUP // HEAD)
    chunks = normed.shape[0] // BLOCK
    pairs = GROUP // (2 * HEAD)
    roll_heads(ends, ends_g, base)
    roll_heads(starts, starts_g, base)
    roll_heads(steps, steps_g, base)
    padded[0:8] = jnp.zeros((8, GROUP), f32)

    def project(c, carry):
        rows = chunk(c)
        block = dot(normed[rows], content[...])
        padded[pl.ds(pl.multiple_of(c * BLOCK + 8, 8), BLOCK)] = block
        values[rows] = block.astype(bf16)
        return carry

    lax.fori_loop(0, chunks, project, 0)

    def gains(c, carry):
        rows = chunk(c)
        pre = conv_taps(padded[halo(c)], filters)
        inside = (c * BLOCK + iota((BLOCK, GROUP), 0)) < length[0]
        act = jnp.where(inside, pre * sigmoid(pre), 0.0).astype(bf16)
        x_low[rows] = act
        low = lane_low()
        end_block = ends_g[rows]
        start_block = starts_g[rows]
        step_block = steps_g[rows]
        for p in range(pairs):
            lanes = slice(2 * HEAD * p, 2 * HEAD * (p + 1))
            end = jnp.where(low, spread(end_block, 2 * p), spread(end_block, 2 * p + 1))
            start = jnp.where(low, spread(start_block, 2 * p), spread(start_block, 2 * p + 1))
            step = jnp.where(low, spread(step_block, 2 * p), spread(step_block, 2 * p + 1))
            total = end[BLOCK - 1 : BLOCK]
            xs = act[:, lanes].astype(f32) * step
            scaled[rows, lanes] = xs
            totals[c, :, lanes] = jnp.broadcast_to(total, (8, 2 * HEAD))
            both = jnp.concatenate((jnp.exp2(total - end) * xs, jnp.exp2(start) * xs), axis=1)
            gain = dot(select_t[c, :STATE], both.astype(bf16))
            gain_e[c, :, lanes] = gain[:, : 2 * HEAD]
            gain_l[c, :, lanes] = gain[:, 2 * HEAD :]
        return carry

    lax.fori_loop(0, chunks, gains, 0)

    state = jnp.zeros((STATE, GROUP), f32)
    for c in range(chunks):
        early[c] = state.astype(bf16)
        state = jnp.exp2(totals[c, :1]) * state + gain_e[c]
    state = jnp.zeros((STATE, GROUP), f32)
    for c in reversed(range(chunks)):
        late[c] = state.astype(bf16)
        state = jnp.exp2(totals[c, :1]) * state + gain_l[c]

    def mix(c, carry):
        rows = chunk(c)
        low = lane_low()
        end_block = ends_g[rows]
        start_block = starts_g[rows]
        coupled = gram[c]
        for p in range(pairs):
            lanes = slice(2 * HEAD * p, 2 * HEAD * (p + 1))
            ends_p = [spread(end_block, 2 * p + k) for k in range(2)]
            starts_p = [spread(start_block, 2 * p + k) for k in range(2)]
            coupling = []
            for k in range(2):
                end_row = ends_t[0, 2 * p + k : 2 * p + k + 1, rows]
                start_row = starts_t[0, 2 * p + k : 2 * p + k + 1, rows]
                power = jnp.exp2(jnp.minimum(ends_p[k] - end_row, start_row - starts_p[k]))
                coupling.append((coupled * power).astype(bf16))
            xs = scaled[rows, lanes]
            inner = dot(jnp.concatenate(coupling, axis=1), pair_rows(xs, low))
            states = jnp.concatenate((early[c, :, lanes], late[c, :, lanes]), axis=1)
            outer = dot(c_rows[rows], states)
            end = jnp.where(low, ends_p[0], ends_p[1])
            start = jnp.where(low, starts_p[0], starts_p[1])
            total = end[BLOCK - 1 : BLOCK]
            mixed[rows, lanes] = (
                inner
                + jnp.exp2(end) * outer[:, : 2 * HEAD]
                + jnp.exp2(total - start) * outer[:, 2 * HEAD :]
                + shortcut[:, lanes] * x_low[rows, lanes].astype(f32)
            )
        return carry

    lax.fori_loop(0, chunks, mix, 0)


def gate_kernel(
    first, last, inner_width, *refs
):
    refs = list(refs)
    length, normed, gating, out_t, amplitude, mixed = refs[:6]
    refs = refs[6:]
    if not first:
        squares_in, total_in = refs[:2]
        refs = refs[2:]
    if last:
        tokens, cotangent = refs[:2]
        refs = refs[2:]
        gate_out, scale_out, cross_out, layer_out, squares, total = refs
    else:
        gate_out, squares, total = refs
    chunks = normed.shape[0] // BLOCK
    step = pl.program_id(0)

    @pl.when(step == 0)
    def _():
        if first:
            squares[...] = jnp.zeros(squares.shape, f32)
            total[...] = jnp.zeros(total.shape, f32)
        else:
            squares[...] = squares_in[...]
            total[...] = total_in[...]

    def body(c, carry):
        rows = chunk(c)
        gate = dot(normed[rows], gating[...])
        gate_out[rows] = gate
        gated = mixed[rows] * (gate * sigmoid(gate))
        square = gated * gated
        squares[rows] += square[:, : GROUP // 2] + square[:, GROUP // 2 :]
        total[rows] += dot_nt((gated * amplitude[...]).astype(bf16), out_t[...])
        return carry

    lax.fori_loop(0, chunks, body, 0)

    if last:

        @pl.when(step == pl.num_programs(0) - 1)
        def _():
            def finish(c, carry):
                rows = chunk(c)
                mean = jnp.sum(squares[rows], axis=1, keepdims=True) / inner_width
                scale = lax.rsqrt(mean + epsilon)
                inside = (c * BLOCK + iota((BLOCK, 1), 0)) < length[0]
                projected = total[rows]
                sum_out = tokens[rows].astype(f32) + scale * projected
                layer_out[rows] = jnp.where(inside, sum_out, 0.0).astype(bf16)
                inner = jnp.sum(cotangent[rows].astype(f32) * projected, axis=1, keepdims=True)
                cross = scale * scale * scale * inner / inner_width
                scale_out[rows] = jnp.broadcast_to(scale, (BLOCK, BLOCK))
                cross_out[rows] = jnp.broadcast_to(cross, (BLOCK, BLOCK))
                return carry

            lax.fori_loop(0, chunks, finish, 0)


def gate_back_kernel(
    cotangent, cotangent_t, normed_t, out_t, amplitude, mixed, gate_in, x_low, scale_in, cross_in,
    mixed_grad, gate_grad, gating_grad, out_grad, amplitude_grad, shortcut_grad, gated_s,
):
    chunks = cotangent.shape[0] // BLOCK

    def body(c, carry):
        amplitude_sum, shortcut_sum = carry
        rows = chunk(c)
        dgated = dot(cotangent[rows], out_t[...])
        gate = gate_in[rows]
        sig = sigmoid(gate)
        act = gate * sig
        slope = sig * (1.0 + gate * (1.0 - sig))
        y = mixed[rows]
        gz = y * act
        scale = jnp.concatenate((scale_in[rows], scale_in[rows]), axis=1)
        cross = jnp.concatenate((cross_in[rows], cross_in[rows]), axis=1)
        unit = gz * scale
        gated_s[rows] = (unit * amplitude[...]).astype(bf16)
        dgz = scale * (amplitude[...] * dgated) - gz * cross
        gate_grad[rows] = (dgz * y * slope).astype(bf16)
        dmix = dgz * act
        mixed_grad[rows] = dmix.astype(bf16)
        amplitude_sum = amplitude_sum + jnp.sum(dgated * unit, axis=0, keepdims=True)
        shortcut_sum = shortcut_sum + jnp.sum(
            dmix * x_low[rows].astype(f32), axis=0, keepdims=True
        )
        return amplitude_sum, shortcut_sum

    zero = jnp.zeros((1, GROUP), f32)
    amplitude_sum, shortcut_sum = lax.fori_loop(0, chunks, body, (zero, zero))
    amplitude_grad[...] = amplitude_sum
    shortcut_grad[...] = shortcut_sum
    gating_grad[...] = dot(normed_t[...], gate_grad[...]).astype(bf16)
    out_grad[...] = dot(cotangent_t[...], gated_s[...]).astype(bf16)


def mix_back_kernel(half, first, last, *refs):
    refs = list(refs)
    (
        length, normed_t, filters, shortcut, b_rows, c_rows, select_t, gram_t,
        ends, starts, steps, ends_t, starts_t, mixed_grad, x_low, values, early, late,
    ) = refs[:18]
    refs = refs[18:]
    if not first:
        gram_in, b_in, c_in = refs[:3]
        refs = refs[3:]
    (
        values_grad, content_grad, filters_grad, decay_grad, direct_grad, gram_grad, b_grad, c_grad,
        padded, ends_g, starts_g, steps_g, pre_grad, gain_e, gain_l, totals,
        early_grad, late_grad, sums, inside_sums, through,
    ) = refs
    step_id = pl.program_id(0)
    heads_half = pl.num_programs(0) * (GROUP // HEAD)
    base = half * heads_half + step_id * (GROUP // HEAD)
    rows_all = x_low.shape[0]
    chunks = rows_all // BLOCK
    pairs = GROUP // (2 * HEAD)

    @pl.when(step_id == 0)
    def _():
        if first:
            gram_grad[...] = jnp.zeros(gram_grad.shape, f32)
            b_grad[...] = jnp.zeros(b_grad.shape, f32)
            c_grad[...] = jnp.zeros(c_grad.shape, f32)
        else:
            gram_grad[...] = gram_in[...]
            b_grad[...] = b_in[...]
            c_grad[...] = c_in[...]

    roll_heads(ends, ends_g, base)
    roll_heads(starts, starts_g, base)
    roll_heads(steps, steps_g, base)
    padded[0:8] = jnp.zeros((8, GROUP), f32)
    pre_grad[rows_all : rows_all + 8] = jnp.zeros((8, GROUP), f32)

    def gains(c, carry):
        rows = chunk(c)
        low = lane_low()
        padded[pl.ds(pl.multiple_of(c * BLOCK + 8, 8), BLOCK)] = values[rows].astype(f32)
        end_block = ends_g[rows]
        start_block = starts_g[rows]
        for p in range(pairs):
            lanes = slice(2 * HEAD * p, 2 * HEAD * (p + 1))
            end = jnp.where(low, spread(end_block, 2 * p), spread(end_block, 2 * p + 1))
            start = jnp.where(low, spread(start_block, 2 * p), spread(start_block, 2 * p + 1))
            total = end[BLOCK - 1 : BLOCK]
            totals[c, :, lanes] = jnp.broadcast_to(total, (8, 2 * HEAD))
            dy = mixed_grad[rows, lanes].astype(f32)
            both = jnp.concatenate((jnp.exp2(end) * dy, jnp.exp2(total - start) * dy), axis=1)
            gain = dot(select_t[c, STATE:], both.astype(bf16))
            gain_e[c, :, lanes] = gain[:, : 2 * HEAD]
            gain_l[c, :, lanes] = gain[:, 2 * HEAD :]
        return carry

    lax.fori_loop(0, chunks, gains, 0)

    state = jnp.zeros((STATE, GROUP), f32)
    for c in reversed(range(chunks)):
        early_grad[c] = state.astype(bf16)
        kept = jnp.exp2(totals[c, :1]) * state
        through[c : c + 1] = jnp.sum(kept * early[c].astype(f32), axis=0, keepdims=True)
        state = kept + gain_e[c]
    state = jnp.zeros((STATE, GROUP), f32)
    for c in range(chunks):
        late_grad[c] = state.astype(bf16)
        kept = jnp.exp2(totals[c, :1]) * state
        through[c : c + 1] += jnp.sum(kept * late[c].astype(f32), axis=0, keepdims=True)
        state = kept + gain_l[c]

    down = iota((BLOCK, BLOCK), 0)
    across = iota((BLOCK, BLOCK), 1)

    def mix(c, carry):
        rows = chunk(c)
        low = lane_low()
        both_tri = jnp.concatenate((down >= across, down <= across), axis=1).astype(f32).astype(bf16)
        end_block = ends_g[rows]
        start_block = starts_g[rows]
        step_block = steps_g[rows]
        coupled = gram_t[c]
        gram_sum = gram_grad[c]
        b_sum = b_grad[rows]
        c_sum = c_grad[rows]
        lane_sums = [jnp.zeros((8, BLOCK), f32) for _ in range(5)]
        head_rows = []
        for p in range(pairs):
            lanes = slice(2 * HEAD * p, 2 * HEAD * (p + 1))
            ends_p = [spread(end_block, 2 * p + k) for k in range(2)]
            starts_p = [spread(start_block, 2 * p + k) for k in range(2)]
            end = jnp.where(low, ends_p[0], ends_p[1])
            start = jnp.where(low, starts_p[0], starts_p[1])
            total = end[BLOCK - 1 : BLOCK]
            step = jnp.where(low, spread(step_block, 2 * p), spread(step_block, 2 * p + 1))
            x = x_low[rows, lanes].astype(f32)
            dy = mixed_grad[rows, lanes].astype(f32)
            xs = x * step
            dy_rows = pair_rows(dy, low)
            powers = []
            coupling = []
            for k in range(2):
                end_row = ends_t[0, 2 * p + k : 2 * p + k + 1, rows]
                start_row = starts_t[0, 2 * p + k : 2 * p + k + 1, rows]
                power = jnp.exp2(jnp.minimum(end_row - ends_p[k], starts_p[k] - start_row))
                powers.append(power)
                coupling.append((coupled * power).astype(bf16))
            coupling_both = jnp.concatenate(coupling, axis=1)
            inner = dot(coupling_both, dy_rows)
            pair_products = dot_nt(xs.astype(bf16), dy_rows)
            for k in range(2):
                product = pair_products[:, BLOCK * k : BLOCK * (k + 1)]
                gram_sum = gram_sum + product * powers[k]
                spread_log = (product * coupling[k].astype(f32)).astype(bf16)
                crossing = dot(spread_log, both_tri)
                picked = jnp.where(
                    down < across,
                    crossing[:, :BLOCK],
                    jnp.where(down > across, crossing[:, BLOCK:], 0.0),
                )
                head_rows.append(jnp.sum(picked, axis=0, keepdims=True))
            states = jnp.concatenate((early[c, :, lanes], late[c, :, lanes]), axis=1)
            states_grad = jnp.concatenate((early_grad[c, :, lanes], late_grad[c, :, lanes]), axis=1)
            raw_y = dot(c_rows[rows], states)
            raw_x = dot(b_rows[rows], states_grad)
            dy_both = jnp.concatenate((jnp.exp2(end) * dy, jnp.exp2(total - start) * dy), axis=1)
            weight_both = jnp.concatenate((jnp.exp2(total - end), jnp.exp2(start)), axis=1)
            xs_both = jnp.concatenate((xs, xs), axis=1) * weight_both
            outer_both = weight_both * raw_x
            c_sum = c_sum + dot_nt(dy_both.astype(bf16), states)
            b_sum = b_sum + dot_nt(xs_both.astype(bf16), states_grad)
            grad_xs = inner + outer_both[:, : 2 * HEAD] + outer_both[:, 2 * HEAD :]
            from_y = dy_both * raw_y
            from_x = xs_both * raw_x
            products = (
                from_y[:, : 2 * HEAD],
                from_y[:, 2 * HEAD :],
                from_x[:, : 2 * HEAD],
                from_x[:, 2 * HEAD :],
                x * grad_xs,
            )
            row_id = iota((8, BLOCK), 0)
            lane_id = iota((8, BLOCK), 1)
            pick = (row_id == 2 * p + lane_id // HEAD).astype(f32).astype(bf16)
            for q in range(5):
                lane_sums[q] = lane_sums[q] + dot_nt(pick, products[q].astype(bf16))
            pre_grad[rows, lanes] = step * grad_xs + shortcut[:, lanes] * dy
        gram_grad[c] = gram_sum
        b_grad[rows] = b_sum
        c_grad[rows] = c_sum
        tile = pl.ds(pl.multiple_of(c * 8, 8), 8)
        for q in range(5):
            sums[q, tile] = lane_sums[q]
        inside_sums[tile] = jnp.concatenate(head_rows + [jnp.zeros((4, BLOCK), f32)], axis=0)
        return carry

    lax.fori_loop(0, chunks, mix, 0)

    head_cols = (iota((GROUP, BLOCK), 0) // HEAD == iota((GROUP, BLOCK), 1)).astype(f32)
    through_heads = dot_full(through[...], head_cols)
    tall = 8 * chunks
    chunk_rows = (iota((tall, chunks), 0) // 8 == iota((tall, chunks), 1)).astype(f32)
    through_tall = dot_full(chunk_rows, through_heads)
    own = iota((tall, BLOCK), 1) == iota((tall, BLOCK), 0) % 8
    through_rows = jnp.sum(jnp.where(own, through_tall, 0.0), axis=1, keepdims=True)
    decay_grad[0] = (
        inside_sums[...]
        + dot_full(sums[0], (down >= across).astype(f32))
        + dot_full(sums[1], (down <= across).astype(f32))
        + dot_full(sums[2], (down < across).astype(f32))
        + dot_full(sums[3], (down > across).astype(f32))
        + through_rows
    )
    direct_grad[0] = sums[4]

    def conv_back(c, carry):
        rows = chunk(c)
        window = padded[halo(c)]
        pre = conv_taps(window, filters)
        sig = sigmoid(pre)
        inside = (c * BLOCK + iota((BLOCK, GROUP), 0)) < length[0]
        grad = jnp.where(inside, pre_grad[rows] * (sig * (1.0 + pre * (1.0 - sig))), 0.0)
        pre_grad[rows] = grad
        return tuple(
            carry[k]
            + jnp.sum(grad * window[5 + k : 5 + k + BLOCK], axis=0, keepdims=True)
            for k in range(4)
        )

    zero = jnp.zeros((1, GROUP), f32)
    filter_sums = lax.fori_loop(0, chunks, conv_back, (zero,) * 4)
    filters_grad[...] = jnp.concatenate(filter_sums, axis=0)

    def conv_shift(c, carry):
        rows = chunk(c)
        window = pre_grad[halo(c)]
        total = window[:BLOCK] * filters[3:4]
        for ahead in range(1, 4):
            total = total + window[ahead : ahead + BLOCK] * filters[3 - ahead : 4 - ahead]
        values_grad[rows] = total.astype(bf16)
        return carry

    lax.fori_loop(0, chunks, conv_shift, 0)
    content_grad[...] = dot(normed_t[...], values_grad[...]).astype(bf16)

    if last:

        @pl.when(step_id == pl.num_programs(0) - 1)
        def _():
            def finish(c, carry):
                rows = chunk(c)
                grad = jnp.where(down != across, gram_grad[c], 0.0)
                b_grad[rows] += dot(grad.astype(bf16), c_rows[rows])
                c_grad[rows] += dot(grad.T.astype(bf16), b_rows[rows])
                return carry

            lax.fori_loop(0, chunks, finish, 0)


def whole(shape):
    return pl.BlockSpec(shape, lambda *_: (0,) * len(shape))


def columns(rows, width=GROUP, after=0):
    return pl.BlockSpec((rows, width), lambda g, *_: (0, g + after))


def planes(shape):
    return pl.BlockSpec(shape, lambda g, *_: (0,) * (len(shape) - 1) + (g,))


def turned(after, rows):
    return pl.BlockSpec((1, 8, rows), lambda g, *_: (g + after, 0, 0))


def lead(shape):
    return pl.BlockSpec((1,) + shape, lambda g, *_: (g,) + (0,) * len(shape))


scalar = pl.BlockSpec(memory_space=pltpu.SMEM)


def shaped(shape, dtype):
    return jax.ShapeDtypeStruct(shape, dtype)


def params(limit=60):
    return pltpu.CompilerParams(vmem_limit_bytes=limit << 20)


def prepare(normed, selector, timestep, kernels, biases, rates, heads):
    rows = normed.shape[0]
    chunks = rows // BLOCK
    groups = heads // (GROUP // HEAD)
    return pl.pallas_call(
        prep_kernel,
        out_shape=(
            shaped((rows, BLOCK), f32),
            shaped((rows, STATE), bf16),
            shaped((rows, STATE), bf16),
            shaped((chunks, BLOCK, BLOCK), bf16),
            shaped((chunks, BLOCK, BLOCK), f32),
            shaped((chunks, BLOCK, BLOCK), f32),
            shaped((rows, BLOCK), f32),
            shaped((rows, BLOCK), f32),
            shaped((rows, BLOCK), f32),
            shaped((groups, 8, rows), f32),
            shaped((groups, 8, rows), f32),
            shaped((groups, 8, rows), f32),
            shaped((groups, 8, rows), f32),
        ),
        scratch_shapes=[pltpu.VMEM((rows + 8, BLOCK), f32)],
        compiler_params=params(),
        name="prep",
    )(normed, selector, timestep, kernels, biases, rates)


def mix_forward(half, length, normed, content, filters, shortcut, prep, inner):
    (_, _, c_rows, select_t, gram, _, ends, starts, steps, ends_t, starts_t, _, _) = prep
    rows, width = normed.shape
    chunks = rows // BLOCK
    grid = inner // GROUP
    return pl.pallas_call(
        functools.partial(mix_kernel, half),
        grid=(grid,),
        in_specs=[
            scalar, whole(normed.shape), columns(width), columns(4), columns(1),
            whole(c_rows.shape), whole(select_t.shape), whole(gram.shape),
            whole(ends.shape), whole(starts.shape), whole(steps.shape),
            turned(half * grid, rows), turned(half * grid, rows),
        ],
        out_specs=(
            columns(rows), columns(rows), columns(rows),
            planes((chunks, STATE, GROUP)), planes((chunks, STATE, GROUP)),
        ),
        out_shape=(
            shaped((rows, inner), f32),
            shaped((rows, inner), bf16),
            shaped((rows, inner), bf16),
            shaped((chunks, STATE, inner), bf16),
            shaped((chunks, STATE, inner), bf16),
        ),
        scratch_shapes=[
            pltpu.VMEM((rows + 8, GROUP), f32),
            pltpu.VMEM((rows, BLOCK), f32),
            pltpu.VMEM((rows, BLOCK), f32),
            pltpu.VMEM((rows, BLOCK), f32),
            pltpu.VMEM((rows, GROUP), f32),
            pltpu.VMEM((chunks, STATE, GROUP), f32),
            pltpu.VMEM((chunks, STATE, GROUP), f32),
            pltpu.VMEM((chunks, 8, GROUP), f32),
        ],
        compiler_params=params(),
        name="mix",
    )(length, normed, content, filters, shortcut, c_rows, select_t, gram, ends, starts, steps, ends_t, starts_t)


def gate_forward(length, normed, weights, amplitude, mixed, carried, finals, inner_width):
    rows, width = normed.shape
    inner = mixed.shape[1]
    grid = inner // GROUP
    first = carried is None
    last = finals is not None
    ins = [length, normed, weights, weights, amplitude, mixed]
    specs = [scalar, whole(normed.shape), columns(width), columns(width, after=grid), columns(1), columns(rows)]
    if not first:
        ins += list(carried)
        specs += [whole(c.shape) for c in carried]
    outs = [shaped((rows, inner), f32)]
    out_specs = [columns(rows)]
    scratch = []
    if last:
        ins += list(finals)
        specs += [whole(c.shape) for c in finals]
        outs += [shaped((rows, BLOCK), f32), shaped((rows, BLOCK), f32), shaped((rows, width), bf16)]
        out_specs += [whole((rows, BLOCK)), whole((rows, BLOCK)), whole((rows, width))]
        scratch = [pltpu.VMEM((rows, BLOCK), f32), pltpu.VMEM((rows, width), f32)]
    else:
        outs += [shaped((rows, BLOCK), f32), shaped((rows, width), f32)]
        out_specs += [whole((rows, BLOCK)), whole((rows, width))]
    return pl.pallas_call(
        functools.partial(gate_kernel, first, last, inner_width),
        grid=(grid,),
        in_specs=specs,
        out_specs=tuple(out_specs),
        out_shape=tuple(outs),
        scratch_shapes=scratch,
        compiler_params=params(),
        name="gate",
    )(*ins)


def gate_backward(
    cotangent, cotangent_t, normed_t, weights, amplitude, mixed, gate_in, x_low, scale, cross
):
    rows, width = cotangent.shape
    inner = mixed.shape[1]
    return pl.pallas_call(
        gate_back_kernel,
        grid=(inner // GROUP,),
        in_specs=[
            whole(cotangent.shape), whole(cotangent_t.shape), whole(normed_t.shape),
            columns(width, after=inner // GROUP), columns(1), columns(rows), columns(rows),
            columns(rows), whole(scale.shape), whole(cross.shape),
        ],
        out_specs=(
            columns(rows), columns(rows), columns(width), columns(width), columns(1), columns(1),
        ),
        out_shape=(
            shaped((rows, inner), bf16),
            shaped((rows, inner), bf16),
            shaped((width, inner), bf16),
            shaped((width, inner), bf16),
            shaped((1, inner), f32),
            shaped((1, inner), f32),
        ),
        scratch_shapes=[pltpu.VMEM((rows, GROUP), bf16)],
        compiler_params=params(),
        name="gate_back",
    )(cotangent, cotangent_t, normed_t, weights, amplitude, mixed, gate_in, x_low, scale, cross)


def mix_backward(half, length, normed_t, filters, shortcut, prep, mixed_grad, kept, carried, last):
    (_, b_rows, c_rows, select_t, _, gram_t, ends, starts, steps, ends_t, starts_t, _, _) = prep
    _, x_low, values, early, late = kept
    width, rows = normed_t.shape
    inner = x_low.shape[1]
    chunks = rows // BLOCK
    grid = inner // GROUP
    first = carried is None
    shared = (b_rows, c_rows, select_t, gram_t, ends, starts, steps, ends_t, starts_t)
    ins = [length, normed_t, filters, shortcut, *shared, mixed_grad, x_low, values, early, late]
    specs = [scalar, whole(normed_t.shape), columns(4), columns(1)]
    specs += [whole(s.shape) for s in shared[:-2]] + [turned(half * grid, rows)] * 2
    specs += [columns(rows)] * 3 + [planes((chunks, STATE, GROUP))] * 2
    if not first:
        ins += list(carried)
        specs += [whole(c.shape) for c in carried]
    tall = 8 * chunks
    return pl.pallas_call(
        functools.partial(mix_back_kernel, half, first, last),
        grid=(grid,),
        in_specs=specs,
        out_specs=(
            columns(rows), columns(width), columns(4), lead((tall, BLOCK)), lead((tall, BLOCK)),
            whole((chunks, BLOCK, BLOCK)), whole((rows, STATE)), whole((rows, STATE)),
        ),
        out_shape=(
            shaped((rows, inner), bf16),
            shaped((width, inner), bf16),
            shaped((4, inner), f32),
            shaped((grid, tall, BLOCK), f32),
            shaped((grid, tall, BLOCK), f32),
            shaped((chunks, BLOCK, BLOCK), f32),
            shaped((rows, STATE), f32),
            shaped((rows, STATE), f32),
        ),
        scratch_shapes=[
            pltpu.VMEM((rows + 8, GROUP), f32),
            pltpu.VMEM((rows, BLOCK), f32),
            pltpu.VMEM((rows, BLOCK), f32),
            pltpu.VMEM((rows, BLOCK), f32),
            pltpu.VMEM((rows + 8, GROUP), f32),
            pltpu.VMEM((chunks, STATE, GROUP), f32),
            pltpu.VMEM((chunks, STATE, GROUP), f32),
            pltpu.VMEM((chunks, 8, GROUP), f32),
            pltpu.VMEM((chunks, STATE, GROUP), bf16),
            pltpu.VMEM((chunks, STATE, GROUP), bf16),
            pltpu.VMEM((5, tall, BLOCK), f32),
            pltpu.VMEM((tall, BLOCK), f32),
            pltpu.VMEM((chunks, GROUP), f32),
        ],
        compiler_params=params(),
        name="mix_back",
    )(*ins)


def shift_down(v, by):
    return jnp.pad(v, ((by, 0), (0, 0)))[: v.shape[0]]


def shift_up(v, by):
    return jnp.pad(v, ((0, by), (0, 0)))[by:]


def select_back(select_in, grad, kernels):
    taps = kernels.shape[0]
    shifted = [shift_down(select_in, taps - 1 - k) for k in range(taps)]
    pre = sum(shifted[k] * kernels[k] for k in range(taps))
    sig = sigmoid(pre)
    grad_pre = grad * (sig * (1.0 + pre * (1.0 - sig)))
    kernels_grad = jnp.stack([jnp.sum(grad_pre * shifted[k], axis=0) for k in range(taps)])
    select_grad = sum(shift_up(grad_pre, taps - 1 - k) * kernels[k] for k in range(taps))
    return select_grad, kernels_grad


def heads_to_rows(tall):
    grid, rows, tokens = tall.shape
    shaped_up = tall.reshape(grid, rows // 8, 8, tokens)[:, :, :4]
    return shaped_up.transpose(0, 2, 1, 3).reshape(grid * 4, (rows // 8) * tokens)


def tree_sum(terms):
    while len(terms) > 1:
        terms = [terms[k] + terms[k + 1] for k in range(0, len(terms), 2)]
    return terms[0]


PLANE = 4


def plane_pairs(size, by):
    return [(i, i - i % PLANE + ((i % PLANE) ^ by)) for i in range(size)]


def column_pairs(size, by):
    return [(i, ((i // PLANE) ^ by) * PLANE + i % PLANE) for i in range(size)]


def place_kernel(count, places, *refs):
    parts, target, sems = refs[:PLANE], refs[PLANE], refs[PLANE + 1]
    copies = []
    for k in range(PLANE):
        for s in range(count):
            slot = k * count + s
            copies.append(
                pltpu.make_async_copy(parts[k].at[s], target.at[places[slot]], sems.at[slot])
            )
    for copy in copies:
        copy.start()
    for copy in copies:
        copy.wait()


def gather_rows(local):
    size = lax.axis_size("dp")
    count = size // PLANE
    me = lax.axis_index("dp")
    pieces = [local] + [
        lax.ppermute(local, "dp", column_pairs(size, s)) for s in range(1, count)
    ]
    column = jnp.stack(pieces)
    parts = [column] + [
        lax.ppermute(column, "dp", plane_pairs(size, k)) for k in range(1, PLANE)
    ]
    high, low = me // PLANE, me % PLANE
    places = jnp.stack([(high ^ s) * PLANE + (low ^ k) for k in range(PLANE) for s in range(count)])
    placed = pl.pallas_call(
        functools.partial(place_kernel, count),
        in_specs=[scalar] + [pl.BlockSpec(memory_space=ANY)] * PLANE,
        out_specs=pl.BlockSpec(memory_space=ANY),
        out_shape=shaped((size,) + local.shape, local.dtype),
        scratch_shapes=[pltpu.SemaphoreType.DMA((PLANE * count,))],
        name="place",
    )(places.astype(jnp.int32), *parts)
    return placed.reshape(size * local.shape[0], local.shape[1])


def reduce_rows(total):
    size = lax.axis_size("dp")
    count = size // PLANE
    me = lax.axis_index("dp")
    high, low = me // PLANE, me % PLANE
    blocks = total.reshape(count, PLANE, total.shape[0] // size, total.shape[1])

    def of_plane(k):
        return lax.dynamic_index_in_dim(blocks, low ^ k, 1, keepdims=False)

    terms = [of_plane(0).astype(f32)] + [
        lax.ppermute(of_plane(k), "dp", plane_pairs(size, k)).astype(f32) for k in range(1, PLANE)
    ]
    column = tree_sum(terms)
    column_low = column.astype(bf16)

    def of_column(s, source):
        return lax.dynamic_index_in_dim(source, high ^ s, 0, keepdims=False)

    terms = [of_column(0, column)] + [
        lax.ppermute(of_column(s, column_low), "dp", column_pairs(size, s)).astype(f32)
        for s in range(1, count)
    ]
    return tree_sum(terms)


def sum_all(vector):
    size = lax.axis_size("dp")
    vector = tree_sum(
        [vector] + [lax.ppermute(vector, "dp", plane_pairs(size, k)) for k in range(1, PLANE)]
    )
    return tree_sum(
        [vector]
        + [lax.ppermute(vector, "dp", column_pairs(size, s)) for s in range(1, size // PLANE)]
    )


def swap(v):
    return lax.ppermute(v, "tensor", [(0, 1), (1, 0)])


def pad_columns(v, width):
    return jnp.pad(v, ((0, 0), (0, width - v.shape[1])))


def on_device(
    layer_in,
    upstream,
    lengths,
    rescale,
    gating,
    content,
    selector,
    timestep,
    filters,
    kernels,
    biases,
    decays,
    shortcut,
    amplitude,
    outgoing,
):
    parts = lax.axis_size("tensor")
    rank = lax.axis_index("tensor")
    micro = lengths.shape[0]
    half_rows = layer_in.shape[0] // micro
    rows = half_rows * parts
    width = layer_in.shape[1]
    inner = gating.shape[1]
    heads = timestep.shape[1]
    state_cols = selector.shape[1]
    inner_width = inner * parts

    first_local = jnp.concatenate((content, selector, pad_columns(timestep, BLOCK)), axis=1)
    second_local = jnp.concatenate((gating, outgoing.T), axis=1)
    first_own = gather_rows(first_local)
    first_other = swap(first_own)
    second_own = gather_rows(second_local)
    second_other = swap(second_own)

    def to_sequence(array):
        blocks = array.reshape(micro, half_rows, width)
        mine = lax.dynamic_index_in_dim(blocks, rank, 0, keepdims=False)
        got = swap(lax.dynamic_index_in_dim(blocks, 1 - rank, 0, keepdims=False))
        return jnp.where(
            rank == 0, jnp.concatenate((mine, got)), jnp.concatenate((got, mine))
        )

    def from_sequence(array):
        mine = lax.dynamic_slice_in_dim(array, rank * half_rows, half_rows, 0)
        got = swap(lax.dynamic_slice_in_dim(array, (1 - rank) * half_rows, half_rows, 0))
        return jnp.where(
            rank == 0, jnp.concatenate((mine, got)), jnp.concatenate((got, mine))
        )

    tokens = to_sequence(layer_in)
    cotangent = to_sequence(upstream)
    length = lax.dynamic_slice_in_dim(lengths, rank, 1, 0)

    flat = jnp.concatenate((filters.reshape(-1), amplitude, biases, decays, shortcut))
    flat_other = swap(flat)
    taps = filters.shape[0]

    def unpack(vector):
        edges = [0, taps * inner, (taps + 1) * inner]
        edges += [edges[-1] + heads * k for k in range(1, 4)]
        cut = [vector[a:b] for a, b in zip(edges[:-1], edges[1:])]
        return (cut[0].reshape(taps, inner), cut[1].reshape(1, inner), *cut[2:])

    filters_2, amplitude_2, biases_2, decays_2, shortcut_2 = zip(unpack(flat), unpack(flat_other))

    def head_lanes(pair):
        return pad_columns(jnp.concatenate(pair).reshape(1, -1), BLOCK)

    rates = jnp.exp(jnp.concatenate(decays_2))
    rate_lanes = pad_columns(rates.reshape(1, -1), BLOCK)
    shortcut_lanes = [jnp.repeat(s, HEAD).reshape(1, inner) for s in shortcut_2]
    split = inner + state_cols
    selector_full = first_own[:, inner:split]
    timestep_full = jnp.concatenate(
        (first_own[:, split : split + heads], first_other[:, split : split + heads]), axis=1
    )

    tok = tokens.astype(f32)
    inverse = lax.rsqrt(jnp.mean(tok * tok, axis=-1, keepdims=True) + epsilon)
    unit = tok * inverse
    normed = (unit * rescale).astype(bf16)
    inside = jnp.arange(rows)[:, None] < length[0]
    dbranch = jnp.where(inside, cotangent, jnp.zeros_like(cotangent))
    normed_t = normed.T
    dbranch_t = dbranch.T

    prep = prepare(
        normed, selector_full, pad_columns(timestep_full, BLOCK), kernels,
        head_lanes(biases_2), rate_lanes, 2 * heads,
    )
    firsts = (first_own, first_other)
    seconds = (second_own, second_other)
    kept = [
        mix_forward(h, length, normed, firsts[h], filters_2[h], shortcut_lanes[h], prep, inner)
        for h in range(2)
    ]
    gate_own, squares, total = gate_forward(
        length, normed, seconds[0], amplitude_2[0], kept[0][0], None, None, inner_width
    )
    gate_other, scale, cross, layer_seq = gate_forward(
        length, normed, seconds[1], amplitude_2[1], kept[1][0], (squares, total),
        (tokens, dbranch), inner_width,
    )
    gates = (gate_own, gate_other)
    layer_out = from_sequence(layer_seq)

    back = [None, None]
    for h in (1, 0):
        back[h] = gate_backward(
            dbranch, dbranch_t, normed_t, seconds[h], amplitude_2[h], kept[h][0], gates[h],
            kept[h][1], scale, cross,
        )
    second_grads = jnp.concatenate(
        [(back[0][k].astype(f32) + swap(back[1][k]).astype(f32)).astype(bf16) for k in (2, 3)],
        axis=1,
    )
    second_total = reduce_rows(second_grads)

    deep = [None, None]
    deep[1] = mix_backward(
        1, length, normed_t, filters_2[1], shortcut_lanes[1], prep, back[1][0], kept[1], None, False
    )
    deep[0] = mix_backward(
        0, length, normed_t, filters_2[0], shortcut_lanes[0], prep, back[0][0], kept[0],
        deep[1][5:8], True,
    )
    content_total = deep[0][1].astype(f32) + swap(deep[1][1]).astype(f32)

    select_grad, kernels_part = select_back(
        prep[0], jnp.concatenate((deep[0][6], deep[0][7]), axis=1), kernels
    )
    select_grad = select_grad.astype(bf16)
    decay_rows = jnp.concatenate([heads_to_rows(deep[h][3]) for h in range(2)])
    direct_rows = jnp.concatenate([heads_to_rows(deep[h][4]) for h in range(2)])

    def all_heads(tiles):
        return tiles[:, : GROUP // HEAD].reshape(2 * heads, rows)

    step_rows = (direct_rows - rates[:, None] * decay_rows) * all_heads(prep[12])
    biases_part = jnp.sum(step_rows, axis=1)
    decays_part = -rates * jnp.sum(all_heads(prep[11]) * decay_rows, axis=1)
    step_rows = step_rows.astype(bf16)
    selector_part = dot(normed_t, select_grad)
    timestep_part = dot_nt(normed_t, step_rows)
    timestep_sum = timestep_part[:, :heads] + swap(timestep_part[:, heads:])
    selector_sum = selector_part + swap(selector_part)
    first_grads = jnp.concatenate(
        (content_total, selector_sum, pad_columns(timestep_sum, BLOCK)), axis=1
    ).astype(bf16)
    first_total = reduce_rows(first_grads)

    grad_normed = dot_nt(select_grad, selector_full) + lax.dot_general(
        step_rows, timestep_full, (((0,), (1,)), ((), ())), preferred_element_type=f32
    )
    for h in range(2):
        grad_normed = grad_normed + dot_nt(deep[h][0], firsts[h][:, :inner])
        grad_normed = grad_normed + dot_nt(back[h][1], seconds[h][:, :inner])
    weighted = grad_normed * rescale
    grad_seq = (
        dbranch.astype(f32)
        + inverse * weighted
        - unit * inverse * jnp.mean(weighted * unit, axis=-1, keepdims=True)
    ).astype(bf16)
    input_grad = from_sequence(grad_seq)
    rescale_part = jnp.sum(grad_normed * unit, axis=0)

    def split_part(own, other):
        return own + swap(other)

    def per_head(row):
        return jnp.sum(row.reshape(heads, HEAD), axis=1)

    tensor_split = split_part(
        *[
            jnp.concatenate(
                (
                    deep[h][2].reshape(-1),
                    back[h][4].reshape(-1),
                    biases_part[h * heads : (h + 1) * heads],
                    decays_part[h * heads : (h + 1) * heads],
                    per_head(back[h][5]),
                )
            )
            for h in range(2)
        ]
    )
    copied = jnp.concatenate((rescale_part, kernels_part.reshape(-1)))
    copied = copied + swap(copied)
    small = sum_all(jnp.concatenate((tensor_split, copied)))
    cut = tensor_split.shape[0]
    filters_grad, amplitude_grad, biases_grad, decays_grad, shortcut_grad = unpack(small[:cut])
    return (
        layer_out,
        input_grad,
        small[cut : cut + width],
        second_total[:, :inner],
        first_total[:, :inner],
        first_total[:, inner:split],
        first_total[:, split : split + heads],
        filters_grad,
        small[cut + width :].reshape(taps, state_cols),
        biases_grad,
        decays_grad,
        shortcut_grad,
        amplitude_grad.reshape(inner),
        second_total[:, inner:].T,
    )


def solution(mesh):
    return jax.shard_map(
        on_device,
        mesh=mesh,
        in_specs=(
            P(("dp", "tensor"), None),
            P(("dp", "tensor"), None),
            P("dp"),
            P(),
            P("dp", "tensor"),
            P("dp", "tensor"),
            P("dp", None),
            P("dp", "tensor"),
            P(None, "tensor"),
            P(),
            P("tensor"),
            P("tensor"),
            P("tensor"),
            P("tensor"),
            P("tensor", "dp"),
        ),
        out_specs=(
            P(("dp", "tensor"), None),
            P(("dp", "tensor"), None),
            P(),
            P("dp", "tensor"),
            P("dp", "tensor"),
            P("dp", None),
            P("dp", "tensor"),
            P(None, "tensor"),
            P(),
            P("tensor"),
            P("tensor"),
            P("tensor"),
            P("tensor"),
            P("tensor", "dp"),
        ),
        check_vma=False,
    )
```

time: 1320 us -> 601 us (0.46)
  Pallas kernels: 0 us -> 369 us
  other arithmetic: 348 us -> 38.5 us
  matrix products: 304 us -> 18.2 us
  waiting for transfers between devices: 276 us -> 57.8 us
  local copies, waits for them, and re-layouts: 239 us -> 65.5 us
  blocking collectives: 126 us -> 0 us
  starting transfers between devices: 0.73 us -> 45.4 us
  between operations: 16.9 us -> 1.86 us
    pallas_call x0 -> x11, Pallas kernels: none -> 369 us  [the longest x2 123 us: gather_rows(): pl.pallas_call(functools.partial(place_kernel, count), in_specs=[scalar]...]
    dot_general x44 -> x8, matrix products: 287 us -> 18.2 us  [the longest x6 15.5 us: dot_nt(): lax.dot_general(a, b, (((1,), (1,)), ((), ())), preferred_element_type=f32)]
    reduce_scatter x6 -> x0, waiting for transfers between devices: 226 us -> none  [the longest x1 128 us: on_device(): lax.psum_scatter(total_out, 'dp', scatter_dimension=1, tiled=True)]
    reduce_sum x50 -> x5, other arithmetic: 119 us -> 6.42 us  [the longest x1 2.4 us: on_device(): decays_part = -rates * jnp.sum(all_heads(prep[11]) * decay_rows, axis=1)]
    all_gather x2 -> x0, blocking collectives: 79.5 us -> none  [the longest x1 42.8 us: on_device(): lax.all_gather(timestep, 'dp', axis=0, tiled=True)]
    dynamic_update_slice x69 -> x0, other arithmetic: 71.4 us -> none  [the longest x64 71 us: mix_heads(): lax.scan(carry_step, empty_state, (carry_decay, gained_ahead))]
    dynamic_slice x72 -> x10, local copies, waits for them, and re-layouts: 66.5 us -> 8.17 us  [the longest x6 2.77 us: of_column(): return lax.dynamic_index_in_dim(source, high ^ s, 0, keepdims=False)]
    ppermute x0 -> x44, waiting for transfers between devices: none -> 57.8 us  [the longest x6 19.5 us: reduce_rows(): lax.ppermute(of_plane(k), 'dp', plane_pairs(size, k)).astype(f32)]
  transfers between devices with their start and end apart: 14 -> 44, of which waited for: 5 -> 16; matrix products, arithmetic and copies ran while one was open for 31% -> 15% of each run, Pallas kernels for 0% -> 36%
where the time goes in v1:
time: 601 us; the launch traced here: 596 us
  Pallas kernels  369 us (61%)
  local copies, waits for them, and re-layouts  65.5 us (11%)
  waiting for transfers between devices  57.8 us (10%)
  starting transfers between devices  45.4 us (8%)
  other arithmetic  38.5 us (6%)
  matrix products  18.2 us (3%)
    pallas_call x2, Pallas kernels, gather_rows(): pl.pallas_call(functools.partial(place_kernel, count), in_specs=[scalar]...  123 us
    pallas_call x2, Pallas kernels, mix_backward(): pl.pallas_call(functools.partial(mix_back_kernel, half, first, last), gri...  104 us
    pallas_call x2, Pallas kernels, mix_forward(): pl.pallas_call(functools.partial(mix_kernel, half), grid=(grid,), in_spec...  64.9 us
    pallas_call x2, Pallas kernels, gate_forward(): pl.pallas_call(functools.partial(gate_kernel, first, last, inner_width),...  36.6 us
    pallas_call x2, Pallas kernels, gate_backward(): pl.pallas_call(gate_back_kernel, grid=(inner // GROUP,), in_specs=[whole(...  29.2 us
    ppermute x6, waiting for transfers between devices, reduce_rows(): lax.ppermute(of_plane(k), 'dp', plane_pairs(size, k)).astype(f32)  19.5 us
    ppermute x6, waiting for transfers between devices, gather_rows(): lax.ppermute(local, 'dp', column_pairs(size, s))  16.4 us
    unnamed x122, local copies, waits for them, and re-layouts  15.5 us
  transfers between devices with their start and end apart: 44, of which 16 were waited for; matrix products, arithmetic and copies ran while one was open for 15% of the time, Pallas kernels for 36%

profile of v1, /device:TPU:0, one launch (start us, length us, event | category | flops | bytes accessed | tf_op | source)
XLA Modules:
  0.0 596.1 jit_solution(2510583774497186576)
XLA Ops:
  1.7 3.1 collective-permute-start.1
  7.3 3.3 collective-permute-done.1
  10.6 8.1 %collective-permute-done.2 = bf16[48,1536]{1,0:T(8,128)(2,1)S(1)} collective-permute-done((bf16[48,1536]{1,0:T(8,128)(2,1)S(1)}, bf16[48,1536]{1,0:T(8,128)(2,1)S(1)}, u32[]{:S(2)}, u32[]{:S(2)}) %collective-permute-start.2) | collective-permute-done | bytes 147488 | tf_op jit(solution)/shard_map/ppermute | solution.py:829
  28.1 2.9 collective-permute-start.11
  38.2 5.6 collective-permute-done.5.refs_2_
  43.9 5.0 collective-permute-done.6.refs_3_
  49.7 73.4 %place.2 = bf16[16,48,1536]{2,1,0:T(8,128)(2,1)} custom-call(s32[16]{0:T(128)} %stack.129.places, bf16[4,48,1536]{2,1,0:T(8,128)(2,1)} %copy-done.9, bf16[4,48,1536]{2,1,0:T(8,128)(2,1)} %copy-done.15, bf16[4,48,1536]{2,1,0:T(8,128)(2,1)} %copy-done.16, bf16[4,48,1536]{2,1,0:T(8,128)(2,1)} %copy-done.17), custom_call_target="tpu_custom_call" | custom-call | tf_op jit(solution)/shard_map/place/pallas_call | solution.py:837
  137.9 49.6 %place.3 = bf16[16,48,1024]{2,1,0:T(8,128)(2,1)} custom-call(s32[16]{0:T(128)} %stack.129.places, bf16[4,48,1024]{2,1,0:T(8,128)(2,1)} %copy-done.11, bf16[4,48,1024]{2,1,0:T(8,128)(2,1)} %collective-permute-done.12.refs_1_, bf16[4,48,1024]{2,1,0:T(8,128)(2,1)} %collective-permute-done.13.refs_2_, bf16[4,48,1024]{2,1,0:T(8,128)(2,1)} %collective-permute-done.14.refs_3_), custom_call_target="tpu_custom_call" | custom-call | tf_op jit(solution)/shard_map/place/pallas_call | solution.py:837
  208.0 10.9 %prep.1 = (f32[1024,128]{1,0:T(8,128)}, bf16[1024,64]{1,0:T(8,128)(2,1)}, bf16[1024,64]{1,0:T(8,128)(2,1)}, bf16[8,128,128]{2,1,0:T(8,128)(2,1)}, f32[8,128,128]...) custom-call(bf16[1024,768]{1,0:T(8,128)(2,1)} %copy.142.normed.refs_, ...), custom_call_target="tpu_custom_call" | custom-call | tf_op jit(solution)/shard_map/prep/pallas_call | solution.py:584
  218.9 32.4 %mix.3 = (f32[1024,768]{1,0:T(8,128)}, bf16[1024,768]{1,0:T(8,128)(2,1)}, bf16[1024,768]{1,0:T(8,128)(2,1)}, bf16[8,64,768]{2,1,0:T(8,128)(2,1)}, bf16[8,64,768]{2,1,0:T(8,128)(2,1)}) custom-call(s32[1]{0:T(128)} %dynamic_slice.82.length.refs_0_, bf16[1024,768]{1,0:T(8,128)(2,1)} %copy.142.normed.refs_1_, bf16[768,1024]{1,0:T(8,128)(2,1)} %bitcast.153, ...), custom_call_target="tpu_custom_call" | custom-call | tf_op jit(solution)/shard_map/mix/pallas_call | solution.py:612
  251.3 16.8 %gate.2 = (f32[1024,768]{1,0:T(8,128)}, f32[1024,128]{1,0:T(8,128)}, f32[1024,768]{1,0:T(8,128)}) custom-call(s32[1]{0:T(128)} %dynamic_slice.82.length.refs_0_, bf16[1024,768]{1,0:T(8,128)(2,1)} %copy.142.normed.refs_1_, bf16[768,1536]{1,0:T(8,128)(2,1)} %bitcast.144, bf16[768,1536]{1,0:T(8,128)(2,1)} %bitcast.145, f32[1,768]{1,0:T(1,128)} %reshape.208.refs_4_.amplitude, ...), custom_call_target="tpu_custom_call" | custom-call | tf_op jit(solution)/shard_map/gate/pallas_call | solution.py:670
  268.1 32.5 %mix.2 = (f32[1024,768]{1,0:T(8,128)}, bf16[1024,768]{1,0:T(8,128)(2,1)}, bf16[1024,768]{1,0:T(8,128)(2,1)}, bf16[8,64,768]{2,1,0:T(8,128)(2,1)}, bf16[8,64,768]{2,1,0:T(8,128)(2,1)}) custom-call(s32[1]{0:T(128)} %dynamic_slice.82.length.refs_0_, bf16[1024,768]{1,0:T(8,128)(2,1)} %copy.142.normed.refs_1_, bf16[768,1024]{1,0:T(8,128)(2,1)} %collective-permute-done.15.content, ...), custom_call_target="tpu_custom_call" | custom-call | tf_op jit(solution)/shard_map/mix/pallas_call | solution.py:612
  300.7 19.8 %gate.3 = (f32[1024,768]{1,0:T(8,128)}, f32[1024,128]{1,0:T(8,128)}, f32[1024,128]{1,0:T(8,128)}, bf16[1024,768]{1,0:T(8,128)(2,1)}) custom-call(s32[1]{0:T(128)} %dynamic_slice.82.length.refs_0_, bf16[1024,768]{1,0:T(8,128)(2,1)} %copy.142.normed.refs_1_, bf16[768,1536]{1,0:T(8,128)(2,1)} %collective-permute-done.7.refs_2_.refs_3_.out_t, ...), custom_call_target="tpu_custom_call" | custom-call | tf_op jit(solution)/shard_map/gate/pallas_call | solution.py:670
  320.5 14.6 %gate_back.2 = (bf16[1024,768]{1,0:T(8,128)(2,1)}, bf16[1024,768]{1,0:T(8,128)(2,1)}, bf16[768,768]{1,0:T(8,128)(2,1)}, bf16[768,768]{1,0:T(8,128)(2,1)}, f32[1,768]{1,0:T(1,128)}, /*index=5*/f32[1,768]{1,0:T(1,128)}) custom-call(bf16[1024,768]{1,0:T(8,128)(2,1)} %copy.144.refs_9_.cotangent, bf16[768,1024]{1,0:T(8,128)(2,1)} %bitcast.141, ...), custom_call_target="tpu_custom_call" | custom-call | tf_op jit(solution)/shard_map/gate_back/pallas_call | solution.py:687
  335.0 14.6 %gate_back.3 = (bf16[1024,768]{1,0:T(8,128)(2,1)}, bf16[1024,768]{1,0:T(8,128)(2,1)}, bf16[768,768]{1,0:T(8,128)(2,1)}, bf16[768,768]{1,0:T(8,128)(2,1)}, f32[1,768]{1,0:T(1,128)}, /*index=5*/f32[1,768]{1,0:T(1,128)}) custom-call(bf16[1024,768]{1,0:T(8,128)(2,1)} %copy.144.refs_9_.cotangent, bf16[768,1024]{1,0:T(8,128)(2,1)} %bitcast.142, ...), custom_call_target="tpu_custom_call" | custom-call | tf_op jit(solution)/shard_map/gate_back/pallas_call | solution.py:687
  349.6 50.7 %mix_back.2 = (bf16[1024,768]{1,0:T(8,128)(2,1)}, bf16[768,768]{1,0:T(8,128)(2,1)}, f32[4,768]{1,0:T(4,128)}, f32[3,64,128]{2,1,0:T(8,128)}, f32[3,64,128]{2,1,0...) custom-call(s32[1]{0:T(128)} %dynamic_slice.82.length.refs_0_, ...), custom_call_target="tpu_custom_call" | custom-call | tf_op jit(solution)/shard_map/mix_back/pallas_call | solution.py:729
  400.4 53.7 %mix_back.3 = (bf16[1024,768]{1,0:T(8,128)(2,1)}, bf16[768,768]{1,0:T(8,128)(2,1)}, f32[4,768]{1,0:T(4,128)}, f32[3,64,128]{2,1,0:T(8,128)}, f32[3,64,128]{2,1,0...) custom-call(s32[1]{0:T(128)} %dynamic_slice.82.length.refs_0_, ...), custom_call_target="tpu_custom_call" | custom-call | tf_op jit(solution)/shard_map/mix_back/pallas_call | solution.py:729
  474.5 3.3 fusion.38
  486.6 3.0 fusion.18
  494.8 3.8 fusion.9
  525.7 3.1 maximum_select_fusion.3
  560.6 4.1 collective-permute-done.29
  566.2 11.8 %collective-permute-done.30 = bf16[4,48,1536]{2,1,0:T(8,128)(2,1)} collective-permute-done((bf16[4,48,1536]{2,1,0:T(8,128)(2,1)}, bf16[4,48,1536]{2,1,0:T(8,128)(2,1)}, u32[]{:S(2)}, u32[]{:S(2)}) %collective-permute-start.30) | collective-permute-done | bytes 589856 | tf_op jit(solution)/shard_map/ppermute | solution.py:859
  588.5 5.5 collective-permute-done.33
  (321 shorter events, 162.6 us)
Async XLA Ops:
  18.8 18.9 %collective-permute-start.4 = (bf16[4,48,1536]{2,1,0:T(8,128)(2,1)S(1)}, bf16[4,48,1536]{2,1,0:T(8,128)(2,1)S(1)}, u32[]{:S(2)}, u32[]{:S(2)}) collective-permute-start(bf16[4,48,1536]{2,1,0:T(8,128)(2,1)S(1)} %pad_maximum_fusion.2.refs_0_), channel_id=1, source_target_pairs={{0,2},{2,0},{4,6},{6,4},{8,10},{10,8},{12,14},{14,12},{16,18},{18,... | collective-permute-start | bytes 1769480 | tf_op jit(solution)/shard_map/ppermute | solution.py:833
  20.4 23.5 %collective-permute-start.5 = (bf16[4,48,1536]{2,1,0:T(8,128)(2,1)S(1)}, bf16[4,48,1536]{2,1,0:T(8,128)(2,1)S(1)}, u32[]{:S(2)}, u32[]{:S(2)}) collective-permute-start(bf16[4,48,1536]{2,1,0:T(8,128)(2,1)S(1)} %pad_maximum_fusion.2.refs_0_), channel_id=1, source_target_pairs={{0,4},{2,6},{4,0},{6,2},{8,12},{10,14},{12,8},{14,10},{16,20},{18,... | collective-permute-start | bytes 1769480 | tf_op jit(solution)/shard_map/ppermute | solution.py:833
  21.9 26.9 %collective-permute-start.6 = (bf16[4,48,1536]{2,1,0:T(8,128)(2,1)S(1)}, bf16[4,48,1536]{2,1,0:T(8,128)(2,1)S(1)}, u32[]{:S(2)}, u32[]{:S(2)}) collective-permute-start(bf16[4,48,1536]{2,1,0:T(8,128)(2,1)S(1)} %pad_maximum_fusion.2.refs_0_), channel_id=1, source_target_pairs={{0,6},{2,4},{4,2},{6,0},{8,14},{10,12},{12,10},{14,8},{16,22},{18,... | collective-permute-start | bytes 1769480 | tf_op jit(solution)/shard_map/ppermute | solution.py:833
  34.6 96.3 %collective-permute-start.12 = (bf16[4,48,1024]{2,1,0:T(8,128)(2,1)S(1)}, bf16[4,48,1024]{2,1,0:T(8,128)(2,1)}, u32[]{:S(2)}, u32[]{:S(2)}) collective-permute-start(bf16[4,48,1024]{2,1,0:T(8,128)(2,1)S(1)} %pad_maximum_fusion.3.refs_0_), channel_id=1, source_target_pairs={{0,2},{2,0},{4,6},{6,4},{8,10},{10,8},{12,14},{14,12},{16,18},{18,... | collective-permute-start | bytes 1179656 | tf_op jit(solution)/shard_map/ppermute | solution.py:833
  36.2 101.2 %collective-permute-start.13 = (bf16[4,48,1024]{2,1,0:T(8,128)(2,1)S(1)}, bf16[4,48,1024]{2,1,0:T(8,128)(2,1)}, u32[]{:S(2)}, u32[]{:S(2)}) collective-permute-start(bf16[4,48,1024]{2,1,0:T(8,128)(2,1)S(1)} %pad_maximum_fusion.3.refs_0_), channel_id=1, source_target_pairs={{0,4},{2,6},{4,0},{6,2},{8,12},{10,14},{12,8},{14,10},{16,20},{18,... | collective-permute-start | bytes 1179656 | tf_op jit(solution)/shard_map/ppermute | solution.py:833
  37.7 100.2 %collective-permute-start.14 = (bf16[4,48,1024]{2,1,0:T(8,128)(2,1)S(1)}, bf16[4,48,1024]{2,1,0:T(8,128)(2,1)}, u32[]{:S(2)}, u32[]{:S(2)}) collective-permute-start(bf16[4,48,1024]{2,1,0:T(8,128)(2,1)S(1)} %pad_maximum_fusion.3.refs_0_), channel_id=1, source_target_pairs={{0,6},{2,4},{4,2},{6,0},{8,14},{10,12},{12,10},{14,8},{16,22},{18,... | collective-permute-start | bytes 1179656 | tf_op jit(solution)/shard_map/ppermute | solution.py:833
  123.1 177.6 %collective-permute-start.7 = (bf16[768,1536]{1,0:T(8,128)(2,1)}, bf16[768,1536]{1,0:T(8,128)(2,1)}, u32[]{:S(2)}, u32[]{:S(2)}) collective-permute-start(bf16[768,1536]{1,0:T(8,128)(2,1)} %bitcast.143), channel_id=1, source_target_pairs={{0,1},{1,0},{2,3},{3,2},{4,5},{5,4},{6,7},{7,6},{8,9},{9,8},{10,11... | collective-permute-start | bytes 7077896 | tf_op jit(solution)/shard_map/ppermute | solution.py:886
  126.4 67.7 %collective-permute-start = (bf16[512,768]{0,1:T(8,128)(2,1)}, bf16[512,768]{0,1:T(8,128)(2,1)}, u32[]{:S(2)}, u32[]{:S(2)}) collective-permute-start(bf16[512,768]{0,1:T(8,128)(2,1)} %bitcast.162), channel_id=1, source_target_pairs={{0,1},{1,0},{2,3},{3,2},{4,5},{5,4},{6,7},{7,6},{8,9},{9,8},{10,11... | collective-permute-start | bytes 2359304 | tf_op jit(solution)/shard_map/ppermute | solution.py:886
  130.9 56.7 %collective-permute-start.8 = (f32[3876]{0:T(1024)}, f32[3876]{0:T(1024)S(1)}, u32[]{:S(2)}, u32[]{:S(2)}) collective-permute-start(f32[3876]{0:T(1024)} %concatenate.107), channel_id=1, source_target_pairs={{0,1},{1,0},{2,3},{3,2},{4,5},{5,4},{6,7},{7,6},{8,9},{9,8},{10,11... | collective-permute-start | bytes 46520 | tf_op jit(solution)/shard_map/ppermute | solution.py:886
  137.5 63.0 %collective-permute-start.16 = (bf16[512,768]{0,1:T(8,128)(2,1)}, bf16[512,768]{0,1:T(8,128)(2,1)}, u32[]{:S(2)}, u32[]{:S(2)}) collective-permute-start(bf16[512,768]{0,1:T(8,128)(2,1)} %bitcast.36), channel_id=1, source_target_pairs={{0,1},{1,0},{2,3},{3,2},{4,5},{5,4},{6,7},{7,6},{8,9},{9,8},{10,11... | collective-permute-start | bytes 2359304 | tf_op jit(solution)/shard_map/ppermute | solution.py:886
  187.5 18.7 %collective-permute-start.15 = (bf16[768,1024]{1,0:T(8,128)(2,1)}, bf16[768,1024]{1,0:T(8,128)(2,1)}, u32[]{:S(2)}, u32[]{:S(2)}) collective-permute-start(bf16[768,1024]{1,0:T(8,128)(2,1)} %bitcast.150), channel_id=1, source_target_pairs={{0,1},{1,0},{2,3},{3,2},{4,5},{5,4},{6,7},{7,6},{8,9},{9,8},{10,11... | collective-permute-start | bytes 4718600 | tf_op jit(solution)/shard_map/ppermute | solution.py:886
  477.8 51.0 %collective-permute-start.35 = (bf16[768,768]{1,0:T(8,128)(2,1)}, bf16[768,768]{1,0:T(8,128)(2,1)}, u32[]{:S(2)}, u32[]{:S(2)}) collective-permute-start(bf16[768,768]{1,0:T(8,128)(2,1)} %get-tuple-element.127), channel_id=1, source_target_pairs={{0,1},{1,0},{2,3},{3,2},{4,5},{5,4},{6,7},{7,6},{8,9},{9,8},{10,11... | collective-permute-start | bytes 3538952 | tf_op jit(solution)/shard_map/ppermute | solution.py:886
  478.3 45.8 %collective-permute-start.36 = (f32[768,128]{1,0:T(8,128)S(1)}, f32[768,128]{1,0:T(8,128)}, u32[]{:S(2)}, u32[]{:S(2)}) collective-permute-start(f32[768,128]{1,0:T(8,128)S(1)} %fusion.52), channel_id=1, source_target_pairs={{0,1},{1,0},{2,3},{3,2},{4,5},{5,4},{6,7},{7,6},{8,9},{9,8},{10,11... | collective-permute-start | bytes 1179656 | tf_op jit(solution)/shard_map/ppermute | solution.py:886
  486.1 17.2 %collective-permute-start.19 = (f32[3876]{0:T(1024)}, f32[3876]{0:T(1024)}, u32[]{:S(2)}, u32[]{:S(2)}) collective-permute-start(f32[3876]{0:T(1024)} %concatenate.130), channel_id=1, source_target_pairs={{0,1},{1,0},{2,3},{3,2},{4,5},{5,4},{6,7},{7,6},{8,9},{9,8},{10,11... | collective-permute-start | bytes 46520 | tf_op jit(solution)/shard_map/ppermute | solution.py:886
  517.2 16.4 %collective-permute-start.27 = (bf16[768,768]{1,0:T(8,128)(2,1)}, bf16[768,768]{1,0:T(8,128)(2,1)S(1)}, u32[]{:S(2)}, u32[]{:S(2)}) collective-permute-start(bf16[768,768]{1,0:T(8,128)(2,1)} %get-tuple-element.123), channel_id=1, source_target_pairs={{0,1},{1,0},{2,3},{3,2},{4,5},{5,4},{6,7},{7,6},{8,9},{9,8},{10,11... | collective-permute-start | bytes 3538952 | tf_op jit(solution)/shard_map/ppermute | solution.py:886
  524.1 17.0 %collective-permute-start.17 = (bf16[512,768]{0,1:T(8,128)(2,1)}, bf16[512,768]{0,1:T(8,128)(2,1)S(1)}, u32[]{:S(2)}, u32[]{:S(2)}) collective-permute-start(bf16[512,768]{0,1:T(8,128)(2,1)} %get-tuple-element.210), channel_id=1, source_target_pairs={{0,1},{1,0},{2,3},{3,2},{4,5},{5,4},{6,7},{7,6},{8,9},{9,8},{10,11... | collective-permute-start | bytes 2359304 | tf_op jit(solution)/shard_map/ppermute | solution.py:886
  533.2 20.8 %collective-permute-start.39 = (bf16[4,48,1024]{2,1,0:T(8,128)(2,1)}, bf16[4,48,1024]{2,1,0:T(8,128)(2,1)}, u32[]{:S(2)}, u32[]{:S(2)}) collective-permute-start(bf16[4,48,1024]{2,1,0:T(8,128)(2,1)} %get-tuple-element.206), channel_id=1, source_target_pairs={{0,4},{2,6},{4,0},{6,2},{8,12},{10,14},{12,8},{14,10},{16,20},{18,... | collective-permute-start | bytes 1179656 | tf_op jit(solution)/shard_map/ppermute | solution.py:859
  533.6 20.4 %collective-permute-start.40 = (bf16[4,48,1024]{2,1,0:T(8,128)(2,1)S(1)}, bf16[4,48,1024]{2,1,0:T(8,128)(2,1)}, u32[]{:S(2)}, u32[]{:S(2)}) collective-permute-start(bf16[4,48,1024]{2,1,0:T(8,128)(2,1)S(1)} %get-tuple-element.205), channel_id=1, source_target_pairs={{0,6},{2,4},{4,2},{6,0},{8,14},{10,12},{12,10},{14,8},{16,22},{18,... | collective-permute-start | bytes 1179656 | tf_op jit(solution)/shard_map/ppermute | solution.py:859
  539.4 25.4 %collective-permute-start.29 = (bf16[4,48,1536]{2,1,0:T(8,128)(2,1)}, bf16[4,48,1536]{2,1,0:T(8,128)(2,1)}, u32[]{:S(2)}, u32[]{:S(2)}) collective-permute-start(bf16[4,48,1536]{2,1,0:T(8,128)(2,1)} %get-tuple-element.201), channel_id=1, source_target_pairs={{0,2},{2,0},{4,6},{6,4},{8,10},{10,8},{12,14},{14,12},{16,18},{18,... | collective-permute-start | bytes 1769480 | tf_op jit(solution)/shard_map/ppermute | solution.py:859
  541.1 36.9 %collective-permute-start.30 = (bf16[4,48,1536]{2,1,0:T(8,128)(2,1)}, bf16[4,48,1536]{2,1,0:T(8,128)(2,1)}, u32[]{:S(2)}, u32[]{:S(2)}) collective-permute-start(bf16[4,48,1536]{2,1,0:T(8,128)(2,1)} %get-tuple-element.203), channel_id=1, source_target_pairs={{0,4},{2,6},{4,0},{6,2},{8,12},{10,14},{12,8},{14,10},{16,20},{18,... | collective-permute-start | bytes 1769480 | tf_op jit(solution)/shard_map/ppermute | solution.py:859
  544.3 33.7 %collective-permute-start.31 = (bf16[4,48,1536]{2,1,0:T(8,128)(2,1)}, bf16[4,48,1536]{2,1,0:T(8,128)(2,1)}, u32[]{:S(2)}, u32[]{:S(2)}) collective-permute-start(bf16[4,48,1536]{2,1,0:T(8,128)(2,1)} %get-tuple-element.202), channel_id=1, source_target_pairs={{0,6},{2,4},{4,2},{6,0},{8,14},{10,12},{12,10},{14,8},{16,22},{18,... | collective-permute-start | bytes 1769480 | tf_op jit(solution)/shard_map/ppermute | solution.py:859
  556.6 26.5 %collective-permute-start.41 = (bf16[48,1024]{0,1:T(8,128)(2,1)}, bf16[48,1024]{0,1:T(8,128)(2,1)}, u32[]{:S(2)}, u32[]{:S(2)}) collective-permute-start(bf16[48,1024]{0,1:T(8,128)(2,1)} %bitcast.177), channel_id=1, source_target_pairs={{0,8},{2,10},{4,12},{6,14},{8,0},{10,2},{12,4},{14,6},{16,24},{18,... | collective-permute-start | bytes 294920 | tf_op jit(solution)/shard_map/ppermute | solution.py:868
  557.6 27.6 %collective-permute-start.42 = (bf16[48,1024]{0,1:T(8,128)(2,1)}, bf16[48,1024]{0,1:T(8,128)(2,1)}, u32[]{:S(2)}, u32[]{:S(2)}) collective-permute-start(bf16[48,1024]{0,1:T(8,128)(2,1)} %bitcast.176), channel_id=1, source_target_pairs={{0,16},{2,18},{4,20},{6,22},{8,24},{10,26},{12,28},{14,30},{16,0},... | collective-permute-start | bytes 294920 | tf_op jit(solution)/shard_map/ppermute | solution.py:868
  564.8 20.5 %collective-permute-start.43 = (bf16[48,1024]{0,1:T(8,128)(2,1)}, bf16[48,1024]{0,1:T(8,128)(2,1)S(1)}, u32[]{:S(2)}, u32[]{:S(2)}) collective-permute-start(bf16[48,1024]{0,1:T(8,128)(2,1)} %bitcast.178), channel_id=1, source_target_pairs={{0,24},{2,26},{4,28},{6,30},{8,16},{10,18},{12,20},{14,22},{16,8},... | collective-permute-start | bytes 294920 | tf_op jit(solution)/shard_map/ppermute | solution.py:868
  (70 other events, 624.5 us)

commit v2 on v1

v2 whole, which is shorter than its diff:
```python
import functools

import jax
import jax.numpy as jnp
from jax import lax
from jax.experimental import pallas as pl
from jax.experimental.pallas import tpu as pltpu
from jax.sharding import Mesh
from jax.sharding import PartitionSpec as P

BLOCK = 128
HEAD = 64
STATE = 64
GROUP = 256
LOG2E = 1.4426950408889634
epsilon = 1e-05
f32 = jnp.float32
bf16 = jnp.bfloat16
ANY = pl.ANY


def dot(a, b):
    return lax.dot_general(a, b, (((1,), (0,)), ((), ())), preferred_element_type=f32)


def dot_nt(a, b):
    return lax.dot_general(a, b, (((1,), (1,)), ((), ())), preferred_element_type=f32)


def dot_full(a, b):
    return lax.dot_general(
        a, b, (((1,), (0,)), ((), ())), preferred_element_type=f32, precision=lax.Precision.HIGHEST
    )


def iota(shape, axis):
    return lax.broadcasted_iota(jnp.int32, shape, axis)


def chunk(c, after=0):
    return slice(c * BLOCK + after, (c + 1) * BLOCK + after)


def each_chunk(chunks, body, carry):
    for c in range(chunks):
        carry = body(c, carry)
    return carry


def sigmoid(v):
    return 1.0 / (1.0 + jnp.exp(-v))


def conv_taps(padded, c, taps_ref):
    total = padded[chunk(c, 8)] * taps_ref[3:4]
    for back in range(1, 4):
        total = total + padded[chunk(c, 8 - back)] * taps_ref[3 - back : 4 - back]
    return total


def lane_low():
    return iota((BLOCK, 2 * HEAD), 1) < HEAD


def spread(block, column):
    index = jnp.full((BLOCK, BLOCK), column, jnp.int32)
    return jnp.take_along_axis(block, index, axis=1, mode="promise_in_bounds")


def pair_rows(piece, low):
    return jnp.concatenate(
        (jnp.where(low, piece, 0.0), jnp.where(low, 0.0, piece)), axis=0
    ).astype(bf16)


def prep_kernel(
    heads, rank, normed, extra_own, extra_other, kernels, biases, rates,
    select_in, b_rows, c_rows, select_t, gram, gram_t,
    ends, starts, steps, ends_t, starts_t, steps_t, slope_t, padded, logits_s,
):
    chunks = normed.shape[0] // BLOCK
    groups = ends_t.shape[0]
    per = GROUP // HEAD
    down = iota((BLOCK, BLOCK), 0)
    across = iota((BLOCK, BLOCK), 1)
    tri = (down >= across).astype(f32)
    off = (down != across).astype(f32)
    padded[0:8] = jnp.zeros((8, BLOCK), f32)

    own = dot(normed[...], extra_own[...])
    other = dot(normed[...], extra_other[...])
    lane = iota(own.shape, 1)
    first = jnp.where(rank[0] == 0, own, other)
    second = jnp.where(rank[0] == 0, other, own)
    selected = jnp.where(lane < STATE, first, pltpu.roll(second, STATE, 1))
    select_in[...] = selected
    padded[8:] = selected
    logits_s[...] = jnp.where(
        lane < heads, pltpu.roll(own, BLOCK - STATE, 1), pltpu.roll(other, BLOCK - STATE + heads, 1)
    )

    def body(c, carry):
        rows = chunk(c)
        pre = conv_taps(padded, c, kernels)
        act = pre * sigmoid(pre)
        act_t = act.T.astype(bf16)
        act = act.astype(bf16)
        b_rows[rows] = act[:, :STATE]
        c_rows[rows] = act[:, STATE:]
        select_t[c] = act_t
        gram[c] = dot(act[:, STATE:], act_t[:STATE]) * off
        gram_t[c] = dot(act[:, :STATE], act_t[STATE:]) * off
        logits = logits_s[rows] + biases[...]
        small = jnp.exp(-jnp.abs(logits))
        whole = 1.0 + small
        log_part = jnp.where(
            whole == 1.0, small, jnp.log(whole) * (small / jnp.where(whole == 1.0, 1.0, whole - 1.0))
        )
        step = jnp.maximum(logits, 0.0) + log_part
        decay = -rates[...] * step
        inclusive = dot_full(tri, decay)
        end = inclusive * LOG2E
        start = (inclusive - decay) * LOG2E
        ends[rows] = end
        starts[rows] = start
        steps[rows] = step
        turned = ((ends_t, end), (starts_t, start), (steps_t, step), (slope_t, sigmoid(logits)))
        for target, value in turned:
            value_t = value.T
            for g in range(groups):
                target[g, 0:per, rows] = value_t[g * per : (g + 1) * per]
        return carry

    each_chunk(chunks, body, 0)


def mix_kernel(
    half, length, normed, content, filters, shortcut, c_rows, select_t, gram,
    ends, starts, steps, ends_t, starts_t,
    mixed, x_low, values, early, late,
    ends_w, starts_w, padded, scaled, gain_e, gain_l, totals,
):
    heads_half = pl.num_programs(0) * (GROUP // HEAD)
    base = half * heads_half + pl.program_id(0) * (GROUP // HEAD)
    chunks = normed.shape[0] // BLOCK
    pairs = GROUP // (2 * HEAD)
    padded[0:8] = jnp.zeros((8, GROUP), f32)
    block = dot(normed[...], content[...])
    padded[8:] = block
    values[...] = block.astype(bf16)

    def gains(c, carry):
        rows = chunk(c)
        pre = conv_taps(padded, c, filters)
        inside = (c * BLOCK + iota((BLOCK, GROUP), 0)) < length[0]
        act = jnp.where(inside, pre * sigmoid(pre), 0.0).astype(bf16)
        x_low[rows] = act
        low = lane_low()
        end_block = ends[rows]
        start_block = starts[rows]
        step_block = steps[rows]
        for p in range(pairs):
            lanes = slice(2 * HEAD * p, 2 * HEAD * (p + 1))
            ends_p = [spread(end_block, base + 2 * p + k) for k in range(2)]
            starts_p = [spread(start_block, base + 2 * p + k) for k in range(2)]
            steps_p = [spread(step_block, base + 2 * p + k) for k in range(2)]
            for k in range(2):
                wide = slice(BLOCK * (2 * p + k), BLOCK * (2 * p + k + 1))
                ends_w[rows, wide] = ends_p[k]
                starts_w[rows, wide] = starts_p[k]
            end = jnp.where(low, *ends_p)
            start = jnp.where(low, *starts_p)
            step = jnp.where(low, *steps_p)
            total = end[BLOCK - 1 : BLOCK]
            xs = act[:, lanes].astype(f32) * step
            scaled[rows, lanes] = xs
            totals[c, :, lanes] = jnp.broadcast_to(total, (8, 2 * HEAD))
            both = jnp.concatenate((jnp.exp2(total - end) * xs, jnp.exp2(start) * xs), axis=1)
            gain = dot(select_t[c, :STATE], both.astype(bf16))
            gain_e[c, :, lanes] = gain[:, : 2 * HEAD]
            gain_l[c, :, lanes] = gain[:, 2 * HEAD :]
        return carry

    each_chunk(chunks, gains, 0)

    state = jnp.zeros((STATE, GROUP), f32)
    for c in range(chunks):
        early[c] = state.astype(bf16)
        state = jnp.exp2(totals[c, :1]) * state + gain_e[c]
    state = jnp.zeros((STATE, GROUP), f32)
    for c in reversed(range(chunks)):
        late[c] = state.astype(bf16)
        state = jnp.exp2(totals[c, :1]) * state + gain_l[c]

    def mix(c, carry):
        rows = chunk(c)
        low = lane_low()
        coupled = gram[c]
        for p in range(pairs):
            lanes = slice(2 * HEAD * p, 2 * HEAD * (p + 1))
            wides = [slice(BLOCK * (2 * p + k), BLOCK * (2 * p + k + 1)) for k in range(2)]
            ends_p = [ends_w[rows, w] for w in wides]
            starts_p = [starts_w[rows, w] for w in wides]
            coupling = []
            for k in range(2):
                end_row = ends_t[0, 2 * p + k : 2 * p + k + 1, rows]
                start_row = starts_t[0, 2 * p + k : 2 * p + k + 1, rows]
                power = jnp.exp2(jnp.minimum(ends_p[k] - end_row, start_row - starts_p[k]))
                coupling.append((coupled * power).astype(bf16))
            xs = scaled[rows, lanes]
            inner = dot(jnp.concatenate(coupling, axis=1), pair_rows(xs, low))
            states = jnp.concatenate((early[c, :, lanes], late[c, :, lanes]), axis=1)
            outer = dot(c_rows[rows], states)
            end = jnp.where(low, *ends_p)
            start = jnp.where(low, *starts_p)
            total = end[BLOCK - 1 : BLOCK]
            mixed[rows, lanes] = (
                inner
                + jnp.exp2(end) * outer[:, : 2 * HEAD]
                + jnp.exp2(total - start) * outer[:, 2 * HEAD :]
                + shortcut[:, lanes] * x_low[rows, lanes].astype(f32)
            ).astype(bf16)
        return carry

    each_chunk(chunks, mix, 0)


def gate_kernel(
    first, last, inner_width, *refs
):
    refs = list(refs)
    length, normed, gating, out_t, amplitude, mixed = refs[:6]
    refs = refs[6:]
    if not first:
        squares_in, total_in = refs[:2]
        refs = refs[2:]
    if last:
        tokens, cotangent = refs[:2]
        refs = refs[2:]
        gate_out, scale_out, cross_out, layer_out, squares, total, gated_s, gate_s = refs
    else:
        gate_out, squares, total, gated_s, gate_s = refs
    chunks = normed.shape[0] // BLOCK
    step = pl.program_id(0)

    @pl.when(step == 0)
    def _():
        if first:
            squares[...] = jnp.zeros(squares.shape, f32)
            total[...] = jnp.zeros(total.shape, f32)
        else:
            squares[...] = squares_in[...]
            total[...] = total_in[...]

    gate_s[...] = dot(normed[...], gating[...])

    def body(c, carry):
        rows = chunk(c)
        gate = gate_s[rows]
        gate_out[rows] = gate
        gated = mixed[rows].astype(f32) * (gate * sigmoid(gate))
        square = gated * gated
        squares[rows] += square[:, : GROUP // 2] + square[:, GROUP // 2 :]
        gated_s[rows] = (gated * amplitude[...]).astype(bf16)
        return carry

    each_chunk(chunks, body, 0)
    total[...] += dot_nt(gated_s[...], out_t[...])

    if last:

        @pl.when(step == pl.num_programs(0) - 1)
        def _():
            def finish(c, carry):
                rows = chunk(c)
                mean = jnp.sum(squares[rows], axis=1, keepdims=True) / inner_width
                scale = lax.rsqrt(mean + epsilon)
                inside = (c * BLOCK + iota((BLOCK, 1), 0)) < length[0]
                projected = total[rows]
                sum_out = tokens[rows].astype(f32) + scale * projected
                layer_out[rows] = jnp.where(inside, sum_out, 0.0).astype(bf16)
                inner = jnp.sum(cotangent[rows].astype(f32) * projected, axis=1, keepdims=True)
                cross = scale * scale * scale * inner / inner_width
                scale_out[rows] = jnp.broadcast_to(scale, (BLOCK, BLOCK))
                cross_out[rows] = jnp.broadcast_to(cross, (BLOCK, BLOCK))
                return carry

            each_chunk(chunks, finish, 0)


def gate_back_kernel(
    cotangent, cotangent_t, normed_t, out_t, amplitude, mixed, gate_in, x_low, scale_in, cross_in,
    mixed_grad, gate_grad, gating_grad, out_grad, amplitude_grad, shortcut_grad, gated_s, dgated_s,
):
    chunks = cotangent.shape[0] // BLOCK
    dgated_s[...] = dot(cotangent[...], out_t[...])

    def body(c, carry):
        amplitude_sum, shortcut_sum = carry
        rows = chunk(c)
        dgated = dgated_s[rows]
        gate = gate_in[rows].astype(f32)
        sig = sigmoid(gate)
        act = gate * sig
        slope = sig * (1.0 + gate * (1.0 - sig))
        y = mixed[rows].astype(f32)
        gz = y * act
        scale = jnp.concatenate((scale_in[rows], scale_in[rows]), axis=1)
        cross = jnp.concatenate((cross_in[rows], cross_in[rows]), axis=1)
        unit = gz * scale
        gated_s[rows] = (unit * amplitude[...]).astype(bf16)
        dgz = scale * (amplitude[...] * dgated) - gz * cross
        gate_grad[rows] = (dgz * y * slope).astype(bf16)
        dmix = dgz * act
        mixed_grad[rows] = dmix.astype(bf16)
        amplitude_sum = amplitude_sum + jnp.sum(dgated * unit, axis=0, keepdims=True)
        shortcut_sum = shortcut_sum + jnp.sum(
            dmix * x_low[rows].astype(f32), axis=0, keepdims=True
        )
        return amplitude_sum, shortcut_sum

    zero = jnp.zeros((1, GROUP), f32)
    amplitude_sum, shortcut_sum = each_chunk(chunks, body, (zero, zero))
    amplitude_grad[...] = amplitude_sum
    shortcut_grad[...] = shortcut_sum
    gating_grad[...] = dot(normed_t[...], gate_grad[...]).astype(bf16)
    out_grad[...] = dot(cotangent_t[...], gated_s[...]).astype(bf16)


def mix_back_kernel(half, first, last, *refs):
    refs = list(refs)
    (
        length, normed_t, filters, shortcut, b_rows, c_rows, select_t, gram_t,
        ends, starts, steps, ends_t, starts_t, mixed_grad, x_low, values, early, late,
    ) = refs[:18]
    refs = refs[18:]
    if not first:
        gram_in, b_in, c_in = refs[:3]
        refs = refs[3:]
    (
        values_grad, content_grad, filters_grad, decay_grad, direct_grad, gram_grad, b_grad, c_grad,
        ends_w, starts_w, steps_w, padded, pre_grad, gain_e, gain_l, totals,
        early_grad, late_grad, sums, local_rows, through,
    ) = refs
    step_id = pl.program_id(0)
    heads_half = pl.num_programs(0) * (GROUP // HEAD)
    base = half * heads_half + step_id * (GROUP // HEAD)
    rows_all = x_low.shape[0]
    chunks = rows_all // BLOCK
    pairs = GROUP // (2 * HEAD)

    @pl.when(step_id == 0)
    def _():
        if first:
            gram_grad[...] = jnp.zeros(gram_grad.shape, f32)
            b_grad[...] = jnp.zeros(b_grad.shape, f32)
            c_grad[...] = jnp.zeros(c_grad.shape, f32)
        else:
            gram_grad[...] = gram_in[...]
            b_grad[...] = b_in[...]
            c_grad[...] = c_in[...]

    padded[0:8] = jnp.zeros((8, GROUP), f32)
    padded[8:] = values[...].astype(f32)
    pre_grad[rows_all : rows_all + 8] = jnp.zeros((8, GROUP), f32)

    def gains(c, carry):
        rows = chunk(c)
        low = lane_low()
        end_block = ends[rows]
        start_block = starts[rows]
        step_block = steps[rows]
        for p in range(pairs):
            lanes = slice(2 * HEAD * p, 2 * HEAD * (p + 1))
            ends_p = [spread(end_block, base + 2 * p + k) for k in range(2)]
            starts_p = [spread(start_block, base + 2 * p + k) for k in range(2)]
            for k in range(2):
                wide = slice(BLOCK * (2 * p + k), BLOCK * (2 * p + k + 1))
                ends_w[rows, wide] = ends_p[k]
                starts_w[rows, wide] = starts_p[k]
            steps_w[rows, lanes] = jnp.where(
                low, *[spread(step_block, base + 2 * p + k) for k in range(2)]
            )
            end = jnp.where(low, *ends_p)
            start = jnp.where(low, *starts_p)
            total = end[BLOCK - 1 : BLOCK]
            totals[c, :, lanes] = jnp.broadcast_to(total, (8, 2 * HEAD))
            dy = mixed_grad[rows, lanes].astype(f32)
            both = jnp.concatenate((jnp.exp2(end) * dy, jnp.exp2(total - start) * dy), axis=1)
            gain = dot(select_t[c, STATE:], both.astype(bf16))
            gain_e[c, :, lanes] = gain[:, : 2 * HEAD]
            gain_l[c, :, lanes] = gain[:, 2 * HEAD :]
        return carry

    each_chunk(chunks, gains, 0)

    state = jnp.zeros((STATE, GROUP), f32)
    for c in reversed(range(chunks)):
        early_grad[c] = state.astype(bf16)
        kept = jnp.exp2(totals[c, :1]) * state
        through[c] = jnp.broadcast_to(
            jnp.sum(kept * early[c].astype(f32), axis=0, keepdims=True), (8, GROUP)
        )
        state = kept + gain_e[c]
    state = jnp.zeros((STATE, GROUP), f32)
    for c in range(chunks):
        late_grad[c] = state.astype(bf16)
        kept = jnp.exp2(totals[c, :1]) * state
        through[c] += jnp.broadcast_to(
            jnp.sum(kept * late[c].astype(f32), axis=0, keepdims=True), (8, GROUP)
        )
        state = kept + gain_l[c]

    down = iota((BLOCK, BLOCK), 0)
    across = iota((BLOCK, BLOCK), 1)

    def mix(c, carry):
        rows = chunk(c)
        low = lane_low()
        coupled = gram_t[c]
        gram_sum = gram_grad[c]
        b_sum = b_grad[rows]
        c_sum = c_grad[rows]
        row_id = iota((8, BLOCK), 0)
        lane_id = iota((8, BLOCK), 1)
        flow = jnp.zeros((8, BLOCK), f32)
        apart = jnp.zeros((16, BLOCK), f32)
        columns_sum = jnp.zeros((BLOCK, BLOCK), f32)
        below_rows = []
        above_rows = []
        for p in range(pairs):
            lanes = slice(2 * HEAD * p, 2 * HEAD * (p + 1))
            wides = [slice(BLOCK * (2 * p + k), BLOCK * (2 * p + k + 1)) for k in range(2)]
            ends_p = [ends_w[rows, w] for w in wides]
            starts_p = [starts_w[rows, w] for w in wides]
            end = jnp.where(low, *ends_p)
            start = jnp.where(low, *starts_p)
            total = end[BLOCK - 1 : BLOCK]
            step = steps_w[rows, lanes]
            x = x_low[rows, lanes].astype(f32)
            dy = mixed_grad[rows, lanes].astype(f32)
            xs = x * step
            dy_rows = pair_rows(dy, low)
            powers = []
            coupling = []
            for k in range(2):
                end_row = ends_t[0, 2 * p + k : 2 * p + k + 1, rows]
                start_row = starts_t[0, 2 * p + k : 2 * p + k + 1, rows]
                power = jnp.exp2(jnp.minimum(end_row - ends_p[k], starts_p[k] - start_row))
                powers.append(power)
                coupling.append(coupled * power)
            inner = dot(jnp.concatenate(coupling, axis=1).astype(bf16), dy_rows)
            pair_products = dot_nt(xs.astype(bf16), dy_rows)
            for k in range(2):
                product = pair_products[:, BLOCK * k : BLOCK * (k + 1)]
                gram_sum = gram_sum + product * powers[k]
                spread_log = product * coupling[k]
                below = jnp.where(down < across, spread_log, 0.0)
                above = spread_log - below
                below_rows.append(jnp.sum(below, axis=0, keepdims=True))
                above_rows.append(jnp.sum(above, axis=0, keepdims=True))
                below_cols = jnp.sum(below, axis=1, keepdims=True)
                above_cols = jnp.sum(above, axis=1, keepdims=True)
                lane = 2 * p + k
                columns_sum = jnp.where(across == lane, below_cols, columns_sum)
                columns_sum = jnp.where(across == lane + 8, above_cols, columns_sum)
            states = jnp.concatenate((early[c, :, lanes], late[c, :, lanes]), axis=1)
            states_grad = jnp.concatenate((early_grad[c, :, lanes], late_grad[c, :, lanes]), axis=1)
            raw_y = dot(c_rows[rows], states)
            raw_x = dot(b_rows[rows], states_grad)
            dy_both = jnp.concatenate((jnp.exp2(end) * dy, jnp.exp2(total - start) * dy), axis=1)
            weight_both = jnp.concatenate((jnp.exp2(total - end), jnp.exp2(start)), axis=1)
            xs_both = jnp.concatenate((xs, xs), axis=1) * weight_both
            outer_both = weight_both * raw_x
            c_sum = c_sum + dot_nt(dy_both.astype(bf16), states)
            b_sum = b_sum + dot_nt(xs_both.astype(bf16), states_grad)
            grad_xs = inner + outer_both[:, : 2 * HEAD] + outer_both[:, 2 * HEAD :]
            from_y = dy_both * raw_y
            from_x = xs_both * raw_x
            local = from_y[:, 2 * HEAD :] - from_x[:, 2 * HEAD :]
            moving = from_y[:, : 2 * HEAD] - from_x[:, : 2 * HEAD] - local
            passed = from_x[:, : 2 * HEAD] + from_y[:, 2 * HEAD :]
            through[c, :, lanes] += jnp.broadcast_to(
                jnp.sum(passed, axis=0, keepdims=True), (8, 2 * HEAD)
            )
            pick = (row_id == 2 * p + lane_id // HEAD).astype(f32)
            none = jnp.zeros((8, BLOCK), f32)
            pick_same = jnp.concatenate((pick, pick), axis=1).astype(bf16)
            pick_apart = jnp.concatenate(
                (
                    jnp.concatenate((pick, none), axis=1),
                    jnp.concatenate((none, pick), axis=1),
                ),
                axis=0,
            ).astype(bf16)
            high = moving.astype(bf16)
            rest = (moving - high.astype(f32)).astype(bf16)
            flow = flow + dot_nt(pick_same, jnp.concatenate((high, rest), axis=1))
            apart = apart + dot_nt(
                pick_apart, jnp.concatenate((local, x * grad_xs), axis=1).astype(bf16)
            )
            pre_grad[rows, lanes] = step * grad_xs + shortcut[:, lanes] * dy
        gram_grad[c] = gram_sum
        b_grad[rows] = b_sum
        c_grad[rows] = c_sum
        tile = slice(c * 8, c * 8 + 8)
        flat = columns_sum.T
        pad = jnp.zeros((4, BLOCK), f32)
        below_all = jnp.concatenate(below_rows + [pad], axis=0)
        above_all = jnp.concatenate(above_rows + [pad], axis=0)
        below_flat = flat[0:8]
        above_flat = flat[8:16]
        sums[tile] = flow + (below_all - below_flat) - (above_all - above_flat)
        local_rows[tile] = apart[:8] + (above_all - above_flat)
        direct_grad[0, tile] = apart[8:]
        return carry

    each_chunk(chunks, mix, 0)

    head_cols = (iota((GROUP, BLOCK), 0) // HEAD == iota((GROUP, BLOCK), 1)).astype(f32)
    tall = 8 * chunks
    through_tall = dot_full(through[...].reshape(tall, GROUP), head_cols)
    own = iota((tall, BLOCK), 1) == iota((tall, BLOCK), 0) % 8
    through_rows = jnp.sum(jnp.where(own, through_tall, 0.0), axis=1, keepdims=True)
    decay_grad[0] = (
        dot_full(sums[...], (down >= across).astype(f32)) + local_rows[...] + through_rows
    )

    def conv_back(c, carry):
        rows = chunk(c)
        pre = conv_taps(padded, c, filters)
        sig = sigmoid(pre)
        inside = (c * BLOCK + iota((BLOCK, GROUP), 0)) < length[0]
        grad = jnp.where(inside, pre_grad[rows] * (sig * (1.0 + pre * (1.0 - sig))), 0.0)
        pre_grad[rows] = grad
        return tuple(
            carry[k]
            + jnp.sum(grad * padded[chunk(c, 5 + k)], axis=0, keepdims=True)
            for k in range(4)
        )

    zero = jnp.zeros((1, GROUP), f32)
    filter_sums = each_chunk(chunks, conv_back, (zero,) * 4)
    filters_grad[...] = jnp.concatenate(filter_sums, axis=0)

    def conv_shift(c, carry):
        rows = chunk(c)
        total = pre_grad[rows] * filters[3:4]
        for ahead in range(1, 4):
            total = total + pre_grad[chunk(c, ahead)] * filters[3 - ahead : 4 - ahead]
        values_grad[rows] = total.astype(bf16)
        return carry

    each_chunk(chunks, conv_shift, 0)
    content_grad[...] = dot(normed_t[...], values_grad[...]).astype(bf16)

    if last:

        @pl.when(step_id == pl.num_programs(0) - 1)
        def _():
            def finish(c, carry):
                rows = chunk(c)
                grad = jnp.where(down != across, gram_grad[c], 0.0)
                b_grad[rows] += dot(grad.astype(bf16), c_rows[rows])
                c_grad[rows] += dot(grad.T.astype(bf16), b_rows[rows])
                return carry

            each_chunk(chunks, finish, 0)


def whole(shape):
    return pl.BlockSpec(shape, lambda *_: (0,) * len(shape), pipeline_mode=pl.Buffered(1))


def columns(rows, width=GROUP, after=0):
    return pl.BlockSpec((rows, width), lambda g, *_: (0, g + after))


def planes(shape):
    return pl.BlockSpec(shape, lambda g, *_: (0,) * (len(shape) - 1) + (g,))


def turned(after, rows):
    return pl.BlockSpec((1, 8, rows), lambda g, *_: (g + after, 0, 0))


def lead(shape):
    return pl.BlockSpec((1,) + shape, lambda g, *_: (g,) + (0,) * len(shape))


scalar = pl.BlockSpec(memory_space=pltpu.SMEM)


def shaped(shape, dtype):
    return jax.ShapeDtypeStruct(shape, dtype)


def params(limit=60):
    return pltpu.CompilerParams(vmem_limit_bytes=limit << 20)


def cost(micros):
    return pl.CostEstimate(flops=0, bytes_accessed=int(micros * 3.0e6), transcendentals=0)


def prepare(rank, normed, first_own, first_other, kernels, biases, rates, heads):
    rows, width = normed.shape
    chunks = rows // BLOCK
    groups = 2 * heads // (GROUP // HEAD)
    extra_at = first_own.shape[1] // BLOCK - 1
    extra = pl.BlockSpec((width, BLOCK), lambda g: (0, extra_at))
    shapes = (
        shaped((rows, BLOCK), f32),
        shaped((rows, STATE), bf16),
        shaped((rows, STATE), bf16),
        shaped((chunks, BLOCK, BLOCK), bf16),
        shaped((chunks, BLOCK, BLOCK), f32),
        shaped((chunks, BLOCK, BLOCK), f32),
        shaped((rows, BLOCK), f32),
        shaped((rows, BLOCK), f32),
        shaped((rows, BLOCK), f32),
        shaped((groups, 8, rows), f32),
        shaped((groups, 8, rows), f32),
        shaped((groups, 8, rows), f32),
        shaped((groups, 8, rows), f32),
    )
    return pl.pallas_call(
        functools.partial(prep_kernel, heads),
        grid=(1,),
        in_specs=[
            scalar, whole(normed.shape), extra, extra,
            whole(kernels.shape), whole(biases.shape), whole(rates.shape),
        ],
        out_specs=tuple(whole(o.shape) for o in shapes),
        out_shape=shapes,
        scratch_shapes=[pltpu.VMEM((rows + 8, BLOCK), f32), pltpu.VMEM((rows, BLOCK), f32)],
        compiler_params=params(),
        cost_estimate=cost(4),
        name="prep",
    )(rank, normed, first_own, first_other, kernels, biases, rates)


def front_kernel(tokens, rescale, normed, normed_t, inverse_out):
    width = tokens.shape[1]

    def body(c, carry):
        rows = chunk(c)
        tok = tokens[rows].astype(f32)
        inverse = lax.rsqrt(jnp.sum(tok * tok, axis=1, keepdims=True) / width + epsilon)
        scaled = tok * inverse * rescale[...]
        normed[rows] = scaled.astype(bf16)
        inverse_out[rows] = jnp.broadcast_to(inverse, (BLOCK, BLOCK))
        for k in range(width // BLOCK):
            normed_t[chunk(k), rows] = scaled[:, chunk(k)].T.astype(bf16)
        return carry

    each_chunk(tokens.shape[0] // BLOCK, body, 0)


def front(tokens, rescale):
    rows, width = tokens.shape
    vmem = pl.BlockSpec(memory_space=pltpu.VMEM)
    return pl.pallas_call(
        front_kernel,
        in_specs=[vmem, vmem],
        out_specs=(vmem, vmem, vmem),
        out_shape=(
            shaped((rows, width), bf16), shaped((width, rows), bf16), shaped((rows, BLOCK), f32)
        ),
        compiler_params=params(),
        cost_estimate=cost(5),
        name="front",
    )(tokens, rescale.reshape(1, width))


def mask_kernel(length, cotangent, masked, masked_t):
    width = cotangent.shape[1]

    def body(c, carry):
        rows = chunk(c)
        inside = (c * BLOCK + iota((BLOCK, width), 0)) < length[0]
        kept = jnp.where(inside, cotangent[rows].astype(f32), 0.0)
        masked[rows] = kept.astype(bf16)
        for k in range(width // BLOCK):
            masked_t[chunk(k), rows] = kept[:, chunk(k)].T.astype(bf16)
        return carry

    each_chunk(cotangent.shape[0] // BLOCK, body, 0)


def mask_rows(length, cotangent):
    rows, width = cotangent.shape
    vmem = pl.BlockSpec(memory_space=pltpu.VMEM)
    return pl.pallas_call(
        mask_kernel,
        in_specs=[scalar, vmem],
        out_specs=(vmem, vmem),
        out_shape=(shaped((rows, width), bf16), shaped((width, rows), bf16)),
        compiler_params=params(),
        cost_estimate=cost(5),
        name="mask_rows",
    )(length, cotangent)


def finish_kernel(
    heads, rank, normed_t, select_in, b_grad, c_grad, kernels, rates, decay_own, decay_other,
    direct_own, direct_other, slope_t, steps_t,
    select_grad, step_grad, extra_own, extra_other, kernels_grad, biases_grad, decays_grad,
    padded, grad_s, tall,
):
    rows = select_in.shape[0]
    chunks = rows // BLOCK
    half = decay_own.shape[0]
    padded[0:8] = jnp.zeros((8, BLOCK), f32)
    padded[8:] = select_in[...]
    grad_s[rows : rows + 8] = jnp.zeros((8, BLOCK), f32)

    def back(c, carry):
        here = chunk(c)
        pre = conv_taps(padded, c, kernels)
        sig = sigmoid(pre)
        grad = jnp.concatenate((b_grad[here], c_grad[here]), axis=1)
        grad = grad * (sig * (1.0 + pre * (1.0 - sig)))
        grad_s[here] = grad
        return tuple(
            carry[k] + jnp.sum(grad * padded[chunk(c, 5 + k)], axis=0, keepdims=True)
            for k in range(4)
        )

    zero = jnp.zeros((1, BLOCK), f32)
    kernels_grad[...] = jnp.concatenate(each_chunk(chunks, back, (zero,) * 4), axis=0)

    def shift(c, carry):
        here = chunk(c)
        total = grad_s[here] * kernels[3:4]
        for ahead in range(1, 4):
            total = total + grad_s[chunk(c, ahead)] * kernels[3 - ahead : 4 - ahead]
        select_grad[here] = total.astype(bf16)
        return carry

    each_chunk(chunks, shift, 0)

    for g in range(2 * half):
        decay = decay_own if g < half else decay_other
        direct = direct_own if g < half else direct_other
        k = g % half
        sum_step = jnp.zeros((8, BLOCK), f32)
        sum_decay = jnp.zeros((8, BLOCK), f32)
        rate = rates[g]
        for c in range(chunks):
            tile = slice(8 * c, 8 * c + 8)
            here = chunk(c)
            valid = iota((8, BLOCK), 0) < GROUP // HEAD
            fall = jnp.where(valid, decay[k, tile], 0.0)
            slope = jnp.where(valid, slope_t[g, :, here], 0.0)
            size = jnp.where(valid, steps_t[g, :, here], 0.0)
            step = (direct[k, tile] - rate * fall) * slope
            tall[8 * g : 8 * g + 8, here] = step
            sum_step = sum_step + step
            sum_decay = sum_decay - rate * size * fall
        biases_grad[g] = sum_step
        decays_grad[g] = sum_decay
    step_grad[...] = tall[...].astype(bf16)
    selector_part = dot(normed_t[...], select_grad[...])
    steps_part = dot_nt(normed_t[...], step_grad[...])
    lane = iota(selector_part.shape, 1)
    turned = pltpu.roll(selector_part, STATE, 1)
    first = jnp.where(rank[0] == 0, selector_part, turned)
    second = jnp.where(rank[0] == 0, turned, selector_part)
    width = 8 * half
    blank = jnp.zeros((selector_part.shape[0], BLOCK - 2 * width), f32)
    wide = jnp.concatenate((steps_part, blank), axis=1)
    extra_own[...] = jnp.where(
        lane < STATE, first, jnp.where(lane < STATE + width, pltpu.roll(wide, STATE, 1), 0.0)
    )
    extra_other[...] = jnp.where(
        lane < STATE,
        second,
        jnp.where(lane < STATE + width, pltpu.roll(wide, STATE - width, 1), 0.0),
    ).astype(bf16)


def finish(rank, normed_t, prep, b_grad, c_grad, kernels, rates, deep, heads):
    width, rows = normed_t.shape
    groups = prep[11].shape[0]
    vmem = pl.BlockSpec(memory_space=pltpu.VMEM)
    shapes = (
        shaped((rows, BLOCK), bf16),
        shaped((8 * groups, rows), bf16),
        shaped((width, BLOCK), f32),
        shaped((width, BLOCK), bf16),
        shaped(kernels.shape, f32),
        shaped((groups, 8, BLOCK), f32),
        shaped((groups, 8, BLOCK), f32),
    )
    per = GROUP // HEAD
    rate_tiles = jnp.broadcast_to(
        jnp.pad(rates.reshape(groups, per), ((0, 0), (0, 8 - per)))[:, :, None], (groups, 8, BLOCK)
    )
    return pl.pallas_call(
        functools.partial(finish_kernel, heads),
        in_specs=[scalar] + [vmem] * 12,
        out_specs=(vmem,) * len(shapes),
        out_shape=shapes,
        scratch_shapes=[
            pltpu.VMEM((rows + 8, BLOCK), f32),
            pltpu.VMEM((rows + 8, BLOCK), f32),
            pltpu.VMEM((8 * groups, rows), f32),
        ],
        compiler_params=params(),
        cost_estimate=cost(5),
        name="finish",
    )(
        rank, normed_t, prep[0], b_grad, c_grad, kernels, rate_tiles, deep[0][3], deep[1][3],
        deep[0][4], deep[1][4], prep[12], prep[11],
    )


def mix_forward(half, length, normed, content, filters, shortcut, prep, inner):
    (_, _, c_rows, select_t, gram, _, ends, starts, steps, ends_t, starts_t, _, _) = prep
    rows, width = normed.shape
    chunks = rows // BLOCK
    grid = inner // GROUP
    wide = GROUP // HEAD * BLOCK
    return pl.pallas_call(
        functools.partial(mix_kernel, half),
        grid=(grid,),
        in_specs=[
            scalar, whole(normed.shape), columns(width), columns(4), columns(1),
            whole(c_rows.shape), whole(select_t.shape), whole(gram.shape),
            whole(ends.shape), whole(starts.shape), whole(steps.shape),
            turned(half * grid, rows), turned(half * grid, rows),
        ],
        out_specs=(
            columns(rows), columns(rows), columns(rows),
            planes((chunks, STATE, GROUP)), planes((chunks, STATE, GROUP)),
        ),
        out_shape=(
            shaped((rows, inner), bf16),
            shaped((rows, inner), bf16),
            shaped((rows, inner), bf16),
            shaped((chunks, STATE, inner), bf16),
            shaped((chunks, STATE, inner), bf16),
        ),
        scratch_shapes=[
            pltpu.VMEM((rows, wide), f32),
            pltpu.VMEM((rows, wide), f32),
            pltpu.VMEM((rows + 8, GROUP), f32),
            pltpu.VMEM((rows, GROUP), f32),
            pltpu.VMEM((chunks, STATE, GROUP), f32),
            pltpu.VMEM((chunks, STATE, GROUP), f32),
            pltpu.VMEM((chunks, 8, GROUP), f32),
        ],
        compiler_params=params(),
        cost_estimate=cost(14),
        name="mix",
    )(length, normed, content, filters, shortcut, c_rows, select_t, gram, ends, starts, steps, ends_t, starts_t)


def gate_forward(length, normed, weights, amplitude, mixed, carried, finals, inner_width):
    rows, width = normed.shape
    inner = mixed.shape[1]
    grid = inner // GROUP
    first = carried is None
    last = finals is not None
    ins = [length, normed, weights, weights, amplitude, mixed]
    specs = [scalar, whole(normed.shape), columns(width), columns(width, after=grid), columns(1), columns(rows)]
    if not first:
        ins += list(carried)
        specs += [whole(c.shape) for c in carried]
    outs = [shaped((rows, inner), f32)]
    out_specs = [columns(rows)]
    scratch = [pltpu.VMEM((rows, GROUP), bf16), pltpu.VMEM((rows, GROUP), f32)]
    if last:
        ins += list(finals)
        specs += [whole(c.shape) for c in finals]
        outs += [shaped((rows, BLOCK), f32), shaped((rows, BLOCK), f32), shaped((rows, width), bf16)]
        out_specs += [whole((rows, BLOCK)), whole((rows, BLOCK)), whole((rows, width))]
        scratch = [pltpu.VMEM((rows, BLOCK), f32), pltpu.VMEM((rows, width), f32)] + scratch
    else:
        outs += [shaped((rows, BLOCK), f32), shaped((rows, width), f32)]
        out_specs += [whole((rows, BLOCK)), whole((rows, width))]
    return pl.pallas_call(
        functools.partial(gate_kernel, first, last, inner_width),
        grid=(grid,),
        in_specs=specs,
        out_specs=tuple(out_specs),
        out_shape=tuple(outs),
        scratch_shapes=scratch,
        compiler_params=params(),
        cost_estimate=cost(7),
        name="gate",
    )(*ins)


def gate_backward(
    cotangent, cotangent_t, normed_t, weights, amplitude, mixed, gate_in, x_low, scale, cross
):
    rows, width = cotangent.shape
    inner = mixed.shape[1]
    return pl.pallas_call(
        gate_back_kernel,
        grid=(inner // GROUP,),
        in_specs=[
            whole(cotangent.shape), whole(cotangent_t.shape), whole(normed_t.shape),
            columns(width, after=inner // GROUP), columns(1), columns(rows), columns(rows),
            columns(rows), whole(scale.shape), whole(cross.shape),
        ],
        out_specs=(
            columns(rows), columns(rows), columns(width), columns(width), columns(1), columns(1),
        ),
        out_shape=(
            shaped((rows, inner), bf16),
            shaped((rows, inner), bf16),
            shaped((width, inner), bf16),
            shaped((width, inner), bf16),
            shaped((1, inner), f32),
            shaped((1, inner), f32),
        ),
        scratch_shapes=[pltpu.VMEM((rows, GROUP), bf16), pltpu.VMEM((rows, GROUP), f32)],
        compiler_params=params(),
        cost_estimate=cost(8),
        name="gate_back",
    )(cotangent, cotangent_t, normed_t, weights, amplitude, mixed, gate_in, x_low, scale, cross)


def mix_backward(half, length, normed_t, filters, shortcut, prep, mixed_grad, kept, carried, last):
    (_, b_rows, c_rows, select_t, _, gram_t, ends, starts, steps, ends_t, starts_t, _, _) = prep
    _, x_low, values, early, late = kept
    width, rows = normed_t.shape
    inner = x_low.shape[1]
    chunks = rows // BLOCK
    grid = inner // GROUP
    first = carried is None
    wide = GROUP // HEAD * BLOCK
    shared = (b_rows, c_rows, select_t, gram_t, ends, starts, steps, ends_t, starts_t)
    ins = [length, normed_t, filters, shortcut, *shared, mixed_grad, x_low, values, early, late]
    specs = [scalar, whole(normed_t.shape), columns(4), columns(1)]
    specs += [whole(s.shape) for s in shared[:-2]] + [turned(half * grid, rows)] * 2
    specs += [columns(rows)] * 3 + [planes((chunks, STATE, GROUP))] * 2
    if not first:
        ins += list(carried)
        specs += [whole(c.shape) for c in carried]
    tall = 8 * chunks
    return pl.pallas_call(
        functools.partial(mix_back_kernel, half, first, last),
        grid=(grid,),
        in_specs=specs,
        out_specs=(
            columns(rows), columns(width), columns(4), lead((tall, BLOCK)), lead((tall, BLOCK)),
            whole((chunks, BLOCK, BLOCK)), whole((rows, STATE)), whole((rows, STATE)),
        ),
        out_shape=(
            shaped((rows, inner), bf16),
            shaped((width, inner), bf16),
            shaped((4, inner), f32),
            shaped((grid, tall, BLOCK), f32),
            shaped((grid, tall, BLOCK), f32),
            shaped((chunks, BLOCK, BLOCK), f32),
            shaped((rows, STATE), f32),
            shaped((rows, STATE), f32),
        ),
        scratch_shapes=[
            pltpu.VMEM((rows, wide), f32),
            pltpu.VMEM((rows, wide), f32),
            pltpu.VMEM((rows, GROUP), f32),
            pltpu.VMEM((rows + 8, GROUP), f32),
            pltpu.VMEM((rows + 8, GROUP), f32),
            pltpu.VMEM((chunks, STATE, GROUP), f32),
            pltpu.VMEM((chunks, STATE, GROUP), f32),
            pltpu.VMEM((chunks, 8, GROUP), f32),
            pltpu.VMEM((chunks, STATE, GROUP), bf16),
            pltpu.VMEM((chunks, STATE, GROUP), bf16),
            pltpu.VMEM((tall, BLOCK), f32),
            pltpu.VMEM((tall, BLOCK), f32),
            pltpu.VMEM((chunks, 8, GROUP), f32),
        ],
        compiler_params=params(),
        cost_estimate=cost(28),
        name="mix_back",
    )(*ins)


def shift_down(v, by):
    return jnp.pad(v, ((by, 0), (0, 0)))[: v.shape[0]]


def shift_up(v, by):
    return jnp.pad(v, ((0, by), (0, 0)))[by:]


def select_back(select_in, grad, kernels):
    taps = kernels.shape[0]
    shifted = [shift_down(select_in, taps - 1 - k) for k in range(taps)]
    pre = sum(shifted[k] * kernels[k] for k in range(taps))
    sig = sigmoid(pre)
    grad_pre = grad * (sig * (1.0 + pre * (1.0 - sig)))
    kernels_grad = jnp.stack([jnp.sum(grad_pre * shifted[k], axis=0) for k in range(taps)])
    select_grad = sum(shift_up(grad_pre, taps - 1 - k) * kernels[k] for k in range(taps))
    return select_grad, kernels_grad


def heads_to_rows(tall):
    grid, rows, tokens = tall.shape
    shaped_up = tall.reshape(grid, rows // 8, 8, tokens)[:, :, :4]
    return shaped_up.transpose(0, 2, 1, 3).reshape(grid * 4, (rows // 8) * tokens)


def place_kernel(count, places, *refs):
    parts, target = refs[:PLANE], refs[PLANE]
    for k in range(PLANE):
        for s in range(count):
            target[places[k * count + s]] = parts[k][s]


PLANE = 4
DP = ("column", "plane")


def pairs_by(size, by):
    return [(i, i ^ by) for i in range(size)]


def gather_column(local):
    count = lax.axis_size("column")
    others = [lax.ppermute(local, "column", pairs_by(count, s)) for s in range(1, count)]
    return jnp.stack([local] + others)


def gather_plane(column):
    return [column] + [
        lax.ppermute(column, "plane", pairs_by(PLANE, k)) for k in range(1, PLANE)
    ]


def place(parts):
    count, block, width = parts[0].shape
    high, low = lax.axis_index("column"), lax.axis_index("plane")
    places = jnp.stack([(high ^ s) * PLANE + (low ^ k) for k in range(PLANE) for s in range(count)])
    vmem = pl.BlockSpec(memory_space=pltpu.VMEM)
    placed = pl.pallas_call(
        functools.partial(place_kernel, count),
        in_specs=[scalar] + [vmem] * PLANE,
        out_specs=vmem,
        out_shape=shaped((PLANE * count, block, width), parts[0].dtype),
        compiler_params=params(),
        cost_estimate=cost(2),
        name="place",
    )(places.astype(jnp.int32), *parts)
    return placed.reshape(PLANE * count * block, width)


def block_of(blocks, index, axis):
    return lax.dynamic_index_in_dim(blocks, index, axis, keepdims=False)


def plane_send(v, by):
    return lax.ppermute(v, "plane", pairs_by(PLANE, by))


def start_sum(total):
    count = lax.axis_size("column")
    low = lax.axis_index("plane")
    rows, width = total.shape
    blocks = total.reshape(count, PLANE, rows // (count * PLANE), width)
    half = width // 2
    parts = (blocks[..., :half], blocks[..., half:])
    sent = []
    for part, near, far in ((parts[0], 1, 2), (parts[1], 2, 1)):
        away = jnp.stack((block_of(part, low ^ near, 1), block_of(part, low ^ 3, 1)))
        keep = jnp.stack((block_of(part, low, 1), block_of(part, low ^ far, 1)))
        sent.append((keep, plane_send(away, near)))
    return sent


def middle_sum(sent):
    moved = []
    for (keep, got), by in zip(sent, (2, 1)):
        both = (keep.astype(f32) + got.astype(f32)).astype(bf16)
        moved.append((both[0], plane_send(both[1], by)))
    return moved


def last_sum(moved):
    count = lax.axis_size("column")
    high = lax.axis_index("column")
    column = jnp.concatenate(
        [(keep.astype(f32) + got.astype(f32)).astype(bf16) for keep, got in moved], axis=-1
    )
    return [block_of(column, high, 0)] + [
        lax.ppermute(block_of(column, high ^ s, 0), "column", pairs_by(count, s))
        for s in range(1, count)
    ]


def finish_sum(terms):
    return tree_sum([t.astype(f32) for t in terms])


def tree_sum(terms):
    while len(terms) > 1:
        terms = [terms[k] + terms[k + 1] for k in range(0, len(terms), 2)]
    return terms[0]


def exchange(total):
    return lax.all_to_all(total, DP, 0, 0, tiled=True)


def sum_blocks(received, blocks):
    cut = received.reshape(blocks, received.shape[0] // blocks, received.shape[1])
    return jnp.sum(cut.astype(f32), axis=0)


def swap(v):
    return lax.ppermute(v, "tensor", [(0, 1), (1, 0)])


def pad_columns(v, width):
    return jnp.pad(v, ((0, 0), (0, width - v.shape[1])))


def tie(value, *others):
    return lax.optimization_barrier((value, *others))[0]


def on_device(
    layer_in,
    upstream,
    lengths,
    rescale,
    gating,
    content,
    selector,
    timestep,
    filters,
    kernels,
    biases,
    decays,
    shortcut,
    amplitude,
    outgoing,
):
    parts = lax.axis_size("tensor")
    rank = lax.axis_index("tensor")
    micro = lengths.shape[0]
    half_rows = layer_in.shape[0] // micro
    rows = half_rows * parts
    width = layer_in.shape[1]
    inner = gating.shape[1]
    heads = timestep.shape[1]
    state_cols = selector.shape[1]
    inner_width = inner * parts

    state_half = state_cols // parts
    own_select = lax.dynamic_slice_in_dim(selector, rank * state_half, state_half, 1)
    first_local = jnp.concatenate(
        (content, pad_columns(jnp.concatenate((own_select, timestep), axis=1), BLOCK)), axis=1
    )
    second_local = jnp.concatenate((gating, outgoing.T), axis=1)
    first_column = gather_column(first_local)
    second_own = lax.all_gather(second_local, DP, axis=0, tiled=True)

    def across(array):
        blocks = array.reshape(micro, half_rows, width)
        return lax.all_to_all(blocks, "tensor", 0, 0, tiled=True).reshape(rows, width)

    def outputs_of(array):
        mine = lax.dynamic_slice_in_dim(array, rank * half_rows, half_rows, 0)
        theirs = lax.dynamic_slice_in_dim(array, (1 - rank) * half_rows, half_rows, 0)
        return mine, swap(theirs)

    def join(mine, got):
        return jnp.where(
            rank == 0, jnp.concatenate((mine, got)), jnp.concatenate((got, mine))
        )

    tokens = across(layer_in)
    cotangent = across(upstream)
    length = lax.dynamic_slice_in_dim(lengths, rank, 1, 0)
    rank_1 = rank.reshape(1)

    flat = jnp.concatenate((filters.reshape(-1), amplitude, biases, decays, shortcut))
    flat_other = swap(flat)
    taps = filters.shape[0]

    def unpack(vector):
        edges = [0, taps * inner, (taps + 1) * inner]
        edges += [edges[-1] + heads * k for k in range(1, 4)]
        cut = [vector[a:b] for a, b in zip(edges[:-1], edges[1:])]
        return (cut[0].reshape(taps, inner), cut[1].reshape(1, inner), *cut[2:])

    filters_2, amplitude_2, biases_2, decays_2, shortcut_2 = zip(unpack(flat), unpack(flat_other))

    def head_lanes(pair):
        return pad_columns(jnp.concatenate(pair).reshape(1, -1), BLOCK)

    rates = jnp.exp(jnp.concatenate(decays_2))
    rate_lanes = pad_columns(rates.reshape(1, -1), BLOCK)
    shortcut_lanes = [jnp.repeat(s, HEAD).reshape(1, inner) for s in shortcut_2]
    normed, normed_t, inverse_wide = front(tokens, rescale)
    dbranch, dbranch_t = mask_rows(length, cotangent)
    first_column, normed = lax.optimization_barrier((first_column, normed))
    first_parts = gather_plane(first_column)
    first_parts[0] = tie(first_parts[0], dbranch)
    first_own = place(first_parts)
    first_other = swap(first_own)
    firsts = (first_own, first_other)
    prep = prepare(
        rank_1, normed, first_own, first_other, kernels, head_lanes(biases_2), rate_lanes, heads
    )
    kept = [None, None]
    kept[0] = mix_forward(
        0, length, normed, first_own, filters_2[0], shortcut_lanes[0], prep, inner
    )
    second_own = tie(second_own, kept[0][0])
    second_other = swap(second_own)
    seconds = (second_own, second_other)
    kept[1] = mix_forward(
        1, length, normed, tie(first_other, second_own), filters_2[1], shortcut_lanes[1], prep, inner
    )
    gate_own, squares, total = gate_forward(
        length, normed, seconds[0], amplitude_2[0], kept[0][0], None, None, inner_width
    )
    gate_other, scale, cross, layer_seq = gate_forward(
        length, normed, seconds[1], amplitude_2[1], kept[1][0], (squares, total),
        (tokens, dbranch), inner_width,
    )
    gates = (gate_own, gate_other)
    layer_pair = outputs_of(layer_seq)

    back = [None, None]
    for h in (1, 0):
        back[h] = gate_backward(
            dbranch, dbranch_t, normed_t, seconds[h], amplitude_2[h], kept[h][0], gates[h],
            kept[h][1], scale, cross,
        )
    second_grads = jnp.concatenate(
        [(back[0][k].astype(f32) + swap(back[1][k]).astype(f32)).astype(bf16) for k in (2, 3)],
        axis=1,
    )
    second_grads, later_grad = lax.optimization_barrier((second_grads, back[1][0]))
    second_sent = start_sum(second_grads)

    deep = [None, None]
    deep[1] = mix_backward(
        1, length, normed_t, filters_2[1], shortcut_lanes[1], prep, later_grad, kept[1], None, False
    )
    content_swapped = swap(deep[1][1])
    early_grad, *landed = lax.optimization_barrier((back[0][0], *[got for _, got in second_sent]))
    second_sent = [(keep, got) for (keep, _), got in zip(second_sent, landed)]
    second_sent[0] = (second_sent[0][0], tie(second_sent[0][1], deep[1][1]))
    second_moved = middle_sum(second_sent)
    deep[0] = mix_backward(
        0, length, normed_t, filters_2[0], shortcut_lanes[0], prep, early_grad, kept[0],
        deep[1][5:8], True,
    )
    content_own, *landed = lax.optimization_barrier((deep[0][1], *[got for _, got in second_moved]))
    second_moved = [(keep, got) for (keep, _), got in zip(second_moved, landed)]
    second_terms = last_sum(second_moved)

    (select_grad, step_rows, extra_own, extra_other, kernels_part, biases_tile, decays_tile) = finish(
        rank_1, normed_t, prep, deep[0][6], deep[0][7], kernels, rates, deep, heads
    )

    def compact(tiles):
        return jnp.sum(tiles[:, : GROUP // HEAD], axis=2).reshape(2 * heads)

    biases_part, decays_part = compact(biases_tile), compact(decays_tile)
    extra_sum = extra_own + swap(extra_other).astype(f32)
    content_sum = content_own.astype(f32) + content_swapped.astype(f32)
    first_grads = jnp.concatenate((content_sum, extra_sum), axis=1).astype(bf16)
    first_terms = last_sum(middle_sum(start_sum(first_grads)))

    spaced = 2 * heads
    select_2 = [first[:, inner : inner + state_half] for first in firsts]
    selector_full = jnp.where(
        rank == 0,
        jnp.concatenate(select_2, axis=1),
        jnp.concatenate(select_2[::-1], axis=1),
    )

    def space_heads(weights):
        per = GROUP // HEAD
        cut = weights[:, inner + state_half : inner + state_half + heads]
        cut = jnp.pad(cut.reshape(width, heads // per, per), ((0, 0), (0, 0), (0, 8 - per)))
        return cut.reshape(width, spaced)

    timestep_full = jnp.concatenate([space_heads(first) for first in firsts], axis=1)

    def weight_rows(weights, grads):
        return jnp.sum(weights.astype(f32) * grads.astype(f32), axis=1)

    extra_local = jnp.concatenate(
        (select_2[0], timestep_full[:, :spaced], select_2[1], timestep_full[:, spaced:]), axis=1
    )
    used_cols = state_half + spaced
    extra_part = jnp.concatenate(
        (extra_own[:, :used_cols], extra_other[:, :used_cols].astype(f32)), axis=1
    )
    scaled_rows = weight_rows(extra_local, extra_part)
    for h in range(2):
        scaled_rows = scaled_rows + weight_rows(firsts[h][:, :inner], tie(deep[h][1], content_own))
        scaled_rows = scaled_rows + weight_rows(
            seconds[h][:, :inner], tie(back[h][2], content_own)
        )
    rescale_part = scaled_rows / rescale

    grad_normed = dot_nt(select_grad, selector_full) + lax.dot_general(
        step_rows, timestep_full, (((0,), (1,)), ((), ())), preferred_element_type=f32
    )
    for h in range(2):
        grad_normed = grad_normed + dot_nt(tie(deep[h][0], content_own), firsts[h][:, :inner])
        grad_normed = grad_normed + dot_nt(tie(back[h][1], content_own), seconds[h][:, :inner])
    inverse = inverse_wide[:, :1]
    unit = tokens.astype(f32) * inverse
    weighted = grad_normed * rescale
    grad_seq = (
        dbranch.astype(f32)
        + inverse * weighted
        - unit * inverse * jnp.mean(weighted * unit, axis=-1, keepdims=True)
    ).astype(bf16)
    input_grad = join(*outputs_of(grad_seq))
    layer_out = join(*lax.optimization_barrier((*layer_pair, content_own))[:2])

    def per_head(row):
        return jnp.sum(row.reshape(heads, HEAD), axis=1)

    small_own, small_other = (
        jnp.concatenate(
            (
                deep[h][2].reshape(-1),
                back[h][4].reshape(-1),
                biases_part[h * heads : (h + 1) * heads],
                decays_part[h * heads : (h + 1) * heads],
                per_head(back[h][5]),
                rescale_part,
                kernels_part.reshape(-1),
            )
        )
        for h in range(2)
    )
    small = small_own + swap(small_other)
    used = small.shape[0]
    lines = -(-used // (8 * BLOCK)) * 8
    small = jnp.pad(small, (0, lines * BLOCK - used)).reshape(1, lines, BLOCK)
    blocks = lax.axis_size(DP)
    small_got = exchange(
        jnp.broadcast_to(small, (blocks, lines, BLOCK)).reshape(blocks * lines, BLOCK)
    )
    summed = sum_blocks(small_got, blocks).reshape(-1)
    cut = (taps + 1) * inner + 3 * heads
    filters_grad, amplitude_grad, biases_grad, decays_grad, shortcut_grad = unpack(summed[:cut])
    second_total = finish_sum(second_terms)
    first_total = finish_sum(first_terms)
    state_own = first_total[:, inner : inner + state_half]
    state_other = swap(state_own)
    selector_grad = jnp.where(
        rank == 0,
        jnp.concatenate((state_own, state_other), axis=1),
        jnp.concatenate((state_other, state_own), axis=1),
    )
    return (
        layer_out,
        input_grad,
        summed[cut : cut + width],
        second_total[:, :inner],
        first_total[:, :inner],
        selector_grad,
        first_total[:, inner + state_half : inner + state_half + spaced]
        .reshape(-1, spaced // 8, 8)[:, :, : GROUP // HEAD]
        .reshape(-1, heads),
        filters_grad,
        summed[cut + width : used].reshape(taps, state_cols),
        biases_grad,
        decays_grad,
        shortcut_grad,
        amplitude_grad.reshape(inner),
        second_total[:, inner:].T,
    )


def solution(mesh):
    devices = mesh.devices
    split = Mesh(
        devices.reshape(devices.shape[0] // PLANE, PLANE, devices.shape[1]), (*DP, "tensor")
    )
    return jax.shard_map(
        on_device,
        mesh=split,
        in_specs=(
            P((*DP, "tensor"), None),
            P((*DP, "tensor"), None),
            P(DP),
            P(),
            P(DP, "tensor"),
            P(DP, "tensor"),
            P(DP, None),
            P(DP, "tensor"),
            P(None, "tensor"),
            P(),
            P("tensor"),
            P("tensor"),
            P("tensor"),
            P("tensor"),
            P("tensor", DP),
        ),
        out_specs=(
            P((*DP, "tensor"), None),
            P((*DP, "tensor"), None),
            P(),
            P(DP, "tensor"),
            P(DP, "tensor"),
            P(DP, None),
            P(DP, "tensor"),
            P(None, "tensor"),
            P(),
            P("tensor"),
            P("tensor"),
            P("tensor"),
            P("tensor"),
            P("tensor", DP),
        ),
        check_vma=False,
    )
```

time: 601 us -> 359 us (0.60)
  Pallas kernels: 369 us -> 166 us
  waiting for transfers between devices: 57.8 us -> 36.6 us
  local copies, waits for them, and re-layouts: 65.5 us -> 45.6 us
  between operations: 1.86 us -> 15.3 us
  matrix products: 18.2 us -> 11.6 us
    pallas_call x3 -> x5, Pallas kernels: 134 us -> 21 us  [the longest x1 5.65 us: prepare(): pl.pallas_call(functools.partial(prep_kernel, heads), grid=(1,), in_specs...]
    pallas_call x2, Pallas kernels: 104 us -> 65.6 us  [mix_backward(): pl.pallas_call(functools.partial(mix_back_kernel, half, first, last), gri...]
    pallas_call x2, Pallas kernels: 64.9 us -> 33.9 us  [mix_forward(): pl.pallas_call(functools.partial(mix_kernel, half), grid=(grid,), in_spec...]
    ppermute x30 -> x20, waiting for transfers between devices: 57.7 us -> 31.4 us  [the longest x6 13.7 us: last_sum(): lax.ppermute(block_of(column, high ^ s, 0), 'column', pairs_by(count, s))]
    ppermute x30 -> x20, starting transfers between devices: 42.5 us -> 28.7 us  [the longest x8 10.5 us: plane_send(): return lax.ppermute(v, 'plane', pairs_by(PLANE, by))]
    all_to_all x0 -> x3, starting transfers between devices: none -> 13.5 us  [the longest x2 7.61 us: across(): lax.all_to_all(blocks, 'tensor', 0, 0, tiled=True).reshape(rows, width)]
    pallas_call x2, Pallas kernels: 36.6 us -> 23.4 us  [gate_forward(): pl.pallas_call(functools.partial(gate_kernel, first, last, inner_width),...]
    pallas_call x2, Pallas kernels: 29.2 us -> 22.4 us  [gate_backward(): pl.pallas_call(gate_back_kernel, grid=(inner // GROUP,), in_specs=[whole(...]
  transfers between devices with their start and end apart: 44 -> 35, of which waited for: 16 -> 9; matrix products, arithmetic and copies ran while one was open for 15% -> 21% of each run, Pallas kernels for 36% -> 40%
where the time goes in v2:
time: 359 us; the launch traced here: 353 us
  Pallas kernels  166 us (46%)
  local copies, waits for them, and re-layouts  45.6 us (13%)
  starting transfers between devices  45 us (13%)
  waiting for transfers between devices  36.6 us (10%)
  other arithmetic  32.8 us (9%)
  between operations  15.3 us (4%)
  matrix products  11.6 us (3%)
    pallas_call x2, Pallas kernels, mix_backward(): pl.pallas_call(functools.partial(mix_back_kernel, half, first, last), gri...  65.6 us
    pallas_call x2, Pallas kernels, mix_forward(): pl.pallas_call(functools.partial(mix_kernel, half), grid=(grid,), in_spec...  33.9 us
    pallas_call x2, Pallas kernels, gate_forward(): pl.pallas_call(functools.partial(gate_kernel, first, last, inner_width),...  23.4 us
    pallas_call x2, Pallas kernels, gate_backward(): pl.pallas_call(gate_back_kernel, grid=(inner // GROUP,), in_specs=[whole(...  22.4 us
    ppermute x6, waiting for transfers between devices, last_sum(): lax.ppermute(block_of(column, high ^ s, 0), 'column', pairs_by(count, s))  13.7 us
    unnamed x133, local copies, waits for them, and re-layouts  12.2 us
    dot_general x5, matrix products, dot_nt(): lax.dot_general(a, b, (((1,), (1,)), ((), ())), preferred_element_type=f32)  11 us
    ppermute x8, waiting for transfers between devices, plane_send(): return lax.ppermute(v, 'plane', pairs_by(PLANE, by))  10.7 us
  transfers between devices with their start and end apart: 35, of which 9 were waited for; matrix products, arithmetic and copies ran while one was open for 21% of the time, Pallas kernels for 40%

profile of v2, /device:TPU:0, one launch (start us, length us, event | category | flops | bytes accessed | tf_op | source)
XLA Modules:
  0.0 353.4 jit_solution(7310329899180410593)
XLA Ops:
  10.7 5.1 %collective-permute-start.2 = (bf16[48,896]{1,0:T(8,128)(2,1)S(1)}, bf16[48,896]{1,0:T(8,128)(2,1)S(1)}, u32[]{:S(2)}, u32[]{:S(2)}) collective-permute-start(bf16[48,896]{1,0:T(8,128)(2,1)S(1)} %get-tuple-element.274), channel_id=1, source_target_pairs={{0,24},{8,16},{16,8},{24,0},{1,25},{9,17},{17,9},{25,1},{2,26},{10... | collective-permute-start | bytes 258056 | tf_op jit(solution)/shard_map/ppermute | solution.py:1026
  16.5 3.8 %all-to-all-start = ((bf16[2,512,768]{2,1,0:T(8,128)(2,1)}), bf16[2,512,768]{2,1,0:T(8,128)(2,1)S(1)}, u32[]{:S(2)}, u32[]{:S(2)}) async-start(bf16[2,512,768]{2,1,0:T(8,128)(2,1)} %bitcast.157), calls=%async_computation | async-start | bytes 3145728 | tf_op jit(solution)/shard_map/all_to_all | solution.py:1166
  23.9 4.1 %front.1 = (bf16[1024,768]{1,0:T(8,128)(2,1)}, bf16[768,1024]{1,0:T(8,128)(2,1)}, f32[1024,128]{1,0:T(8,128)}) custom-call(bf16[1024,768]{1,0:T(8,128)(2,1)} %bitcast.144, f32[1,768]{1,0:T(1,128)} %reshape.213.rescale), custom_call_target="tpu_custom_call" | custom-call | bytes 15000000 | tf_op jit(solution)/shard_map/front/pallas_call | solution.py:663
  31.7 3.8 %all-to-all-start.1 = ((bf16[2,512,768]{2,1,0:T(8,128)(2,1)}), bf16[2,512,768]{2,1,0:T(8,128)(2,1)S(1)}, u32[]{:S(2)}, u32[]{:S(2)}) async-start(bf16[2,512,768]{2,1,0:T(8,128)(2,1)} %bitcast.23), calls=%async_computation.1 | async-start | bytes 3145728 | tf_op jit(solution)/shard_map/all_to_all | solution.py:1166
  39.1 4.3 %mask_rows.1 = (bf16[1024,768]{1,0:T(8,128)(2,1)}, bf16[768,1024]{1,0:T(8,128)(2,1)}) custom-call(s32[1]{0:T(128)} %dynamic_slice.94.length.refs_0_, bf16[1024,768]{1,0:T(8,128)(2,1)} %bitcast.156), custom_call_target="tpu_custom_call" | custom-call | bytes 15000000 | tf_op jit(solution)/shard_map/mask_rows/pallas_call | solution.py:694
  44.1 3.2 collective-permute-done.4.refs_2_
  47.2 3.8 %collective-permute-done.5.refs_3_ = bf16[4,48,896]{2,1,0:T(8,128)(2,1)S(1)} collective-permute-done((bf16[4,48,896]{2,1,0:T(8,128)(2,1)S(1)}, bf16[4,48,896]{2,1,0:T(8,128)(2,1)S(1)}, u32[]{:S(2)}, u32[]{:S(2)}) %collective-permute-start.5) | collective-permute-done | bytes 344096 | tf_op jit(solution)/shard_map/ppermute | solution.py:1032
  59.9 5.7 %prep.1 = (f32[1024,128]{1,0:T(8,128)}, bf16[1024,64]{1,0:T(8,128)(2,1)}, bf16[1024,64]{1,0:T(8,128)(2,1)}, bf16[8,128,128]{2,1,0:T(8,128)(2,1)}, f32[8,128,128]...) custom-call(s32[1]{0:T(128)} %bitcast.26.rank, ...), custom_call_target="tpu_custom_call" | custom-call | bytes 12000000 | tf_op jit(solution)/shard_map/prep/pallas_call | solution.py:627
  65.6 17.0 %mix.2 = (bf16[1024,768]{1,0:T(8,128)(2,1)}, bf16[1024,768]{1,0:T(8,128)(2,1)}, bf16[1024,768]{1,0:T(8,128)(2,1)}, bf16[8,64,768]{2,1,0:T(8,128)(2,1)}, bf16[8,64,768]{2,1,0:T(8,128)(2,1)}) custom-call(s32[1]{0:T(128)} %dynamic_slice.94.length.refs_0_, bf16[1024,768]{1,0:T(8,128)(2,1)} %get-tuple-element.108.normed.refs_1_, bf16[768,896]{1,0:T(8,128)(2,1)} %bitcast.148, ...), custom_call_target="tpu_custom_call" | custom-call | bytes 42000000 | tf_op jit(solution)/shard_map/mix/pallas_call | solution.py:825
  85.6 10.0 %gate.2 = (f32[1024,768]{1,0:T(8,128)}, f32[1024,128]{1,0:T(8,128)}, f32[1024,768]{1,0:T(8,128)}) custom-call(s32[1]{0:T(128)} %dynamic_slice.94.length.refs_0_, bf16[1024,768]{1,0:T(8,128)(2,1)} %get-tuple-element.108.normed.refs_1_, bf16[768,1536]{1,0:T(8,128)(2,1)} %all-gather.2.cloned.1.call-done.refs_2_.refs_3_.out_t, ...), custom_call_target="tpu_custom_call" | custom-call | bytes 21000000 | tf_op jit(solution)/shard_map/gate/pallas_call | solution.py:883
  95.6 17.0 %mix.3 = (bf16[1024,768]{1,0:T(8,128)(2,1)}, bf16[1024,768]{1,0:T(8,128)(2,1)}, bf16[1024,768]{1,0:T(8,128)(2,1)}, bf16[8,64,768]{2,1,0:T(8,128)(2,1)}, bf16[8,64,768]{2,1,0:T(8,128)(2,1)}) custom-call(s32[1]{0:T(128)} %dynamic_slice.94.length.refs_0_, bf16[1024,768]{1,0:T(8,128)(2,1)} %get-tuple-element.108.normed.refs_1_, bf16[768,896]{1,0:T(8,128)(2,1)} %copy-done.9, ...), custom_call_target="tpu_custom_call" | custom-call | bytes 42000000 | tf_op jit(solution)/shard_map/mix/pallas_call | solution.py:825
  114.0 13.4 %gate.3 = (f32[1024,768]{1,0:T(8,128)}, f32[1024,128]{1,0:T(8,128)}, f32[1024,128]{1,0:T(8,128)}, bf16[1024,768]{1,0:T(8,128)(2,1)}) custom-call(s32[1]{0:T(128)} %dynamic_slice.94.length.refs_0_, bf16[1024,768]{1,0:T(8,128)(2,1)} %get-tuple-element.108.normed.refs_1_, bf16[768,1536]{1,0:T(8,128)(2,1)} %copy-done.4, bf16[768,1536]{1,0:T(8,128)(2,1)} %copy-done.4, ...), custom_call_target="tpu_custom_call" | custom-call | bytes 21000000 | tf_op jit(solution)/shard_map/gate/pallas_call | solution.py:883
  127.4 11.2 %gate_back.3 = (bf16[1024,768]{1,0:T(8,128)(2,1)}, bf16[1024,768]{1,0:T(8,128)(2,1)}, bf16[768,768]{1,0:T(8,128)(2,1)}, bf16[768,768]{1,0:T(8,128)(2,1)}, f32[1,768]{1,0:T(1,128)}, /*index=5*/f32[1,768]{1,0:T(1,128)}) custom-call(bf16[1024,768]{1,0:T(8,128)(2,1)} %get-tuple-element.110.refs_9_.cotangent, bf16[768,1024]{1,0:T(8,128)(2,1)} %get-tuple-element.130.cotangent_t, ...), custom_call_target="tpu_custom_call" | custom-call | bytes 24000000 | tf_op jit(solution)/shard_map/gate_back/pallas_call | solution.py:901
  139.2 11.2 %gate_back.2 = (bf16[1024,768]{1,0:T(8,128)(2,1)}, bf16[1024,768]{1,0:T(8,128)(2,1)}, bf16[768,768]{1,0:T(8,128)(2,1)}, bf16[768,768]{1,0:T(8,128)(2,1)}, f32[1,768]{1,0:T(1,128)}, /*index=5*/f32[1,768]{1,0:T(1,128)}) custom-call(bf16[1024,768]{1,0:T(8,128)(2,1)} %get-tuple-element.110.refs_9_.cotangent, bf16[768,1024]{1,0:T(8,128)(2,1)} %get-tuple-element.130.cotangent_t, ...), custom_call_target="tpu_custom_call" | custom-call | bytes 24000000 | tf_op jit(solution)/shard_map/gate_back/pallas_call | solution.py:901
  172.4 32.1 %mix_back.2 = (bf16[1024,768]{1,0:T(8,128)(2,1)}, bf16[768,768]{1,0:T(8,128)(2,1)}, f32[4,768]{1,0:T(4,128)}, f32[3,64,128]{2,1,0:T(8,128)}, f32[3,64,128]{2,1,0...) custom-call(s32[1]{0:T(128)} %dynamic_slice.94.length.refs_0_, ...), custom_call_target="tpu_custom_call" | custom-call | bytes 84000000 | tf_op jit(solution)/shard_map/mix_back/pallas_call | solution.py:945
  214.5 33.5 %mix_back.3 = (bf16[1024,768]{1,0:T(8,128)(2,1)}, bf16[768,768]{1,0:T(8,128)(2,1)}, f32[4,768]{1,0:T(4,128)}, f32[3,64,128]{2,1,0:T(8,128)}, f32[3,64,128]{2,1,0...) custom-call(s32[1]{0:T(128)} %dynamic_slice.94.length.refs_0_, ...), custom_call_target="tpu_custom_call" | custom-call | bytes 84000000 | tf_op jit(solution)/shard_map/mix_back/pallas_call | solution.py:945
  250.0 4.5 %finish.1 = (bf16[1024,128]{1,0:T(8,128)(2,1)}, bf16[48,1024]{1,0:T(8,128)(2,1)}, f32[768,128]{1,0:T(8,128)}, bf16[768,128]{1,0:T(8,128)(2,1)}, f32[4,128]{1,0:T...) custom-call(s32[1]{0:T(128)} %bitcast.26.rank, bf16[768,1024]{1,0:T(8,128)(2,1)} %get-tuple-element.127.normed_t.refs_1_, ...), custom_call_target="tpu_custom_call" | custom-call | bytes 15000000 | tf_op jit(solution)/shard_map/finish/pallas_call | solution.py:800
  267.6 5.1 %multiply_reduce_fusion = (f32[1024]{0:T(1024)S(1)}, f32[1024,768]{1,0:T(8,128)}) fusion(f32[1024]{0:T(1024)S(1)} %slice_reduce_fusion, bf16[2,512,768]{2,1,0:T(8,128)(2,1)S(1)} %copy-done.3, f32[768]{0:T(1024)S(1)} %copy-done.39, bf16[1024,768]{1,0:T(8,128)(2,1)} %get-tuple-element.182, bf16[768,1536]{1,0:T(8,128)(2,1)S(1)} %copy-done.5, ...), kind=kOutput, calls=%fused_computation.1 | convolution fusion | flops 1215822848 | bytes 23212032 | tf_op jit(solution)/shard_map/dot_general | solution.py:27
  279.1 3.6 %collective-permute-start.20 = (bf16[48,1536]{1,0:T(8,128)(2,1)}, bf16[48,1536]{1,0:T(8,128)(2,1)S(1)}, u32[]{:S(2)}, u32[]{:S(2)}) collective-permute-start(bf16[48,1536]{1,0:T(8,128)(2,1)} %get-tuple-element.266), channel_id=1, source_target_pairs={{0,24},{8,16},{16,8},{24,0},{1,25},{9,17},{17,9},{25,1},{2,26},{10... | collective-permute-start | bytes 442376 | tf_op jit(solution)/shard_map/ppermute | solution.py:1091
  283.5 3.1 maximum_select_fusion
  290.8 5.9 %all-to-all-start.2 = ((f32[16,48,128]{2,1,0:T(8,128)}), f32[16,48,128]{2,1,0:T(8,128)S(1)}, u32[]{:S(2)}, u32[]{:S(2)}) async-start(f32[16,48,128]{2,1,0:T(8,128)} %broadcast_in_dim.25), calls=%async_computation.2 | async-start | bytes 786432 | tf_op jit(solution)/shard_map/all_to_all | solution.py:1107
  304.3 9.2 %collective-permute-done.22 = bf16[2,4,48,448]{3,2,1,0:T(8,128)(2,1)S(1)} collective-permute-done((bf16[2,4,48,448]{3,2,1,0:T(8,128)(2,1)S(1)}, bf16[2,4,48,448]{3,2,1,0:T(8,128)(2,1)S(1)}, u32[]{:S(2)}, u32[]{:S(2)}) %collective-permute-start.22) | collective-permute-done | bytes 344096 | tf_op jit(solution)/shard_map/ppermute | solution.py:1058
  326.7 3.1 maximum_select_fusion.1
  332.2 11.5 %collective-permute-done.28 = bf16[48,896]{0,1:T(8,128)(2,1)S(1)} collective-permute-done((bf16[48,896]{0,1:T(8,128)(2,1)S(1)}, bf16[48,896]{0,1:T(8,128)(2,1)S(1)}, u32[]{:S(2)}, u32[]{:S(2)}) %collective-permute-start.28) | collective-permute-done | bytes 86048 | tf_op jit(solution)/shard_map/ppermute | solution.py:1091
  (323 shorter events, 112.9 us)
Async XLA Ops:
  7.2 75.4 %all-gather.2.cloned.1.call-start = ((), (), s32[]{:S(2)}) async-start(), calls=%async_computation.3 | async-start | bytes 2506752 | tf_op jit(solution)/shard_map/all_gather | solution.py:1162
  10.7 17.3 %collective-permute-start.2 = (bf16[48,896]{1,0:T(8,128)(2,1)S(1)}, bf16[48,896]{1,0:T(8,128)(2,1)S(1)}, u32[]{:S(2)}, u32[]{:S(2)}) collective-permute-start(bf16[48,896]{1,0:T(8,128)(2,1)S(1)} %get-tuple-element.274), channel_id=1, source_target_pairs={{0,24},{8,16},{16,8},{24,0},{1,25},{9,17},{17,9},{25,1},{2,26},{10... | collective-permute-start | bytes 258056 | tf_op jit(solution)/shard_map/ppermute | solution.py:1026
  15.8 12.2 %collective-permute-start = (bf16[48,896]{1,0:T(8,128)(2,1)S(1)}, bf16[48,896]{1,0:T(8,128)(2,1)S(1)}, u32[]{:S(2)}, u32[]{:S(2)}) collective-permute-start(bf16[48,896]{1,0:T(8,128)(2,1)S(1)} %get-tuple-element.274), channel_id=1, source_target_pairs={{0,8},{8,0},{16,24},{24,16},{1,9},{9,1},{17,25},{25,17},{2,10},{10... | collective-permute-start | bytes 258056 | tf_op jit(solution)/shard_map/ppermute | solution.py:1026
  28.1 15.9 %collective-permute-start.3 = (bf16[4,48,896]{2,1,0:T(8,128)(2,1)S(1)}, bf16[4,48,896]{2,1,0:T(8,128)(2,1)S(1)}, u32[]{:S(2)}, u32[]{:S(2)}) collective-permute-start(bf16[4,48,896]{2,1,0:T(8,128)(2,1)S(1)} %pad_maximum_fusion.5.refs_0_), channel_id=1, source_target_pairs={{0,2},{2,0},{4,6},{6,4},{1,3},{3,1},{5,7},{7,5},{8,10},{10,8},{12,... | collective-permute-start | bytes 1032200 | tf_op jit(solution)/shard_map/ppermute | solution.py:1032
  29.8 17.4 %collective-permute-start.4 = (bf16[4,48,896]{2,1,0:T(8,128)(2,1)S(1)}, bf16[4,48,896]{2,1,0:T(8,128)(2,1)S(1)}, u32[]{:S(2)}, u32[]{:S(2)}) collective-permute-start(bf16[4,48,896]{2,1,0:T(8,128)(2,1)S(1)} %pad_maximum_fusion.5.refs_0_), channel_id=1, source_target_pairs={{0,4},{2,6},{4,0},{6,2},{1,5},{3,7},{5,1},{7,3},{8,12},{10,14},{12... | collective-permute-start | bytes 1032200 | tf_op jit(solution)/shard_map/ppermute | solution.py:1032
  31.3 19.7 %collective-permute-start.5 = (bf16[4,48,896]{2,1,0:T(8,128)(2,1)S(1)}, bf16[4,48,896]{2,1,0:T(8,128)(2,1)S(1)}, u32[]{:S(2)}, u32[]{:S(2)}) collective-permute-start(bf16[4,48,896]{2,1,0:T(8,128)(2,1)S(1)} %pad_maximum_fusion.5.refs_0_), channel_id=1, source_target_pairs={{0,6},{2,4},{4,2},{6,0},{1,7},{3,5},{5,3},{7,1},{8,14},{10,12},{12... | collective-permute-start | bytes 1032200 | tf_op jit(solution)/shard_map/ppermute | solution.py:1032
  82.6 30.0 %collective-permute-start.8 = (bf16[768,1536]{1,0:T(8,128)(2,1)}, bf16[768,1536]{1,0:T(8,128)(2,1)S(1)}, u32[]{:S(2)}, u32[]{:S(2)}) collective-permute-start(bf16[768,1536]{1,0:T(8,128)(2,1)} %all-gather.2.cloned.1.call-done.refs_2_.refs_3_.out_t), channel_id=1, source_target_pairs={{0,1},{1,0},{2,3},{3,2},{4,5},{5,4},{6,7},{7,6},{8,9},{9,8},{10,11... | collective-permute-start | bytes 7077896 | tf_op jit(solution)/shard_map/ppermute | solution.py:1116
  138.7 13.4 %collective-permute-start.10 = (bf16[768,768]{1,0:T(8,128)(2,1)}, bf16[768,768]{1,0:T(8,128)(2,1)S(1)}, u32[]{:S(2)}, u32[]{:S(2)}) collective-permute-start(bf16[768,768]{1,0:T(8,128)(2,1)} %get-tuple-element.193), channel_id=1, source_target_pairs={{0,1},{1,0},{2,3},{3,2},{4,5},{5,4},{6,7},{7,6},{8,9},{9,8},{10,11... | collective-permute-start | bytes 3538952 | tf_op jit(solution)/shard_map/ppermute | solution.py:1116
  153.9 51.9 %collective-permute-start.12 = (bf16[2,4,48,768]{3,2,1,0:T(8,128)(2,1)}, bf16[2,4,48,768]{3,2,1,0:T(8,128)(2,1)S(1)}, u32[]{:S(2)}, u32[]{:S(2)}) collective-permute-start(bf16[2,4,48,768]{3,2,1,0:T(8,128)(2,1)} %pad_maximum_fusion.1), channel_id=1, source_target_pairs={{0,2},{2,0},{4,6},{6,4},{1,3},{3,1},{5,7},{7,5},{8,10},{10,8},{12,... | collective-permute-start | bytes 1769480 | tf_op jit(solution)/shard_map/ppermute | solution.py:1058
  156.2 49.6 %collective-permute-start.13 = (bf16[2,4,48,768]{3,2,1,0:T(8,128)(2,1)}, bf16[2,4,48,768]{3,2,1,0:T(8,128)(2,1)}, u32[]{:S(2)}, u32[]{:S(2)}) collective-permute-start(bf16[2,4,48,768]{3,2,1,0:T(8,128)(2,1)} %pad_maximum_fusion.2), channel_id=1, source_target_pairs={{0,4},{2,6},{4,0},{6,2},{1,5},{3,7},{5,1},{7,3},{8,12},{10,14},{12... | collective-permute-start | bytes 1769480 | tf_op jit(solution)/shard_map/ppermute | solution.py:1058
  168.3 93.7 %collective-permute-start.9 = (bf16[512,768]{1,0:T(8,128)(2,1)}, bf16[512,768]{1,0:T(8,128)(2,1)}, u32[]{:S(2)}, u32[]{:S(2)}) collective-permute-start(bf16[512,768]{1,0:T(8,128)(2,1)} %get-tuple-element.246), channel_id=1, source_target_pairs={{0,1},{1,0},{2,3},{3,2},{4,5},{5,4},{6,7},{7,6},{8,9},{9,8},{10,11... | collective-permute-start | bytes 2359304 | tf_op jit(solution)/shard_map/ppermute | solution.py:1116
  205.2 92.5 %collective-permute-start.21 = (bf16[768,768]{1,0:T(8,128)(2,1)}, bf16[768,768]{1,0:T(8,128)(2,1)}, u32[]{:S(2)}, u32[]{:S(2)}) collective-permute-start(bf16[768,768]{1,0:T(8,128)(2,1)} %get-tuple-element.192), channel_id=1, source_target_pairs={{0,1},{1,0},{2,3},{3,2},{4,5},{5,4},{6,7},{7,6},{8,9},{9,8},{10,11... | collective-permute-start | bytes 3538952 | tf_op jit(solution)/shard_map/ppermute | solution.py:1116
  208.5 53.5 %collective-permute-start.14 = (bf16[4,48,768]{2,1,0:T(8,128)(2,1)}, bf16[4,48,768]{2,1,0:T(8,128)(2,1)}, u32[]{:S(2)}, u32[]{:S(2)}) collective-permute-start(bf16[4,48,768]{2,1,0:T(8,128)(2,1)} %slice_bitcast_fusion.3), channel_id=1, source_target_pairs={{0,4},{2,6},{4,0},{6,2},{1,5},{3,7},{5,1},{7,3},{8,12},{10,14},{12... | collective-permute-start | bytes 884744 | tf_op jit(solution)/shard_map/ppermute | solution.py:1058
  213.7 48.3 %collective-permute-start.15 = (bf16[4,48,768]{2,1,0:T(8,128)(2,1)}, bf16[4,48,768]{2,1,0:T(8,128)(2,1)}, u32[]{:S(2)}, u32[]{:S(2)}) collective-permute-start(bf16[4,48,768]{2,1,0:T(8,128)(2,1)} %slice_bitcast_fusion.2), channel_id=1, source_target_pairs={{0,2},{2,0},{4,6},{6,4},{1,3},{3,1},{5,7},{7,5},{8,10},{10,8},{12,... | collective-permute-start | bytes 884744 | tf_op jit(solution)/shard_map/ppermute | solution.py:1058
  276.4 12.4 %collective-permute-start.17 = (f32[5156]{0:T(1024)}, f32[5156]{0:T(1024)}, u32[]{:S(2)}, u32[]{:S(2)}) collective-permute-start(f32[5156]{0:T(1024)} %concatenate.115), channel_id=1, source_target_pairs={{0,1},{1,0},{2,3},{3,2},{4,5},{5,4},{6,7},{7,6},{8,9},{9,8},{10,11... | collective-permute-start | bytes 61880 | tf_op jit(solution)/shard_map/ppermute | solution.py:1116
  279.1 17.6 %collective-permute-start.20 = (bf16[48,1536]{1,0:T(8,128)(2,1)}, bf16[48,1536]{1,0:T(8,128)(2,1)S(1)}, u32[]{:S(2)}, u32[]{:S(2)}) collective-permute-start(bf16[48,1536]{1,0:T(8,128)(2,1)} %get-tuple-element.266), channel_id=1, source_target_pairs={{0,24},{8,16},{16,8},{24,0},{1,25},{9,17},{17,9},{25,1},{2,26},{10... | collective-permute-start | bytes 442376 | tf_op jit(solution)/shard_map/ppermute | solution.py:1091
  282.7 14.0 %collective-permute-start.19 = (bf16[48,1536]{1,0:T(8,128)(2,1)S(1)}, bf16[48,1536]{1,0:T(8,128)(2,1)S(1)}, u32[]{:S(2)}, u32[]{:S(2)}) collective-permute-start(bf16[48,1536]{1,0:T(8,128)(2,1)S(1)} %get-tuple-element.265), channel_id=1, source_target_pairs={{0,16},{8,24},{16,0},{24,8},{1,17},{9,25},{17,1},{25,9},{2,18},{10... | collective-permute-start | bytes 442376 | tf_op jit(solution)/shard_map/ppermute | solution.py:1091
  282.7 14.0 %collective-permute-start.18 = (bf16[48,1536]{1,0:T(8,128)(2,1)S(1)}, bf16[48,1536]{1,0:T(8,128)(2,1)}, u32[]{:S(2)}, u32[]{:S(2)}) collective-permute-start(bf16[48,1536]{1,0:T(8,128)(2,1)S(1)} %get-tuple-element.264), channel_id=1, source_target_pairs={{0,8},{8,0},{16,24},{24,16},{1,9},{9,1},{17,25},{25,17},{2,10},{10... | collective-permute-start | bytes 442376 | tf_op jit(solution)/shard_map/ppermute | solution.py:1091
  288.8 37.9 %collective-permute-start.16 = (bf16[512,768]{1,0:T(8,128)(2,1)}, bf16[512,768]{1,0:T(8,128)(2,1)}, u32[]{:S(2)}, u32[]{:S(2)}) collective-permute-start(bf16[512,768]{1,0:T(8,128)(2,1)} %get-tuple-element.245), channel_id=1, source_target_pairs={{0,1},{1,0},{2,3},{3,2},{4,5},{5,4},{6,7},{7,6},{8,9},{9,8},{10,11... | collective-permute-start | bytes 2359304 | tf_op jit(solution)/shard_map/ppermute | solution.py:1116
  290.8 25.8 %all-to-all-start.2 = ((f32[16,48,128]{2,1,0:T(8,128)}), f32[16,48,128]{2,1,0:T(8,128)S(1)}, u32[]{:S(2)}, u32[]{:S(2)}) async-start(f32[16,48,128]{2,1,0:T(8,128)} %broadcast_in_dim.25), calls=%async_computation.2 | async-start | bytes 786432 | tf_op jit(solution)/shard_map/all_to_all | solution.py:1107
  299.5 13.9 %collective-permute-start.22 = (bf16[2,4,48,448]{3,2,1,0:T(8,128)(2,1)S(1)}, bf16[2,4,48,448]{3,2,1,0:T(8,128)(2,1)S(1)}, u32[]{:S(2)}, u32[]{:S(2)}) collective-permute-start(bf16[2,4,48,448]{3,2,1,0:T(8,128)(2,1)S(1)} %pad_maximum_fusion.3), channel_id=1, source_target_pairs={{0,2},{2,0},{4,6},{6,4},{1,3},{3,1},{5,7},{7,5},{8,10},{10,8},{12,... | collective-permute-start | bytes 1032200 | tf_op jit(solution)/shard_map/ppermute | solution.py:1058
  302.7 12.5 %collective-permute-start.25 = (bf16[2,4,48,448]{3,2,1,0:T(8,128)(2,1)S(1)}, bf16[2,4,48,448]{3,2,1,0:T(8,128)(2,1)S(1)}, u32[]{:S(2)}, u32[]{:S(2)}) collective-permute-start(bf16[2,4,48,448]{3,2,1,0:T(8,128)(2,1)S(1)} %pad_maximum_fusion.4), channel_id=1, source_target_pairs={{0,4},{2,6},{4,0},{6,2},{1,5},{3,7},{5,1},{7,3},{8,12},{10,14},{12... | collective-permute-start | bytes 1032200 | tf_op jit(solution)/shard_map/ppermute | solution.py:1058
  324.9 18.8 %collective-permute-start.28 = (bf16[48,896]{0,1:T(8,128)(2,1)S(1)}, bf16[48,896]{0,1:T(8,128)(2,1)S(1)}, u32[]{:S(2)}, u32[]{:S(2)}) collective-permute-start(bf16[48,896]{0,1:T(8,128)(2,1)S(1)} %bitcast.161), channel_id=1, source_target_pairs={{0,16},{8,24},{16,0},{24,8},{1,17},{9,25},{17,1},{25,9},{2,18},{10... | collective-permute-start | bytes 258056 | tf_op jit(solution)/shard_map/ppermute | solution.py:1091
  325.3 18.4 %collective-permute-start.27 = (bf16[48,896]{0,1:T(8,128)(2,1)S(1)}, bf16[48,896]{0,1:T(8,128)(2,1)S(1)}, u32[]{:S(2)}, u32[]{:S(2)}) collective-permute-start(bf16[48,896]{0,1:T(8,128)(2,1)S(1)} %bitcast.162), channel_id=1, source_target_pairs={{0,8},{8,0},{16,24},{24,16},{1,9},{9,1},{17,25},{25,17},{2,10},{10... | collective-permute-start | bytes 258056 | tf_op jit(solution)/shard_map/ppermute | solution.py:1091
  (76 other events, 310.3 us)
Sparse Core Ops, SparseCore 0:
  11.4 68.1 all-gather.1

commit v3 on v2

--- a/solution.py
+++ b/solution.py
@@ -12,6 +12,17 @@
 HEAD = 64
 STATE = 64
 GROUP = 256
+SLOTS = 8
+LIM_prep = 60
+LIM_mix = 60
+LIM_gate = 60
+LIM_gate_back = 60
+LIM_mix_back = 60
+LIM_finish = 60
+LIM_back = 60
+LIM_front = 60
+LIM_mask_rows = 60
+LIM_place = 60
 LOG2E = 1.4426950408889634
 epsilon = 1e-05
 f32 = jnp.float32
@@ -64,6 +75,11 @@
 
 def spread(block, column):
     index = jnp.full((BLOCK, BLOCK), column, jnp.int32)
+    return jnp.take_along_axis(block, index, axis=1, mode="promise_in_bounds")
+
+
+def spread_pair(block, column):
+    index = column + iota((BLOCK, BLOCK), 1) // HEAD
     return jnp.take_along_axis(block, index, axis=1, mode="promise_in_bounds")
 
 
@@ -80,7 +96,6 @@
 ):
     chunks = normed.shape[0] // BLOCK
     groups = ends_t.shape[0]
-    per = GROUP // HEAD
     down = iota((BLOCK, BLOCK), 0)
     across = iota((BLOCK, BLOCK), 1)
     tri = (down >= across).astype(f32)
@@ -128,7 +143,7 @@
         for target, value in turned:
             value_t = value.T
             for g in range(groups):
-                target[g, 0:per, rows] = value_t[g * per : (g + 1) * per]
+                target[g, :, rows] = value_t[g * SLOTS : (g + 1) * SLOTS]
         return carry
 
     each_chunk(chunks, body, 0)
@@ -140,8 +155,7 @@
     mixed, x_low, values, early, late,
     ends_w, starts_w, padded, scaled, gain_e, gain_l, totals,
 ):
-    heads_half = pl.num_programs(0) * (GROUP // HEAD)
-    base = half * heads_half + pl.program_id(0) * (GROUP // HEAD)
+    base = (half * pl.num_programs(0) + pl.program_id(0)) * SLOTS
     chunks = normed.shape[0] // BLOCK
     pairs = GROUP // (2 * HEAD)
     padded[0:8] = jnp.zeros((8, GROUP), f32)
@@ -163,14 +177,13 @@
             lanes = slice(2 * HEAD * p, 2 * HEAD * (p + 1))
             ends_p = [spread(end_block, base + 2 * p + k) for k in range(2)]
             starts_p = [spread(start_block, base + 2 * p + k) for k in range(2)]
-            steps_p = [spread(step_block, base + 2 * p + k) for k in range(2)]
             for k in range(2):
                 wide = slice(BLOCK * (2 * p + k), BLOCK * (2 * p + k + 1))
                 ends_w[rows, wide] = ends_p[k]
                 starts_w[rows, wide] = starts_p[k]
             end = jnp.where(low, *ends_p)
             start = jnp.where(low, *starts_p)
-            step = jnp.where(low, *steps_p)
+            step = spread_pair(step_block, base + 2 * p)
             total = end[BLOCK - 1 : BLOCK]
             xs = act[:, lanes].astype(f32) * step
             scaled[rows, lanes] = xs
@@ -225,126 +238,147 @@
     each_chunk(chunks, mix, 0)
 
 
+def add_products(target, grads, weights):
+    @pl.when(pl.program_id(0) == 0)
+    def _():
+        target[...] = jnp.zeros(target.shape, f32)
+
+    products = grads * weights[...].astype(f32)
+    target[...] += products[:, :BLOCK] + products[:, BLOCK:]
+
+
 def gate_kernel(
-    first, last, inner_width, *refs
+    inner_width,
+    length, normed, normed_t, tokens, cotangent, cotangent_t,
+    gating_own, gating_other, out_own, out_other, amplitude,
+    mixed_own, mixed_other, x_own, x_other,
+    mixed_grad_own, mixed_grad_other, gate_grad_own, gate_grad_other,
+    gating_grad_own, gating_grad_other, out_grad_own, out_grad_other,
+    amplitude_grad_own, amplitude_grad_other, shortcut_grad_own, shortcut_grad_other,
+    layer_out, row_sums,
+    squares, total, gates, scale_s, cross_s, gated_s, dgated_s, mixed_grad_s, gate_grad_s,
 ):
-    refs = list(refs)
-    length, normed, gating, out_t, amplitude, mixed = refs[:6]
-    refs = refs[6:]
-    if not first:
-        squares_in, total_in = refs[:2]
-        refs = refs[2:]
-    if last:
-        tokens, cotangent = refs[:2]
-        refs = refs[2:]
-        gate_out, scale_out, cross_out, layer_out, squares, total, gated_s, gate_s = refs
-    else:
-        gate_out, squares, total, gated_s, gate_s = refs
     chunks = normed.shape[0] // BLOCK
     step = pl.program_id(0)
+    groups = pl.num_programs(0) // 2
+    group = lax.rem(step, groups)
+    own = group < groups // 2
+
+    def pick(first, second):
+        return jnp.where(own, first, second)
 
     @pl.when(step == 0)
     def _():
-        if first:
-            squares[...] = jnp.zeros(squares.shape, f32)
-            total[...] = jnp.zeros(total.shape, f32)
-        else:
-            squares[...] = squares_in[...]
-            total[...] = total_in[...]
-
-    gate_s[...] = dot(normed[...], gating[...])
-
-    def body(c, carry):
-        rows = chunk(c)
-        gate = gate_s[rows]
-        gate_out[rows] = gate
-        gated = mixed[rows].astype(f32) * (gate * sigmoid(gate))
-        square = gated * gated
-        squares[rows] += square[:, : GROUP // 2] + square[:, GROUP // 2 :]
-        gated_s[rows] = (gated * amplitude[...]).astype(bf16)
-        return carry
-
-    each_chunk(chunks, body, 0)
-    total[...] += dot_nt(gated_s[...], out_t[...])
-
-    if last:
-
-        @pl.when(step == pl.num_programs(0) - 1)
+        squares[...] = jnp.zeros(squares.shape, f32)
+        total[...] = jnp.zeros(total.shape, f32)
+        row_sums[...] = jnp.zeros(row_sums.shape, f32)
+
+    @pl.when(step < groups)
+    def _():
+        gates[group] = dot(normed[...], pick(gating_own[...], gating_other[...]))
+
+        def body(c, carry):
+            rows = chunk(c)
+            gate = gates[group, rows]
+            gated = pick(mixed_own[rows], mixed_other[rows]).astype(f32) * (gate * sigmoid(gate))
+            square = gated * gated
+            squares[rows] += square[:, : GROUP // 2] + square[:, GROUP // 2 :]
+            gated_s[rows] = (gated * amplitude[...]).astype(bf16)
+            return carry
+
+        each_chunk(chunks, body, 0)
+        total[...] += dot_nt(gated_s[...], pick(out_own[...], out_other[...]))
+
+    @pl.when(step == groups - 1)
+    def _():
+        def finish(c, carry):
+            rows = chunk(c)
+            mean = jnp.sum(squares[rows], axis=1, keepdims=True) / inner_width
+            scale = lax.rsqrt(mean + epsilon)
+            inside = (c * BLOCK + iota((BLOCK, 1), 0)) < length[0]
+            projected = total[rows]
+            sum_out = tokens[rows].astype(f32) + scale * projected
+            layer_out[rows] = jnp.where(inside, sum_out, 0.0).astype(bf16)
+            inner = jnp.sum(cotangent[rows].astype(f32) * projected, axis=1, keepdims=True)
+            cross = scale * scale * scale * inner / inner_width
+            scale_s[rows] = jnp.broadcast_to(scale, (BLOCK, BLOCK))
+            cross_s[rows] = jnp.broadcast_to(cross, (BLOCK, BLOCK))
+            return carry
+
+        each_chunk(chunks, finish, 0)
+
+    @pl.when(step >= groups)
+    def _():
+        dgated_s[...] = dot(cotangent[...], pick(out_own[...], out_other[...]))
+
+        def body(c, carry):
+            amplitude_sum, shortcut_sum = carry
+            rows = chunk(c)
+            dgated = dgated_s[rows]
+            gate = gates[group, rows]
+            sig = sigmoid(gate)
+            act = gate * sig
+            slope = sig * (1.0 + gate * (1.0 - sig))
+            y = pick(mixed_own[rows], mixed_other[rows]).astype(f32)
+            x = pick(x_own[rows], x_other[rows]).astype(f32)
+            gz = y * act
+            scale = jnp.concatenate((scale_s[rows], scale_s[rows]), axis=1)
+            cross = jnp.concatenate((cross_s[rows], cross_s[rows]), axis=1)
+            unit = gz * scale
+            gated_s[rows] = (unit * amplitude[...]).astype(bf16)
+            dgz = scale * (amplitude[...] * dgated) - gz * cross
+            gate_grad_s[rows] = (dgz * y * slope).astype(bf16)
+            dmix = dgz * act
+            mixed_grad_s[rows] = dmix.astype(bf16)
+            amplitude_sum = amplitude_sum + jnp.sum(dgated * unit, axis=0, keepdims=True)
+            shortcut_sum = shortcut_sum + jnp.sum(dmix * x, axis=0, keepdims=True)
+            return amplitude_sum, shortcut_sum
+
+        zero = jnp.zeros((1, GROUP), f32)
+        amplitude_sum, shortcut_sum = each_chunk(chunks, body, (zero, zero))
+        grads = dot(normed_t[...], gate_grad_s[...])
+        products = grads * pick(gating_own[...], gating_other[...]).astype(f32)
+        row_sums[...] += products[:, :BLOCK] + products[:, BLOCK:]
+        gating = grads.astype(bf16)
+        out = dot(cotangent_t[...], gated_s[...]).astype(bf16)
+
+        @pl.when(own)
         def _():
-            def finish(c, carry):
-                rows = chunk(c)
-                mean = jnp.sum(squares[rows], axis=1, keepdims=True) / inner_width
-                scale = lax.rsqrt(mean + epsilon)
-                inside = (c * BLOCK + iota((BLOCK, 1), 0)) < length[0]
-                projected = total[rows]
-                sum_out = tokens[rows].astype(f32) + scale * projected
-                layer_out[rows] = jnp.where(inside, sum_out, 0.0).astype(bf16)
-                inner = jnp.sum(cotangent[rows].astype(f32) * projected, axis=1, keepdims=True)
-                cross = scale * scale * scale * inner / inner_width
-                scale_out[rows] = jnp.broadcast_to(scale, (BLOCK, BLOCK))
-                cross_out[rows] = jnp.broadcast_to(cross, (BLOCK, BLOCK))
-                return carry
-
-            each_chunk(chunks, finish, 0)
-
-
-def gate_back_kernel(
-    cotangent, cotangent_t, normed_t, out_t, amplitude, mixed, gate_in, x_low, scale_in, cross_in,
-    mixed_grad, gate_grad, gating_grad, out_grad, amplitude_grad, shortcut_grad, gated_s, dgated_s,
-):
-    chunks = cotangent.shape[0] // BLOCK
-    dgated_s[...] = dot(cotangent[...], out_t[...])
-
-    def body(c, carry):
-        amplitude_sum, shortcut_sum = carry
-        rows = chunk(c)
-        dgated = dgated_s[rows]
-        gate = gate_in[rows].astype(f32)
-        sig = sigmoid(gate)
-        act = gate * sig
-        slope = sig * (1.0 + gate * (1.0 - sig))
-        y = mixed[rows].astype(f32)
-        gz = y * act
-        scale = jnp.concatenate((scale_in[rows], scale_in[rows]), axis=1)
-        cross = jnp.concatenate((cross_in[rows], cross_in[rows]), axis=1)
-        unit = gz * scale
-        gated_s[rows] = (unit * amplitude[...]).astype(bf16)
-        dgz = scale * (amplitude[...] * dgated) - gz * cross
-        gate_grad[rows] = (dgz * y * slope).astype(bf16)
-        dmix = dgz * act
-        mixed_grad[rows] = dmix.astype(bf16)
-        amplitude_sum = amplitude_sum + jnp.sum(dgated * unit, axis=0, keepdims=True)
-        shortcut_sum = shortcut_sum + jnp.sum(
-            dmix * x_low[rows].astype(f32), axis=0, keepdims=True
-        )
-        return amplitude_sum, shortcut_sum
-
-    zero = jnp.zeros((1, GROUP), f32)
-    amplitude_sum, shortcut_sum = each_chunk(chunks, body, (zero, zero))
-    amplitude_grad[...] = amplitude_sum
-    shortcut_grad[...] = shortcut_sum
-    gating_grad[...] = dot(normed_t[...], gate_grad[...]).astype(bf16)
-    out_grad[...] = dot(cotangent_t[...], gated_s[...]).astype(bf16)
+            mixed_grad_own[...] = mixed_grad_s[...]
+            gate_grad_own[...] = gate_grad_s[...]
+            gating_grad_own[...] = gating
+            out_grad_own[...] = out
+            amplitude_grad_own[...] = amplitude_sum
+            shortcut_grad_own[...] = shortcut_sum
+
+        @pl.when(jnp.logical_not(own))
+        def _():
+            mixed_grad_other[...] = mixed_grad_s[...]
+            gate_grad_other[...] = gate_grad_s[...]
+            gating_grad_other[...] = gating
+            out_grad_other[...] = out
+            amplitude_grad_other[...] = amplitude_sum
+            shortcut_grad_other[...] = shortcut_sum
 
 
 def mix_back_kernel(half, first, last, *refs):
     refs = list(refs)
     (
-        length, normed_t, filters, shortcut, b_rows, c_rows, select_t, gram_t,
+        length, normed_t, content, filters, shortcut, b_rows, c_rows, select_t, gram_t,
         ends, starts, steps, ends_t, starts_t, mixed_grad, x_low, values, early, late,
-    ) = refs[:18]
-    refs = refs[18:]
+    ) = refs[:19]
+    refs = refs[19:]
     if not first:
         gram_in, b_in, c_in = refs[:3]
         refs = refs[3:]
     (
         values_grad, content_grad, filters_grad, decay_grad, direct_grad, gram_grad, b_grad, c_grad,
+        row_sums,
         ends_w, starts_w, steps_w, padded, pre_grad, gain_e, gain_l, totals,
         early_grad, late_grad, sums, local_rows, through,
     ) = refs
     step_id = pl.program_id(0)
-    heads_half = pl.num_programs(0) * (GROUP // HEAD)
-    base = half * heads_half + step_id * (GROUP // HEAD)
+    base = (half * pl.num_programs(0) + step_id) * SLOTS
     rows_all = x_low.shape[0]
     chunks = rows_all // BLOCK
     pairs = GROUP // (2 * HEAD)
@@ -378,9 +412,7 @@
                 wide = slice(BLOCK * (2 * p + k), BLOCK * (2 * p + k + 1))
                 ends_w[rows, wide] = ends_p[k]
                 starts_w[rows, wide] = starts_p[k]
-            steps_w[rows, lanes] = jnp.where(
-                low, *[spread(step_block, base + 2 * p + k) for k in range(2)]
-            )
+            steps_w[rows, lanes] = spread_pair(step_block, base + 2 * p)
             end = jnp.where(low, *ends_p)
             start = jnp.where(low, *starts_p)
             total = end[BLOCK - 1 : BLOCK]
@@ -552,7 +584,9 @@
         return carry
 
     each_chunk(chunks, conv_shift, 0)
-    content_grad[...] = dot(normed_t[...], values_grad[...]).astype(bf16)
+    grads = dot(normed_t[...], values_grad[...])
+    content_grad[...] = grads.astype(bf16)
+    add_products(row_sums, grads, content)
 
     if last:
 
@@ -606,7 +640,7 @@
 def prepare(rank, normed, first_own, first_other, kernels, biases, rates, heads):
     rows, width = normed.shape
     chunks = rows // BLOCK
-    groups = 2 * heads // (GROUP // HEAD)
+    groups = 2 * heads // SLOTS
     extra_at = first_own.shape[1] // BLOCK - 1
     extra = pl.BlockSpec((width, BLOCK), lambda g: (0, extra_at))
     shapes = (
@@ -634,7 +668,7 @@
         out_specs=tuple(whole(o.shape) for o in shapes),
         out_shape=shapes,
         scratch_shapes=[pltpu.VMEM((rows + 8, BLOCK), f32), pltpu.VMEM((rows, BLOCK), f32)],
-        compiler_params=params(),
+        compiler_params=params(LIM_prep),
         cost_estimate=cost(4),
         name="prep",
     )(rank, normed, first_own, first_other, kernels, biases, rates)
@@ -667,7 +701,7 @@
         out_shape=(
             shaped((rows, width), bf16), shaped((width, rows), bf16), shaped((rows, BLOCK), f32)
         ),
-        compiler_params=params(),
+        compiler_params=params(LIM_front),
         cost_estimate=cost(5),
         name="front",
     )(tokens, rescale.reshape(1, width))
@@ -696,17 +730,17 @@
         in_specs=[scalar, vmem],
         out_specs=(vmem, vmem),
         out_shape=(shaped((rows, width), bf16), shaped((width, rows), bf16)),
-        compiler_params=params(),
+        compiler_params=params(LIM_mask_rows),
         cost_estimate=cost(5),
         name="mask_rows",
     )(length, cotangent)
 
 
 def finish_kernel(
-    heads, rank, normed_t, select_in, b_grad, c_grad, kernels, rates, decay_own, decay_other,
-    direct_own, direct_other, slope_t, steps_t,
-    select_grad, step_grad, extra_own, extra_other, kernels_grad, biases_grad, decays_grad,
-    padded, grad_s, tall,
+    rank, normed_t, weights_own, weights_other, select_in, b_grad, c_grad, kernels, rates,
+    decay_own, decay_other, direct_own, direct_other, slope_t, steps_t, sums_0, sums_1, sums_2,
+    grad_own, grad_other, extra_own, extra_other, kernels_grad, biases_grad, decays_grad, row_sums,
+    padded, grad_s,
 ):
     rows = select_in.shape[0]
     chunks = rows // BLOCK
@@ -729,90 +763,157 @@
 
     zero = jnp.zeros((1, BLOCK), f32)
     kernels_grad[...] = jnp.concatenate(each_chunk(chunks, back, (zero,) * 4), axis=0)
-
-    def shift(c, carry):
+    lane = iota((BLOCK, BLOCK), 1)
+    used = SLOTS * half
+
+    def turn(c, carry):
         here = chunk(c)
         total = grad_s[here] * kernels[3:4]
         for ahead in range(1, 4):
             total = total + grad_s[chunk(c, ahead)] * kernels[3 - ahead : 4 - ahead]
-        select_grad[here] = total.astype(bf16)
-        return carry
-
-    each_chunk(chunks, shift, 0)
-
+        tile = slice(SLOTS * c, SLOTS * (c + 1))
+        tiles = []
+        sums = []
+        valid = iota((SLOTS, BLOCK), 0) < GROUP // HEAD
+        for g in range(2 * half):
+            decay = decay_own if g < half else decay_other
+            direct = direct_own if g < half else direct_other
+            fall = jnp.where(valid, decay[g % half, tile], 0.0)
+            slope = jnp.where(valid, slope_t[g, :, here], 0.0)
+            step = (direct[g % half, tile] - rates[g] * fall) * slope
+            tiles.append(step)
+            sums.append((step, rates[g] * steps_t[g, :, here] * fall))
+        blank = jnp.zeros((BLOCK - 2 * used, BLOCK), f32)
+        steps = jnp.concatenate(tiles + [blank], axis=0).T
+        turned = pltpu.roll(total, STATE, 1)
+        first = jnp.where(rank[0] == 0, total, turned)
+        second = jnp.where(rank[0] == 0, turned, total)
+        keep = lane < STATE + used
+        grad_own[here] = jnp.where(
+            lane < STATE, first, jnp.where(keep, pltpu.roll(steps, STATE, 1), 0.0)
+        ).astype(bf16)
+        grad_other[here] = jnp.where(
+            lane < STATE, second, jnp.where(keep, pltpu.roll(steps, STATE - used, 1), 0.0)
+        ).astype(bf16)
+        return [(a + x, b - y) for (a, b), (x, y) in zip(carry, sums)]
+
+    empty = jnp.zeros((SLOTS, BLOCK), f32)
+    sums = each_chunk(chunks, turn, [(empty, empty)] * (2 * half))
     for g in range(2 * half):
-        decay = decay_own if g < half else decay_other
-        direct = direct_own if g < half else direct_other
-        k = g % half
-        sum_step = jnp.zeros((8, BLOCK), f32)
-        sum_decay = jnp.zeros((8, BLOCK), f32)
-        rate = rates[g]
-        for c in range(chunks):
-            tile = slice(8 * c, 8 * c + 8)
-            here = chunk(c)
-            valid = iota((8, BLOCK), 0) < GROUP // HEAD
-            fall = jnp.where(valid, decay[k, tile], 0.0)
-            slope = jnp.where(valid, slope_t[g, :, here], 0.0)
-            size = jnp.where(valid, steps_t[g, :, here], 0.0)
-            step = (direct[k, tile] - rate * fall) * slope
-            tall[8 * g : 8 * g + 8, here] = step
-            sum_step = sum_step + step
-            sum_decay = sum_decay - rate * size * fall
-        biases_grad[g] = sum_step
-        decays_grad[g] = sum_decay
-    step_grad[...] = tall[...].astype(bf16)
-    selector_part = dot(normed_t[...], select_grad[...])
-    steps_part = dot_nt(normed_t[...], step_grad[...])
-    lane = iota(selector_part.shape, 1)
-    turned = pltpu.roll(selector_part, STATE, 1)
-    first = jnp.where(rank[0] == 0, selector_part, turned)
-    second = jnp.where(rank[0] == 0, turned, selector_part)
-    width = 8 * half
-    blank = jnp.zeros((selector_part.shape[0], BLOCK - 2 * width), f32)
-    wide = jnp.concatenate((steps_part, blank), axis=1)
-    extra_own[...] = jnp.where(
-        lane < STATE, first, jnp.where(lane < STATE + width, pltpu.roll(wide, STATE, 1), 0.0)
-    )
-    extra_other[...] = jnp.where(
-        lane < STATE,
-        second,
-        jnp.where(lane < STATE + width, pltpu.roll(wide, STATE - width, 1), 0.0),
-    ).astype(bf16)
-
-
-def finish(rank, normed_t, prep, b_grad, c_grad, kernels, rates, deep, heads):
+        biases_grad[g] = sums[g][0]
+        decays_grad[g] = sums[g][1]
+    own = dot(normed_t[...], grad_own[...])
+    other = dot(normed_t[...], grad_other[...])
+    extra_own[...] = own
+    extra_other[...] = other.astype(bf16)
+    row_sums[...] = (
+        own * weights_own[...].astype(f32)
+        + other * weights_other[...].astype(f32)
+        + (sums_0[...] + sums_1[...] + sums_2[...])
+    )
+
+
+def extra_columns(weights):
+    at = weights.shape[1] // BLOCK - 1
+    return pl.BlockSpec((weights.shape[0], BLOCK), lambda *_: (0, at))
+
+
+def finish(rank, normed_t, firsts, prep, b_grad, c_grad, kernels, rate_tiles, deep, row_sums):
     width, rows = normed_t.shape
     groups = prep[11].shape[0]
-    vmem = pl.BlockSpec(memory_space=pltpu.VMEM)
     shapes = (
         shaped((rows, BLOCK), bf16),
-        shaped((8 * groups, rows), bf16),
+        shaped((rows, BLOCK), bf16),
         shaped((width, BLOCK), f32),
         shaped((width, BLOCK), bf16),
         shaped(kernels.shape, f32),
-        shaped((groups, 8, BLOCK), f32),
-        shaped((groups, 8, BLOCK), f32),
-    )
-    per = GROUP // HEAD
-    rate_tiles = jnp.broadcast_to(
-        jnp.pad(rates.reshape(groups, per), ((0, 0), (0, 8 - per)))[:, :, None], (groups, 8, BLOCK)
+        shaped((groups, SLOTS, BLOCK), f32),
+        shaped((groups, SLOTS, BLOCK), f32),
+        shaped((width, BLOCK), f32),
+    )
+    rest = (
+        prep[0], b_grad, c_grad, kernels, rate_tiles, deep[0][3], deep[1][3], deep[0][4], deep[1][4],
+        prep[12], prep[11], *row_sums,
     )
     return pl.pallas_call(
-        functools.partial(finish_kernel, heads),
-        in_specs=[scalar] + [vmem] * 12,
-        out_specs=(vmem,) * len(shapes),
+        finish_kernel,
+        grid=(1,),
+        in_specs=[scalar, whole(normed_t.shape)]
+        + [extra_columns(w) for w in firsts]
+        + [whole(r.shape) for r in rest],
+        out_specs=tuple(whole(o.shape) for o in shapes),
         out_shape=shapes,
-        scratch_shapes=[
-            pltpu.VMEM((rows + 8, BLOCK), f32),
-            pltpu.VMEM((rows + 8, BLOCK), f32),
-            pltpu.VMEM((8 * groups, rows), f32),
-        ],
-        compiler_params=params(),
-        cost_estimate=cost(5),
+        scratch_shapes=[pltpu.VMEM((rows + 8, BLOCK), f32), pltpu.VMEM((rows + 8, BLOCK), f32)],
+        compiler_params=params(LIM_finish),
+        cost_estimate=cost(6),
         name="finish",
+    )(rank, normed_t, *firsts, *rest)
+
+
+def back_kernel(
+    values_own, values_other, gate_own, gate_other, content_own, content_other, gating_own,
+    gating_other, extra_own, extra_other, weights_own, weights_other, tokens, inverse_in, rescale,
+    cotangent, grad_out, total,
+):
+    step = pl.program_id(0)
+
+    def products():
+        return (
+            dot_nt(values_own[...], content_own[...])
+            + dot_nt(values_other[...], content_other[...])
+            + dot_nt(gate_own[...], gating_own[...])
+            + dot_nt(gate_other[...], gating_other[...])
+        )
+
+    @pl.when(step == 0)
+    def _():
+        total[...] = (
+            products()
+            + dot_nt(extra_own[...], weights_own[...])
+            + dot_nt(extra_other[...], weights_other[...])
+        )
+
+    @pl.when(step > 0)
+    def _():
+        total[...] += products()
+
+    @pl.when(step == pl.num_programs(0) - 1)
+    def _():
+        width = tokens.shape[1]
+
+        def body(c, carry):
+            rows = chunk(c)
+            inverse = inverse_in[rows, :1]
+            unit = tokens[rows].astype(f32) * inverse
+            weighted = total[rows] * rescale[...]
+            mean = jnp.sum(weighted * unit, axis=1, keepdims=True) / width
+            grad = cotangent[rows].astype(f32) + inverse * (weighted - unit * mean)
+            grad_out[rows] = grad.astype(bf16)
+            return carry
+
+        each_chunk(tokens.shape[0] // BLOCK, body, 0)
+
+
+def backward_rows(deep, back, firsts, seconds, extras, tokens, inverse_wide, rescale, cotangent):
+    rows, width = tokens.shape
+    inner = deep[0][0].shape[1]
+    fixed = (tokens, inverse_wide, rescale.reshape(1, width), cotangent)
+    return pl.pallas_call(
+        back_kernel,
+        grid=(inner // GROUP,),
+        in_specs=[columns(rows)] * 4
+        + [columns(width)] * 4
+        + [whole((rows, BLOCK))] * 2
+        + [extra_columns(w) for w in firsts]
+        + [whole(f.shape) for f in fixed],
+        out_specs=whole((rows, width)),
+        out_shape=shaped((rows, width), bf16),
+        scratch_shapes=[pltpu.VMEM((rows, width), f32)],
+        compiler_params=params(LIM_back),
+        cost_estimate=cost(14),
+        name="back",
     )(
-        rank, normed_t, prep[0], b_grad, c_grad, kernels, rate_tiles, deep[0][3], deep[1][3],
-        deep[0][4], deep[1][4], prep[12], prep[11],
+        deep[0][0], deep[1][0], back[0][1], back[1][1], *firsts, *seconds, *extras, *firsts, *fixed
     )
 
 
@@ -851,80 +952,70 @@
             pltpu.VMEM((chunks, STATE, GROUP), f32),
             pltpu.VMEM((chunks, 8, GROUP), f32),
         ],
-        compiler_params=params(),
+        compiler_params=params(LIM_mix),
         cost_estimate=cost(14),
         name="mix",
     )(length, normed, content, filters, shortcut, c_rows, select_t, gram, ends, starts, steps, ends_t, starts_t)
 
 
-def gate_forward(length, normed, weights, amplitude, mixed, carried, finals, inner_width):
+def gate_both(length, normed, normed_t, tokens, cotangent, cotangent_t, seconds, amplitude, kept, inner_width):
     rows, width = normed.shape
-    inner = mixed.shape[1]
-    grid = inner // GROUP
-    first = carried is None
-    last = finals is not None
-    ins = [length, normed, weights, weights, amplitude, mixed]
-    specs = [scalar, whole(normed.shape), columns(width), columns(width, after=grid), columns(1), columns(rows)]
-    if not first:
-        ins += list(carried)
-        specs += [whole(c.shape) for c in carried]
-    outs = [shaped((rows, inner), f32)]
-    out_specs = [columns(rows)]
-    scratch = [pltpu.VMEM((rows, GROUP), bf16), pltpu.VMEM((rows, GROUP), f32)]
-    if last:
-        ins += list(finals)
-        specs += [whole(c.shape) for c in finals]
-        outs += [shaped((rows, BLOCK), f32), shaped((rows, BLOCK), f32), shaped((rows, width), bf16)]
-        out_specs += [whole((rows, BLOCK)), whole((rows, BLOCK)), whole((rows, width))]
-        scratch = [pltpu.VMEM((rows, BLOCK), f32), pltpu.VMEM((rows, width), f32)] + scratch
-    else:
-        outs += [shaped((rows, BLOCK), f32), shaped((rows, width), f32)]
-        out_specs += [whole((rows, BLOCK)), whole((rows, width))]
-    return pl.pallas_call(
-        functools.partial(gate_kernel, first, last, inner_width),
-        grid=(grid,),
+    inner = kept[0][0].shape[1]
+    half = inner // GROUP
+    groups = 2 * half
+
+    def read(h):
+        def at(g):
+            k = g % groups
+            return jnp.minimum(k, half - 1) if h == 0 else jnp.maximum(k - half, 0)
+
+        return at
+
+    def write(h):
+        return lambda g: jnp.clip(g - groups - h * half, 0, half - 1)
+
+    def blocks(height, at, after=0):
+        return pl.BlockSpec((height, GROUP), lambda g: (0, at(g) + after))
+
+    fixed = (normed, normed_t, tokens, cotangent, cotangent_t)
+    ins = [length, *fixed, *seconds, *seconds, amplitude]
+    ins += [kept[0][0], kept[1][0], kept[0][1], kept[1][1]]
+    specs = [scalar] + [whole(f.shape) for f in fixed]
+    specs += [blocks(width, read(h)) for h in range(2)]
+    specs += [blocks(width, read(h), half) for h in range(2)]
+    specs += [pl.BlockSpec((1, GROUP), lambda g: (0, g % groups))]
+    specs += [blocks(rows, read(h)) for h in range(2)] * 2
+    heights = (rows, rows, width, width, 1, 1)
+    kinds = (bf16, bf16, bf16, bf16, f32, f32)
+    outs = [shaped((n, inner), k) for n, k in zip(heights, kinds) for _ in range(2)]
+    out_specs = [blocks(n, write(h)) for n in heights for h in range(2)]
+    outs += [shaped((rows, width), bf16), shaped((width, BLOCK), f32)]
+    out_specs += [whole((rows, width)), whole((width, BLOCK))]
+    got = pl.pallas_call(
+        functools.partial(gate_kernel, inner_width),
+        grid=(2 * groups,),
         in_specs=specs,
         out_specs=tuple(out_specs),
         out_shape=tuple(outs),
-        scratch_shapes=scratch,
-        compiler_params=params(),
-        cost_estimate=cost(7),
+        scratch_shapes=[
+            pltpu.VMEM((rows, BLOCK), f32),
+            pltpu.VMEM((rows, width), f32),
+            pltpu.VMEM((groups, rows, GROUP), f32),
+            pltpu.VMEM((rows, BLOCK), f32),
+            pltpu.VMEM((rows, BLOCK), f32),
+            pltpu.VMEM((rows, GROUP), bf16),
+            pltpu.VMEM((rows, GROUP), f32),
+            pltpu.VMEM((rows, GROUP), bf16),
+            pltpu.VMEM((rows, GROUP), bf16),
+        ],
+        compiler_params=params(LIM_gate),
+        cost_estimate=cost(35),
         name="gate",
     )(*ins)
-
-
-def gate_backward(
-    cotangent, cotangent_t, normed_t, weights, amplitude, mixed, gate_in, x_low, scale, cross
-):
-    rows, width = cotangent.shape
-    inner = mixed.shape[1]
-    return pl.pallas_call(
-        gate_back_kernel,
-        grid=(inner // GROUP,),
-        in_specs=[
-            whole(cotangent.shape), whole(cotangent_t.shape), whole(normed_t.shape),
-            columns(width, after=inner // GROUP), columns(1), columns(rows), columns(rows),
-            columns(rows), whole(scale.shape), whole(cross.shape),
-        ],
-        out_specs=(
-            columns(rows), columns(rows), columns(width), columns(width), columns(1), columns(1),
-        ),
-        out_shape=(
-            shaped((rows, inner), bf16),
-            shaped((rows, inner), bf16),
-            shaped((width, inner), bf16),
-            shaped((width, inner), bf16),
-            shaped((1, inner), f32),
-            shaped((1, inner), f32),
-        ),
-        scratch_shapes=[pltpu.VMEM((rows, GROUP), bf16), pltpu.VMEM((rows, GROUP), f32)],
-        compiler_params=params(),
-        cost_estimate=cost(8),
-        name="gate_back",
-    )(cotangent, cotangent_t, normed_t, weights, amplitude, mixed, gate_in, x_low, scale, cross)
-
-
-def mix_backward(half, length, normed_t, filters, shortcut, prep, mixed_grad, kept, carried, last):
+    return [got[h:12:2] for h in range(2)], got[12], got[13]
+
+
+def mix_backward(half, length, normed_t, weights, filters, shortcut, prep, mixed_grad, kept, carried, last):
     (_, b_rows, c_rows, select_t, _, gram_t, ends, starts, steps, ends_t, starts_t, _, _) = prep
     _, x_low, values, early, late = kept
     width, rows = normed_t.shape
@@ -934,8 +1025,9 @@
     first = carried is None
     wide = GROUP // HEAD * BLOCK
     shared = (b_rows, c_rows, select_t, gram_t, ends, starts, steps, ends_t, starts_t)
-    ins = [length, normed_t, filters, shortcut, *shared, mixed_grad, x_low, values, early, late]
-    specs = [scalar, whole(normed_t.shape), columns(4), columns(1)]
+    ins = [length, normed_t, weights, filters, shortcut, *shared]
+    ins += [mixed_grad, x_low, values, early, late]
+    specs = [scalar, whole(normed_t.shape), columns(width), columns(4), columns(1)]
     specs += [whole(s.shape) for s in shared[:-2]] + [turned(half * grid, rows)] * 2
     specs += [columns(rows)] * 3 + [planes((chunks, STATE, GROUP))] * 2
     if not first:
@@ -949,6 +1041,7 @@
         out_specs=(
             columns(rows), columns(width), columns(4), lead((tall, BLOCK)), lead((tall, BLOCK)),
             whole((chunks, BLOCK, BLOCK)), whole((rows, STATE)), whole((rows, STATE)),
+            whole((width, BLOCK)),
         ),
         out_shape=(
             shaped((rows, inner), bf16),
@@ -959,6 +1052,7 @@
             shaped((chunks, BLOCK, BLOCK), f32),
             shaped((rows, STATE), f32),
             shaped((rows, STATE), f32),
+            shaped((width, BLOCK), f32),
         ),
         scratch_shapes=[
             pltpu.VMEM((rows, wide), f32),
@@ -975,7 +1069,7 @@
             pltpu.VMEM((tall, BLOCK), f32),
             pltpu.VMEM((chunks, 8, GROUP), f32),
         ],
-        compiler_params=params(),
+        compiler_params=params(LIM_mix_back),
         cost_estimate=cost(28),
         name="mix_back",
     )(*ins)
@@ -1043,7 +1137,7 @@
         in_specs=[scalar] + [vmem] * PLANE,
         out_specs=vmem,
         out_shape=shaped((PLANE * count, block, width), parts[0].dtype),
-        compiler_params=params(),
+        compiler_params=params(LIM_place),
         cost_estimate=cost(2),
         name="place",
     )(places.astype(jnp.int32), *parts)
@@ -1154,8 +1248,13 @@
 
     state_half = state_cols // parts
     own_select = lax.dynamic_slice_in_dim(selector, rank * state_half, state_half, 1)
+    spaced = heads // (GROUP // HEAD) * SLOTS
+    step_local = jnp.pad(
+        timestep.reshape(-1, spaced // SLOTS, GROUP // HEAD),
+        ((0, 0), (0, 0), (0, SLOTS - GROUP // HEAD)),
+    ).reshape(-1, spaced)
     first_local = jnp.concatenate(
-        (content, pad_columns(jnp.concatenate((own_select, timestep), axis=1), BLOCK)), axis=1
+        (content, pad_columns(jnp.concatenate((own_select, step_local), axis=1), BLOCK)), axis=1
     )
     second_local = jnp.concatenate((gating, outgoing.T), axis=1)
     first_column = gather_column(first_local)
@@ -1192,22 +1291,24 @@
 
     filters_2, amplitude_2, biases_2, decays_2, shortcut_2 = zip(unpack(flat), unpack(flat_other))
 
+    per = GROUP // HEAD
+
     def head_lanes(pair):
-        return pad_columns(jnp.concatenate(pair).reshape(1, -1), BLOCK)
+        cut = jnp.concatenate(pair).reshape(-1, per)
+        return pad_columns(jnp.pad(cut, ((0, 0), (0, SLOTS - per))).reshape(1, -1), BLOCK)
 
     rates = jnp.exp(jnp.concatenate(decays_2))
-    rate_lanes = pad_columns(rates.reshape(1, -1), BLOCK)
+    rate_lanes = head_lanes((rates,))
     shortcut_lanes = [jnp.repeat(s, HEAD).reshape(1, inner) for s in shortcut_2]
-    normed, normed_t, inverse_wide = front(tokens, rescale)
+    normed, normed_t, inverse_wide = front(tie(tokens, first_column), rescale)
     dbranch, dbranch_t = mask_rows(length, cotangent)
-    first_column, normed = lax.optimization_barrier((first_column, normed))
     first_parts = gather_plane(first_column)
-    first_parts[0] = tie(first_parts[0], dbranch)
+    first_parts[0] = tie(first_parts[0], dbranch, normed)
     first_own = place(first_parts)
     first_other = swap(first_own)
     firsts = (first_own, first_other)
     prep = prepare(
-        rank_1, normed, first_own, first_other, kernels, head_lanes(biases_2), rate_lanes, heads
+        rank_1, normed, first_own, first_other, kernels, head_lanes(biases_2), rate_lanes, spaced
     )
     kept = [None, None]
     kept[0] = mix_forward(
@@ -1219,22 +1320,11 @@
     kept[1] = mix_forward(
         1, length, normed, tie(first_other, second_own), filters_2[1], shortcut_lanes[1], prep, inner
     )
-    gate_own, squares, total = gate_forward(
-        length, normed, seconds[0], amplitude_2[0], kept[0][0], None, None, inner_width
-    )
-    gate_other, scale, cross, layer_seq = gate_forward(
-        length, normed, seconds[1], amplitude_2[1], kept[1][0], (squares, total),
-        (tokens, dbranch), inner_width,
-    )
-    gates = (gate_own, gate_other)
+    back, layer_seq, gate_sums = gate_both(
+        length, normed, normed_t, tokens, dbranch, dbranch_t, seconds,
+        jnp.concatenate(amplitude_2, axis=1), kept, inner_width,
+    )
     layer_pair = outputs_of(layer_seq)
-
-    back = [None, None]
-    for h in (1, 0):
-        back[h] = gate_backward(
-            dbranch, dbranch_t, normed_t, seconds[h], amplitude_2[h], kept[h][0], gates[h],
-            kept[h][1], scale, cross,
-        )
     second_grads = jnp.concatenate(
         [(back[0][k].astype(f32) + swap(back[1][k]).astype(f32)).astype(bf16) for k in (2, 3)],
         axis=1,
@@ -1244,7 +1334,7 @@
 
     deep = [None, None]
     deep[1] = mix_backward(
-        1, length, normed_t, filters_2[1], shortcut_lanes[1], prep, later_grad, kept[1], None, False
+        1, length, normed_t, firsts[1], filters_2[1], shortcut_lanes[1], prep, later_grad, kept[1], None, False
     )
     content_swapped = swap(deep[1][1])
     early_grad, *landed = lax.optimization_barrier((back[0][0], *[got for _, got in second_sent]))
@@ -1252,76 +1342,45 @@
     second_sent[0] = (second_sent[0][0], tie(second_sent[0][1], deep[1][1]))
     second_moved = middle_sum(second_sent)
     deep[0] = mix_backward(
-        0, length, normed_t, filters_2[0], shortcut_lanes[0], prep, early_grad, kept[0],
+        0, length, normed_t, firsts[0], filters_2[0], shortcut_lanes[0], prep, early_grad, kept[0],
         deep[1][5:8], True,
     )
     content_own, *landed = lax.optimization_barrier((deep[0][1], *[got for _, got in second_moved]))
     second_moved = [(keep, got) for (keep, _), got in zip(second_moved, landed)]
     second_terms = last_sum(second_moved)
 
-    (select_grad, step_rows, extra_own, extra_other, kernels_part, biases_tile, decays_tile) = finish(
-        rank_1, normed_t, prep, deep[0][6], deep[0][7], kernels, rates, deep, heads
+    content_grads = (content_own.astype(f32) + content_swapped.astype(f32)).astype(bf16)
+    content_grads, b_sum = lax.optimization_barrier((content_grads, deep[0][6]))
+    first_sent = start_sum(content_grads)
+    rate_tiles = jnp.broadcast_to(
+        jnp.pad(rates.reshape(-1, per), ((0, 0), (0, SLOTS - per)))[:, :, None],
+        (2 * heads // per, SLOTS, BLOCK),
+    )
+    row_sums = (deep[0][8], deep[1][8], gate_sums)
+    (
+        grad_own, grad_other, extra_own, extra_other, kernels_part, biases_tile, decays_tile, rows_sum
+    ) = finish(
+        rank_1, normed_t, firsts, prep, b_sum, deep[0][7], kernels, rate_tiles, deep, row_sums
     )
 
     def compact(tiles):
-        return jnp.sum(tiles[:, : GROUP // HEAD], axis=2).reshape(2 * heads)
+        return jnp.sum(tiles[:, :per], axis=2).reshape(2 * heads)
 
     biases_part, decays_part = compact(biases_tile), compact(decays_tile)
-    extra_sum = extra_own + swap(extra_other).astype(f32)
-    content_sum = content_own.astype(f32) + content_swapped.astype(f32)
-    first_grads = jnp.concatenate((content_sum, extra_sum), axis=1).astype(bf16)
-    first_terms = last_sum(middle_sum(start_sum(first_grads)))
-
-    spaced = 2 * heads
-    select_2 = [first[:, inner : inner + state_half] for first in firsts]
-    selector_full = jnp.where(
-        rank == 0,
-        jnp.concatenate(select_2, axis=1),
-        jnp.concatenate(select_2[::-1], axis=1),
-    )
-
-    def space_heads(weights):
-        per = GROUP // HEAD
-        cut = weights[:, inner + state_half : inner + state_half + heads]
-        cut = jnp.pad(cut.reshape(width, heads // per, per), ((0, 0), (0, 0), (0, 8 - per)))
-        return cut.reshape(width, spaced)
-
-    timestep_full = jnp.concatenate([space_heads(first) for first in firsts], axis=1)
-
-    def weight_rows(weights, grads):
-        return jnp.sum(weights.astype(f32) * grads.astype(f32), axis=1)
-
-    extra_local = jnp.concatenate(
-        (select_2[0], timestep_full[:, :spaced], select_2[1], timestep_full[:, spaced:]), axis=1
-    )
-    used_cols = state_half + spaced
-    extra_part = jnp.concatenate(
-        (extra_own[:, :used_cols], extra_other[:, :used_cols].astype(f32)), axis=1
-    )
-    scaled_rows = weight_rows(extra_local, extra_part)
-    for h in range(2):
-        scaled_rows = scaled_rows + weight_rows(firsts[h][:, :inner], tie(deep[h][1], content_own))
-        scaled_rows = scaled_rows + weight_rows(
-            seconds[h][:, :inner], tie(back[h][2], content_own)
-        )
-    rescale_part = scaled_rows / rescale
-
-    grad_normed = dot_nt(select_grad, selector_full) + lax.dot_general(
-        step_rows, timestep_full, (((0,), (1,)), ((), ())), preferred_element_type=f32
-    )
-    for h in range(2):
-        grad_normed = grad_normed + dot_nt(tie(deep[h][0], content_own), firsts[h][:, :inner])
-        grad_normed = grad_normed + dot_nt(tie(back[h][1], content_own), seconds[h][:, :inner])
-    inverse = inverse_wide[:, :1]
-    unit = tokens.astype(f32) * inverse
-    weighted = grad_normed * rescale
-    grad_seq = (
-        dbranch.astype(f32)
-        + inverse * weighted
-        - unit * inverse * jnp.mean(weighted * unit, axis=-1, keepdims=True)
-    ).astype(bf16)
+    grad_own, *landed = lax.optimization_barrier((grad_own, *[got for _, got in first_sent]))
+    first_sent = [(keep, got) for (keep, _), got in zip(first_sent, landed)]
+    first_moved = middle_sum(first_sent)
+    rows_sum, extra_other = lax.optimization_barrier((rows_sum, extra_other, first_moved[0][0]))[:2]
+    extra_sum = (extra_own + swap(extra_other).astype(f32)).astype(bf16)
+    rescale_part = jnp.sum(rows_sum, axis=1) / rescale
+    grad_seq = backward_rows(
+        deep, back, firsts, seconds, (grad_own, grad_other), tokens, inverse_wide, rescale, dbranch
+    )
+    grad_seq, *landed = lax.optimization_barrier((grad_seq, *[got for _, got in first_moved]))
+    first_moved = [(keep, got) for (keep, _), got in zip(first_moved, landed)]
+    first_terms = last_sum(first_moved)
     input_grad = join(*outputs_of(grad_seq))
-    layer_out = join(*lax.optimization_barrier((*layer_pair, content_own))[:2])
+    layer_out = join(*lax.optimization_barrier((*layer_pair, grad_seq))[:2])
 
     def per_head(row):
         return jnp.sum(row.reshape(heads, HEAD), axis=1)
@@ -1342,18 +1401,29 @@
     )
     small = small_own + swap(small_other)
     used = small.shape[0]
-    lines = -(-used // (8 * BLOCK)) * 8
+    lines = -(-used // (16 * BLOCK)) * 16
     small = jnp.pad(small, (0, lines * BLOCK - used)).reshape(1, lines, BLOCK)
+    small_high = small.astype(bf16)
+    small_low = (small - small_high.astype(f32)).astype(bf16)
     blocks = lax.axis_size(DP)
-    small_got = exchange(
-        jnp.broadcast_to(small, (blocks, lines, BLOCK)).reshape(blocks * lines, BLOCK)
-    )
-    summed = sum_blocks(small_got, blocks).reshape(-1)
+    own_rows = width // blocks
+    both = jnp.concatenate((small_high, small_low), axis=1)
+    sent = jnp.concatenate(
+        (
+            extra_sum.reshape(blocks, own_rows, BLOCK),
+            jnp.broadcast_to(both, (blocks, 2 * lines, BLOCK)),
+        ),
+        axis=1,
+    )
+    got = lax.all_to_all(sent, DP, 0, 0, tiled=True)
+    gathered = jnp.sum(got.astype(f32), axis=0)
+    extra_total = gathered[:own_rows]
+    summed = (gathered[own_rows : own_rows + lines] + gathered[own_rows + lines :]).reshape(-1)
     cut = (taps + 1) * inner + 3 * heads
     filters_grad, amplitude_grad, biases_grad, decays_grad, shortcut_grad = unpack(summed[:cut])
     second_total = finish_sum(second_terms)
     first_total = finish_sum(first_terms)
-    state_own = first_total[:, inner : inner + state_half]
+    state_own = extra_total[:, :state_half]
     state_other = swap(state_own)
     selector_grad = jnp.where(
         rank == 0,
@@ -1365,10 +1435,10 @@
         input_grad,
         summed[cut : cut + width],
         second_total[:, :inner],
-        first_total[:, :inner],
+        first_total,
         selector_grad,
-        first_total[:, inner + state_half : inner + state_half + spaced]
-        .reshape(-1, spaced // 8, 8)[:, :, : GROUP // HEAD]
+        extra_total[:, state_half : state_half + spaced]
+        .reshape(-1, spaced // SLOTS, SLOTS)[:, :, :per]
         .reshape(-1, heads),
         filters_grad,
         summed[cut + width : used].reshape(taps, state_cols),

time: 359 us -> 313 us (0.87)
  local copies, waits for them, and re-layouts: 45.6 us -> 24.4 us
  other arithmetic: 32.8 us -> 19.9 us
  matrix products: 11.6 us -> 0 us
  Pallas kernels: 166 us -> 172 us
    dot_general x6 -> x0, matrix products: 11.6 us -> none  [the longest x5 11 us: dot_nt(): lax.dot_general(a, b, (((1,), (1,)), ((), ())), preferred_element_type=f32)]
    ppermute x3, waiting for transfers between devices: 6.96 us -> 0.01 us  [gather_plane(): lax.ppermute(column, 'plane', pairs_by(PLANE, k))]
    ppermute x3, waiting for transfers between devices: 0.01 us -> 6.91 us  [gather_column(): lax.ppermute(local, 'column', pairs_by(count, s))]
    pallas_call x5 -> x3, Pallas kernels: 50.3 us -> 55.3 us  [the longest x1 37.4 us: gate_both(): pl.pallas_call(functools.partial(gate_kernel, inner_width), grid=(2 * gro...]
    unnamed x133 -> x58, local copies, waits for them, and re-layouts: 12.2 us -> 7.28 us
    slice x11 -> x4, local copies, waits for them, and re-layouts: 3.91 us -> 0.15 us  [the longest x3 0.14 us: on_device(): extra_total[:, state_half:state_half + spaced]]
  transfers between devices with their start and end apart: 35 -> 35, of which waited for: 9 -> 9; matrix products, arithmetic and copies ran while one was open for 21% -> 11% of each run, Pallas kernels for 40% -> 44%
where the time goes in v3:
time: 313 us; the launch traced here: 307 us
  Pallas kernels  172 us (55%)
  starting transfers between devices  43.3 us (14%)
  waiting for transfers between devices  33.2 us (11%)
  local copies, waits for them, and re-layouts  24.4 us (8%)
  other arithmetic  19.9 us (6%)
  between operations  15.2 us (5%)
    pallas_call x2, Pallas kernels, mix_backward(): pl.pallas_call(functools.partial(mix_back_kernel, half, first, last), gri...  66.4 us
    pallas_call x1, Pallas kernels, gate_both(): pl.pallas_call(functools.partial(gate_kernel, inner_width), grid=(2 * gro...  37.4 us
    pallas_call x2, Pallas kernels, mix_forward(): pl.pallas_call(functools.partial(mix_kernel, half), grid=(grid,), in_spec...  33.2 us
    ppermute x6, waiting for transfers between devices, last_sum(): lax.ppermute(block_of(column, high ^ s, 0), 'column', pairs_by(count, s))  13.5 us
    pallas_call x1, Pallas kernels, backward_rows(): pl.pallas_call(back_kernel, grid=(inner // GROUP,), in_specs=[columns(row...  12.8 us
    ppermute x8, starting transfers between devices, plane_send(): return lax.ppermute(v, 'plane', pairs_by(PLANE, by))  9.37 us
    ppermute x6, starting transfers between devices, last_sum(): lax.ppermute(block_of(column, high ^ s, 0), 'column', pairs_by(count, s))  8.9 us
    all_to_all x2, starting transfers between devices, across(): lax.all_to_all(blocks, 'tensor', 0, 0, tiled=True).reshape(rows, width)  7.48 us
  transfers between devices with their start and end apart: 35, of which 9 were waited for; matrix products, arithmetic and copies ran while one was open for 11% of the time, Pallas kernels for 44%

profile of v3, /device:TPU:0, one launch (start us, length us, event | category | flops | bytes accessed | tf_op | source)
XLA Modules:
  0.0 307.4 jit_solution(6467879167649561136)
XLA Ops:
  10.7 3.1 %collective-permute-start = (bf16[48,896]{1,0:T(8,128)(2,1)S(1)}, bf16[48,896]{1,0:T(8,128)(2,1)S(1)}, u32[]{:S(2)}, u32[]{:S(2)}) collective-permute-start(bf16[48,896]{1,0:T(8,128)(2,1)S(1)} %get-tuple-element.245), channel_id=1, source_target_pairs={{0,8},{8,0},{16,24},{24,16},{1,9},{9,1},{17,25},{25,17},{2,10},{10... | collective-permute-start | bytes 258056 | tf_op jit(solution)/shard_map/ppermute | solution.py:1120
  13.8 2.6 collective-permute-start.1
  16.4 6.9 %collective-permute-done.1 = bf16[48,896]{1,0:T(8,128)(2,1)S(1)} collective-permute-done((bf16[48,896]{1,0:T(8,128)(2,1)S(1)}, bf16[48,896]{1,0:T(8,128)(2,1)S(1)}, u32[]{:S(2)}, u32[]{:S(2)}) %collective-permute-start.1) | collective-permute-done | bytes 86048 | tf_op jit(solution)/shard_map/ppermute | solution.py:1120
  27.0 3.8 %all-to-all-start.1 = ((bf16[2,512,768]{2,1,0:T(8,128)(2,1)}), bf16[2,512,768]{2,1,0:T(8,128)(2,1)S(1)}, u32[]{:S(2)}, u32[]{:S(2)}) async-start(bf16[2,512,768]{2,1,0:T(8,128)(2,1)} %bitcast.150), calls=%async_computation.1 | async-start | bytes 3145728 | tf_op jit(solution)/shard_map/all_to_all | solution.py:1265
  34.4 3.7 %all-to-all-start = ((bf16[2,512,768]{2,1,0:T(8,128)(2,1)}), bf16[2,512,768]{2,1,0:T(8,128)(2,1)S(1)}, u32[]{:S(2)}, u32[]{:S(2)}) async-start(bf16[2,512,768]{2,1,0:T(8,128)(2,1)} %bitcast), calls=%async_computation | async-start | bytes 3145728 | tf_op jit(solution)/shard_map/all_to_all | solution.py:1265
  38.1 4.4 %mask_rows.1 = (bf16[1024,768]{1,0:T(8,128)(2,1)}, bf16[768,1024]{1,0:T(8,128)(2,1)}) custom-call(s32[1]{0:T(128)} %dynamic_slice.94.length.refs_0_, bf16[1024,768]{1,0:T(8,128)(2,1)} %bitcast.148), custom_call_target="tpu_custom_call" | custom-call | bytes 15000000 | tf_op jit(solution)/shard_map/mask_rows/pallas_call | solution.py:728
  44.3 4.1 %front.1 = (bf16[1024,768]{1,0:T(8,128)(2,1)}, bf16[768,1024]{1,0:T(8,128)(2,1)}, f32[1024,128]{1,0:T(8,128)}) custom-call(bf16[1024,768]{1,0:T(8,128)(2,1)} %bitcast.144, f32[1,768]{1,0:T(1,128)} %reshape.219.rescale), custom_call_target="tpu_custom_call" | custom-call | bytes 15000000 | tf_op jit(solution)/shard_map/front/pallas_call | solution.py:697
  50.0 2.5 place.1
  58.3 5.7 %prep.1 = (f32[1024,128]{1,0:T(8,128)}, bf16[1024,64]{1,0:T(8,128)(2,1)}, bf16[1024,64]{1,0:T(8,128)(2,1)}, bf16[8,128,128]{2,1,0:T(8,128)(2,1)}, f32[8,128,128]...) custom-call(s32[1]{0:T(128)} %bitcast.27.rank, ...), custom_call_target="tpu_custom_call" | custom-call | bytes 12000000 | tf_op jit(solution)/shard_map/prep/pallas_call | solution.py:661
  64.0 16.8 %mix.2 = (bf16[1024,768]{1,0:T(8,128)(2,1)}, bf16[1024,768]{1,0:T(8,128)(2,1)}, bf16[1024,768]{1,0:T(8,128)(2,1)}, bf16[8,64,768]{2,1,0:T(8,128)(2,1)}, bf16[8,64,768]{2,1,0:T(8,128)(2,1)}) custom-call(s32[1]{0:T(128)} %dynamic_slice.94.length.refs_0_, bf16[1024,768]{1,0:T(8,128)(2,1)} %get-tuple-element.107.normed, bf16[768,896]{1,0:T(8,128)(2,1)} %bitcast.139, ...), custom_call_target="tpu_custom_call" | custom-call | bytes 42000000 | tf_op jit(solution)/shard_map/mix/pallas_call | solution.py:926
  82.9 16.4 %mix.3 = (bf16[1024,768]{1,0:T(8,128)(2,1)}, bf16[1024,768]{1,0:T(8,128)(2,1)}, bf16[1024,768]{1,0:T(8,128)(2,1)}, bf16[8,64,768]{2,1,0:T(8,128)(2,1)}, bf16[8,64,768]{2,1,0:T(8,128)(2,1)}) custom-call(s32[1]{0:T(128)} %dynamic_slice.94.length.refs_0_, bf16[1024,768]{1,0:T(8,128)(2,1)} %get-tuple-element.107.normed, bf16[768,896]{1,0:T(8,128)(2,1)} %copy-done.2, ...), custom_call_target="tpu_custom_call" | custom-call | bytes 42000000 | tf_op jit(solution)/shard_map/mix/pallas_call | solution.py:926
  100.8 37.4 %gate.1 = (bf16[1024,768]{1,0:T(8,128)(2,1)}, bf16[1024,768]{1,0:T(8,128)(2,1)}, bf16[1024,768]{1,0:T(8,128)(2,1)}, bf16[1024,768]{1,0:T(8,128)(2,1)}, bf16[768,...) custom-call(s32[1]{0:T(128)} %dynamic_slice.94.length.refs_0_, ...), custom_call_target="tpu_custom_call" | custom-call | bytes 105000000 | tf_op jit(solution)/shard_map/gate/pallas_call | solution.py:994
  138.8 2.5 collective-permute-done.10
  148.0 32.6 %mix_back.2 = (bf16[1024,768]{1,0:T(8,128)(2,1)}, bf16[768,768]{1,0:T(8,128)(2,1)}, f32[4,768]{1,0:T(4,128)}, f32[3,64,128]{2,1,0:T(8,128)}, f32[3,64,128]{2,1,0...) custom-call(s32[1]{0:T(128)} %dynamic_slice.94.length.refs_0_, ...), custom_call_target="tpu_custom_call" | custom-call | bytes 84000000 | tf_op jit(solution)/shard_map/mix_back/pallas_call | solution.py:1037
  183.3 33.8 %mix_back.3 = (bf16[1024,768]{1,0:T(8,128)(2,1)}, bf16[768,768]{1,0:T(8,128)(2,1)}, f32[4,768]{1,0:T(4,128)}, f32[3,64,128]{2,1,0:T(8,128)}, f32[3,64,128]{2,1,0...) custom-call(s32[1]{0:T(128)} %dynamic_slice.94.length.refs_0_, ...), custom_call_target="tpu_custom_call" | custom-call | bytes 84000000 | tf_op jit(solution)/shard_map/mix_back/pallas_call | solution.py:1037
  224.6 3.6 %collective-permute-done.24 = bf16[48,1536]{1,0:T(8,128)(2,1)S(1)} collective-permute-done((bf16[48,1536]{1,0:T(8,128)(2,1)S(1)}, bf16[48,1536]{1,0:T(8,128)(2,1)S(1)}, u32[]{:S(2)}, u32[]{:S(2)}) %collective-permute-start.24) | collective-permute-done | bytes 147488 | tf_op jit(solution)/shard_map/ppermute | solution.py:1185
  228.1 6.5 %collective-permute-done.25 = bf16[48,1536]{1,0:T(8,128)(2,1)S(1)} collective-permute-done((bf16[48,1536]{1,0:T(8,128)(2,1)S(1)}, bf16[48,1536]{1,0:T(8,128)(2,1)S(1)}, u32[]{:S(2)}, u32[]{:S(2)}) %collective-permute-start.25) | collective-permute-done | bytes 147488 | tf_op jit(solution)/shard_map/ppermute | solution.py:1185
  235.7 5.1 %finish.1 = (bf16[1024,128]{1,0:T(8,128)(2,1)}, bf16[1024,128]{1,0:T(8,128)(2,1)}, f32[768,128]{1,0:T(8,128)}, bf16[768,128]{1,0:T(8,128)(2,1)}, f32[4,128]{1,0:...) custom-call(s32[1]{0:T(128)} %bitcast.27.rank, ...), custom_call_target="tpu_custom_call" | custom-call | bytes 18000000 | tf_op jit(solution)/shard_map/finish/pallas_call | solution.py:838
  248.8 5.0 %collective-permute-done.18 = bf16[2,4,48,384]{3,2,1,0:T(8,128)(2,1)S(1)} collective-permute-done((bf16[2,4,48,384]{3,2,1,0:T(8,128)(2,1)S(1)}, bf16[2,4,48,384]{3,2,1,0:T(8,128)(2,1)S(1)}, u32[]{:S(2)}, u32[]{:S(2)}) %collective-permute-start.18) | collective-permute-done | bytes 294944 | tf_op jit(solution)/shard_map/ppermute | solution.py:1152
  260.3 6.3 %all-to-all-start.2 = ((bf16[16,144,128]{2,1,0:T(8,128)(2,1)}), bf16[16,144,128]{2,1,0:T(8,128)(2,1)S(1)}, u32[]{:S(2)}, u32[]{:S(2)}) async-start(bf16[16,144,128]{2,1,0:T(8,128)(2,1)} %pad_maximum_fusion.3), calls=%async_computation.2 | async-start | bytes 1179648 | tf_op jit(solution)/shard_map/all_to_all | solution.py:1418
  266.6 12.8 %back.1 = bf16[1024,768]{1,0:T(8,128)(2,1)} custom-call(bf16[1024,768]{1,0:T(8,128)(2,1)} %get-tuple-element.147.values_own, bf16[1024,768]{1,0:T(8,128)(2,1)} %get-tuple-element.148.values_other, bf16[1024,768]{1,0:T(8,128)(2,1)} %get-tuple-element.149.gate_own, bf16[1024,768]{1,0:T(8,128)(2,1)} %get-tuple-element.150.gate_other, ...), custom_call_target="tpu_custom_call" | custom-call | bytes 42000000 | tf_op jit(solution)/shard_map/back/pallas_call | solution.py:901
  283.9 2.4 collective-permute-start.28
  286.3 3.1 %maximum_select_fusion = bf16[1024,768]{1,0:T(8,128)(2,1)} fusion(bf16[512,768]{1,0:T(8,128)(2,1)} %collective-permute-done.9, bf16[512,768]{1,0:T(8,128)(2,1)S(1)} %get-tuple-element.178, pred[]{:T(512)S(6)} %eq.2), kind=kLoop, calls=%fused_computation.4 | loop fusion | flops 7077888 | bytes 3145729 | tf_op jit(solution)/shard_map/jit(_where)/select_n | solution.py:1273
  289.4 3.4 %collective-permute-done.28 = bf16[48,768]{1,0:T(8,128)(2,1)S(1)} collective-permute-done((bf16[48,768]{1,0:T(8,128)(2,1)S(1)}, bf16[48,768]{1,0:T(8,128)(2,1)S(1)}, u32[]{:S(2)}, u32[]{:S(2)}) %collective-permute-start.28) | collective-permute-done | bytes 73760 | tf_op jit(solution)/shard_map/ppermute | solution.py:1185
  (228 shorter events, 67.9 us)
Async XLA Ops:
  7.2 73.5 %all-gather.2.cloned.1.call-start = ((), (), s32[]{:S(2)}) async-start(), calls=%async_computation.3 | async-start | bytes 2506752 | tf_op jit(solution)/shard_map/all_gather | solution.py:1261
  13.8 9.5 %collective-permute-start.1 = (bf16[48,896]{1,0:T(8,128)(2,1)S(1)}, bf16[48,896]{1,0:T(8,128)(2,1)S(1)}, u32[]{:S(2)}, u32[]{:S(2)}) collective-permute-start(bf16[48,896]{1,0:T(8,128)(2,1)S(1)} %get-tuple-element.245), channel_id=1, source_target_pairs={{0,16},{8,24},{16,0},{24,8},{1,17},{9,25},{17,1},{25,9},{2,18},{10... | collective-permute-start | bytes 258056 | tf_op jit(solution)/shard_map/ppermute | solution.py:1120
  23.4 25.0 %collective-permute-start.3 = (bf16[4,48,896]{2,1,0:T(8,128)(2,1)S(1)}, bf16[4,48,896]{2,1,0:T(8,128)(2,1)S(1)}, u32[]{:S(2)}, u32[]{:S(2)}) collective-permute-start(bf16[4,48,896]{2,1,0:T(8,128)(2,1)S(1)} %pad_maximum_fusion.4.refs_0_), channel_id=1, source_target_pairs={{0,2},{2,0},{4,6},{6,4},{1,3},{3,1},{5,7},{7,5},{8,10},{10,8},{12,... | collective-permute-start | bytes 1032200 | tf_op jit(solution)/shard_map/ppermute | solution.py:1126
  25.0 23.5 %collective-permute-start.4 = (bf16[4,48,896]{2,1,0:T(8,128)(2,1)S(1)}, bf16[4,48,896]{2,1,0:T(8,128)(2,1)S(1)}, u32[]{:S(2)}, u32[]{:S(2)}) collective-permute-start(bf16[4,48,896]{2,1,0:T(8,128)(2,1)S(1)} %pad_maximum_fusion.4.refs_0_), channel_id=1, source_target_pairs={{0,4},{2,6},{4,0},{6,2},{1,5},{3,7},{5,1},{7,3},{8,12},{10,14},{12... | collective-permute-start | bytes 1032200 | tf_op jit(solution)/shard_map/ppermute | solution.py:1126
  26.5 22.0 %collective-permute-start.5 = (bf16[4,48,896]{2,1,0:T(8,128)(2,1)S(1)}, bf16[4,48,896]{2,1,0:T(8,128)(2,1)S(1)}, u32[]{:S(2)}, u32[]{:S(2)}) collective-permute-start(bf16[4,48,896]{2,1,0:T(8,128)(2,1)S(1)} %pad_maximum_fusion.4.refs_0_), channel_id=1, source_target_pairs={{0,6},{2,4},{4,2},{6,0},{1,7},{3,5},{5,3},{7,1},{8,14},{10,12},{12... | collective-permute-start | bytes 1032200 | tf_op jit(solution)/shard_map/ppermute | solution.py:1126
  34.4 8.7 %all-to-all-start = ((bf16[2,512,768]{2,1,0:T(8,128)(2,1)}), bf16[2,512,768]{2,1,0:T(8,128)(2,1)S(1)}, u32[]{:S(2)}, u32[]{:S(2)}) async-start(bf16[2,512,768]{2,1,0:T(8,128)(2,1)} %bitcast), calls=%async_computation | async-start | bytes 3145728 | tf_op jit(solution)/shard_map/all_to_all | solution.py:1265
  80.8 18.6 %collective-permute-start.8 = (bf16[768,1536]{1,0:T(8,128)(2,1)}, bf16[768,1536]{1,0:T(8,128)(2,1)S(1)}, u32[]{:S(2)}, u32[]{:S(2)}) collective-permute-start(bf16[768,1536]{1,0:T(8,128)(2,1)} %all-gather.2.cloned.1.call-done.gating_own.out_own), channel_id=1, source_target_pairs={{0,1},{1,0},{2,3},{3,2},{4,5},{5,4},{6,7},{7,6},{8,9},{9,8},{10,11... | collective-permute-start | bytes 7077896 | tf_op jit(solution)/shard_map/ppermute | solution.py:1210
  143.9 36.7 %collective-permute-start.13 = (bf16[2,4,48,768]{3,2,1,0:T(8,128)(2,1)S(1)}, bf16[2,4,48,768]{3,2,1,0:T(8,128)(2,1)S(1)}, u32[]{:S(2)}, u32[]{:S(2)}) collective-permute-start(bf16[2,4,48,768]{3,2,1,0:T(8,128)(2,1)S(1)} %pad_maximum_fusion.2), channel_id=1, source_target_pairs={{0,4},{2,6},{4,0},{6,2},{1,5},{3,7},{5,1},{7,3},{8,12},{10,14},{12... | collective-permute-start | bytes 1769480 | tf_op jit(solution)/shard_map/ppermute | solution.py:1152
  146.5 34.1 %collective-permute-start.12 = (bf16[2,4,48,768]{3,2,1,0:T(8,128)(2,1)}, bf16[2,4,48,768]{3,2,1,0:T(8,128)(2,1)S(1)}, u32[]{:S(2)}, u32[]{:S(2)}) collective-permute-start(bf16[2,4,48,768]{3,2,1,0:T(8,128)(2,1)} %pad_maximum_fusion.1), channel_id=1, source_target_pairs={{0,2},{2,0},{4,6},{6,4},{1,3},{3,1},{5,7},{7,5},{8,10},{10,8},{12,... | collective-permute-start | bytes 1769480 | tf_op jit(solution)/shard_map/ppermute | solution.py:1152
  181.6 35.6 %collective-permute-start.15 = (bf16[4,48,768]{2,1,0:T(8,128)(2,1)}, bf16[4,48,768]{2,1,0:T(8,128)(2,1)S(1)}, u32[]{:S(2)}, u32[]{:S(2)}) collective-permute-start(bf16[4,48,768]{2,1,0:T(8,128)(2,1)} %slice_bitcast_fusion.2), channel_id=1, source_target_pairs={{0,2},{2,0},{4,6},{6,4},{1,3},{3,1},{5,7},{7,5},{8,10},{10,8},{12,... | collective-permute-start | bytes 884744 | tf_op jit(solution)/shard_map/ppermute | solution.py:1152
  182.3 34.8 %collective-permute-start.14 = (bf16[4,48,768]{2,1,0:T(8,128)(2,1)S(1)}, bf16[4,48,768]{2,1,0:T(8,128)(2,1)S(1)}, u32[]{:S(2)}, u32[]{:S(2)}) collective-permute-start(bf16[4,48,768]{2,1,0:T(8,128)(2,1)S(1)} %slice_bitcast_fusion.3), channel_id=1, source_target_pairs={{0,4},{2,6},{4,0},{6,2},{1,5},{3,7},{5,1},{7,3},{8,12},{10,14},{12... | collective-permute-start | bytes 884744 | tf_op jit(solution)/shard_map/ppermute | solution.py:1152
  182.8 51.9 %collective-permute-start.16 = (bf16[768,768]{1,0:T(8,128)(2,1)}, bf16[768,768]{1,0:T(8,128)(2,1)S(1)}, u32[]{:S(2)}, u32[]{:S(2)}) collective-permute-start(bf16[768,768]{1,0:T(8,128)(2,1)} %get-tuple-element.154), channel_id=1, source_target_pairs={{0,1},{1,0},{2,3},{3,2},{4,5},{5,4},{6,7},{7,6},{8,9},{9,8},{10,11... | collective-permute-start | bytes 3538952 | tf_op jit(solution)/shard_map/ppermute | solution.py:1210
  219.1 9.1 %collective-permute-start.24 = (bf16[48,1536]{1,0:T(8,128)(2,1)S(1)}, bf16[48,1536]{1,0:T(8,128)(2,1)S(1)}, u32[]{:S(2)}, u32[]{:S(2)}) collective-permute-start(bf16[48,1536]{1,0:T(8,128)(2,1)S(1)} %get-tuple-element.228), channel_id=1, source_target_pairs={{0,8},{8,0},{16,24},{24,16},{1,9},{9,1},{17,25},{25,17},{2,10},{10... | collective-permute-start | bytes 442376 | tf_op jit(solution)/shard_map/ppermute | solution.py:1185
  220.7 13.9 %collective-permute-start.25 = (bf16[48,1536]{1,0:T(8,128)(2,1)S(1)}, bf16[48,1536]{1,0:T(8,128)(2,1)S(1)}, u32[]{:S(2)}, u32[]{:S(2)}) collective-permute-start(bf16[48,1536]{1,0:T(8,128)(2,1)S(1)} %get-tuple-element.229), channel_id=1, source_target_pairs={{0,16},{8,24},{16,0},{24,8},{1,17},{9,25},{17,1},{25,9},{2,18},{10... | collective-permute-start | bytes 442376 | tf_op jit(solution)/shard_map/ppermute | solution.py:1185
  222.1 12.5 %collective-permute-start.26 = (bf16[48,1536]{1,0:T(8,128)(2,1)S(1)}, bf16[48,1536]{1,0:T(8,128)(2,1)S(1)}, u32[]{:S(2)}, u32[]{:S(2)}) collective-permute-start(bf16[48,1536]{1,0:T(8,128)(2,1)S(1)} %get-tuple-element.230), channel_id=1, source_target_pairs={{0,24},{8,16},{16,8},{24,0},{1,25},{9,17},{17,9},{25,1},{2,26},{10... | collective-permute-start | bytes 442376 | tf_op jit(solution)/shard_map/ppermute | solution.py:1185
  224.5 61.8 %collective-permute-start.9 = (bf16[512,768]{1,0:T(8,128)(2,1)}, bf16[512,768]{1,0:T(8,128)(2,1)}, u32[]{:S(2)}, u32[]{:S(2)}) collective-permute-start(bf16[512,768]{1,0:T(8,128)(2,1)} %get-tuple-element.216), channel_id=1, source_target_pairs={{0,1},{1,0},{2,3},{3,2},{4,5},{5,4},{6,7},{7,6},{8,9},{9,8},{10,11... | collective-permute-start | bytes 2359304 | tf_op jit(solution)/shard_map/ppermute | solution.py:1210
  240.8 17.6 %collective-permute-start.22 = (bf16[768,128]{1,0:T(8,128)(2,1)}, bf16[768,128]{1,0:T(8,128)(2,1)}, u32[]{:S(2)}, u32[]{:S(2)}) collective-permute-start(bf16[768,128]{1,0:T(8,128)(2,1)} %get-tuple-element.183), channel_id=1, source_target_pairs={{0,1},{1,0},{2,3},{3,2},{4,5},{5,4},{6,7},{7,6},{8,9},{9,8},{10,11... | collective-permute-start | bytes 589832 | tf_op jit(solution)/shard_map/ppermute | solution.py:1210
  244.8 9.0 %collective-permute-start.18 = (bf16[2,4,48,384]{3,2,1,0:T(8,128)(2,1)S(1)}, bf16[2,4,48,384]{3,2,1,0:T(8,128)(2,1)S(1)}, u32[]{:S(2)}, u32[]{:S(2)}) collective-permute-start(bf16[2,4,48,384]{3,2,1,0:T(8,128)(2,1)S(1)} %pad_maximum_fusion.6), channel_id=1, source_target_pairs={{0,4},{2,6},{4,0},{6,2},{1,5},{3,7},{5,1},{7,3},{8,12},{10,14},{12... | collective-permute-start | bytes 884744 | tf_op jit(solution)/shard_map/ppermute | solution.py:1152
  247.2 8.9 %collective-permute-start.17 = (bf16[2,4,48,384]{3,2,1,0:T(8,128)(2,1)}, bf16[2,4,48,384]{3,2,1,0:T(8,128)(2,1)S(1)}, u32[]{:S(2)}, u32[]{:S(2)}) collective-permute-start(bf16[2,4,48,384]{3,2,1,0:T(8,128)(2,1)} %pad_maximum_fusion.5), channel_id=1, source_target_pairs={{0,2},{2,0},{4,6},{6,4},{1,3},{3,1},{5,7},{7,5},{8,10},{10,8},{12,... | collective-permute-start | bytes 884744 | tf_op jit(solution)/shard_map/ppermute | solution.py:1152
  256.2 23.3 %collective-permute-start.20 = (bf16[4,48,384]{2,1,0:T(8,128)(2,1)S(1)}, bf16[4,48,384]{2,1,0:T(8,128)(2,1)S(1)}, u32[]{:S(2)}, u32[]{:S(2)}) collective-permute-start(bf16[4,48,384]{2,1,0:T(8,128)(2,1)S(1)} %slice_bitcast_fusion.7), channel_id=1, source_target_pairs={{0,2},{2,0},{4,6},{6,4},{1,3},{3,1},{5,7},{7,5},{8,10},{10,8},{12,... | collective-permute-start | bytes 442376 | tf_op jit(solution)/shard_map/ppermute | solution.py:1152
  257.8 21.7 %collective-permute-start.19 = (bf16[4,48,384]{2,1,0:T(8,128)(2,1)S(1)}, bf16[4,48,384]{2,1,0:T(8,128)(2,1)S(1)}, u32[]{:S(2)}, u32[]{:S(2)}) collective-permute-start(bf16[4,48,384]{2,1,0:T(8,128)(2,1)S(1)} %slice_bitcast_fusion.8), channel_id=1, source_target_pairs={{0,4},{2,6},{4,0},{6,2},{1,5},{3,7},{5,1},{7,3},{8,12},{10,14},{12... | collective-permute-start | bytes 442376 | tf_op jit(solution)/shard_map/ppermute | solution.py:1152
  260.3 35.1 %all-to-all-start.2 = ((bf16[16,144,128]{2,1,0:T(8,128)(2,1)}), bf16[16,144,128]{2,1,0:T(8,128)(2,1)S(1)}, u32[]{:S(2)}, u32[]{:S(2)}) async-start(bf16[16,144,128]{2,1,0:T(8,128)(2,1)} %pad_maximum_fusion.3), calls=%async_computation.2 | async-start | bytes 1179648 | tf_op jit(solution)/shard_map/all_to_all | solution.py:1418
  281.0 12.6 %collective-permute-start.21 = (bf16[512,768]{1,0:T(8,128)(2,1)S(1)}, bf16[512,768]{1,0:T(8,128)(2,1)S(1)}, u32[]{:S(2)}, u32[]{:S(2)}) collective-permute-start(bf16[512,768]{1,0:T(8,128)(2,1)S(1)} %get-tuple-element.215), channel_id=1, source_target_pairs={{0,1},{1,0},{2,3},{3,2},{4,5},{5,4},{6,7},{7,6},{8,9},{9,8},{10,11... | collective-permute-start | bytes 2359304 | tf_op jit(solution)/shard_map/ppermute | solution.py:1210
  283.9 9.0 %collective-permute-start.28 = (bf16[48,768]{1,0:T(8,128)(2,1)S(1)}, bf16[48,768]{1,0:T(8,128)(2,1)S(1)}, u32[]{:S(2)}, u32[]{:S(2)}) collective-permute-start(bf16[48,768]{1,0:T(8,128)(2,1)S(1)} %get-tuple-element.242), channel_id=1, source_target_pairs={{0,16},{8,24},{16,0},{24,8},{1,17},{9,25},{17,1},{25,9},{2,18},{10... | collective-permute-start | bytes 221192 | tf_op jit(solution)/shard_map/ppermute | solution.py:1185
  (40 other events, 153.8 us)
Sparse Core Ops, SparseCore 0:
  11.4 65.1 all-gather.1
